TPU v7x, 128 devices: a whole 4x4x4 slice. The times are simulated.
128 devices in a mesh: pb: 4 (over z), pa: 32 (over y, x, core).
Axes of the slice: x: 4, y: 4, z: 4, core: 2. Of those that a mesh axis runs over, the one named last changes fastest.
Arguments:
- queries: bfloat16 [8192, 1024], P('pb'), may hold values from -16 to 16
- passages: bfloat16 [65536, 1024], P('pa'), may hold values from -5 to 5
- teacher: float32 [8192, 16384], P('pb', 'pa'), may hold values from -20 to 300
- block_ids: int32 [64, 128], P('pb', 'pa'), may hold values from 0 to 511, as said below
Outputs:
- loss: float32 [8192], P(('pb', 'pa'))
- grad_queries: float32 [8192, 1024], P(('pb', 'pa'))
- grad_passages: float32 [65536, 1024], P(('pa', 'pb'))
Inputs may be any that keep to these rules, and one draw needn't show every extreme that they name: Block g belongs to passage shard g // 16. Among the 64 entries of one device's tile of block_ids (rows of one index of pb, columns of one index of pa), at most 4 name blocks of one shard, and in every tile some shard is named exactly 4 times. The 4 entries of one row of a tile name blocks of different shards.
All inputs are finite; a program needn't handle non-finite values.
Results may differ from a plain program's by a relative error of at most 0.0024.
Values sent between devices are 32-bit elements; how exact they have to be, the bound alone decides.
No kernel may reach another device: no remote copies, remote signals or barrier semaphores. Data moves between devices by JAX's collectives and lax.ppermute only.
A program may use at most 192 MiB of HBM per device.

v0:
```python
import math

import jax
import jax.numpy as jnp
from jax import lax
from jax.sharding import PartitionSpec as P

D = 1024
BLOCK = 128
PBLOCKS_DEV = 16


loss_scale = 1024.0


def pack_tiles(source, block_ids, pa_count):
    qblock_count, slots_here = block_ids.shape
    entries = qblock_count * slots_here
    capacity = 2 * ((entries + pa_count - 1) // pa_count)
    flat_ids = block_ids.reshape(entries)
    owners = flat_ids // PBLOCKS_DEV
    local_block = flat_ids % PBLOCKS_DEV
    entry_order = jnp.arange(entries, dtype=jnp.int32)
    same_owner = (owners[:, None] == owners[None, :]) & (
        entry_order[None, :] < entry_order[:, None]
    )
    slot_rank = jnp.sum(same_owner.astype(jnp.int32), axis=1)
    destination = owners * capacity + slot_rank
    onehot = destination[None, :] == jnp.arange(pa_count * capacity, dtype=jnp.int32)[:, None]
    tile_data = source.reshape(qblock_count, BLOCK, slots_here, BLOCK).transpose(0, 2, 1, 3)
    tile_data = tile_data.reshape(entries, BLOCK * BLOCK)
    packed = jnp.dot(
        onehot.astype(jnp.float32),
        tile_data,
        precision=lax.Precision.HIGHEST,
        preferred_element_type=jnp.float32,
    )
    meta_marks = jnp.stack([entry_order // slots_here + 1, local_block + 1], axis=1)
    tile_meta = jnp.sum(onehot.astype(jnp.int32)[:, :, None] * meta_marks[None, :, :], axis=1) - 1
    return (
        packed.reshape(pa_count, capacity, BLOCK * BLOCK),
        tile_meta.reshape(pa_count, capacity, 2),
    )


def per_device(queries, passages, teacher, block_ids):
    query_count = queries.shape[0]
    passage_count = passages.shape[0]
    qblock_count = query_count // BLOCK
    pblock_count = passage_count // BLOCK
    pa_count = lax.axis_size("pa")
    score_scale = 2.0 / math.sqrt(D)
    scores = (
        lax.dot_general(
            queries, passages, (((1,), (1,)), ((), ())), preferred_element_type=jnp.float32
        )
        * score_scale
    )
    row_max = jnp.max(scores, axis=1)
    row_sum = jnp.sum(jnp.exp(scores - row_max[:, None]), axis=1)
    teacher_max = jnp.max(teacher, axis=1)
    teacher_sum = jnp.sum(jnp.exp(teacher - teacher_max[:, None]), axis=1)
    whole_max, whole_tmax = lax.pmax((row_max, teacher_max), "pa")
    whole_sum, whole_tsum = lax.psum(
        (row_sum * jnp.exp(row_max - whole_max), teacher_sum * jnp.exp(teacher_max - whole_tmax)),
        "pa",
    )
    lse_student = whole_max + jnp.log(whole_sum)
    lse_teacher = whole_tmax + jnp.log(whole_tsum)
    teacher_probs = jnp.exp(teacher - lse_teacher[:, None])
    packed, tile_meta = pack_tiles(teacher_probs, block_ids, pa_count)
    got_tiles, got_meta = (
        lax.all_to_all(packed, "pa", split_axis=0, concat_axis=0, tiled=True),
        lax.all_to_all(tile_meta, "pa", split_axis=0, concat_axis=0, tiled=True),
    )
    slot_total = got_tiles.shape[0] * got_tiles.shape[1]
    flat_tiles = got_tiles.reshape(slot_total, BLOCK * BLOCK)
    flat_meta = got_meta.reshape(slot_total, 2)
    row_block = flat_meta[:, 0]
    col_block = flat_meta[:, 1]
    live_slot = col_block >= 0
    flat_tiles = jnp.where(live_slot[:, None], flat_tiles, 0.0)
    target = jnp.where(live_slot, row_block * pblock_count + col_block, -1)
    place = (
        jnp.arange(qblock_count * pblock_count, dtype=jnp.int32)[:, None] == target[None, :]
    ).astype(jnp.float32)
    listed = jnp.dot(
        place, flat_tiles, precision=lax.Precision.HIGHEST, preferred_element_type=jnp.float32
    )
    listed = listed.reshape(qblock_count, pblock_count, BLOCK, BLOCK).transpose(0, 2, 1, 3)
    listed = listed.reshape(query_count, passage_count)
    hard_rows = jnp.sum(listed * scores, axis=1)
    weights = jnp.exp(scores - lse_student[:, None]) - listed
    dscore = (weights * (loss_scale * score_scale)).astype(jnp.bfloat16)
    loss_part = jnp.sum(teacher_probs * (teacher - lse_teacher[:, None]), axis=1) - hard_rows
    query_part = jnp.dot(dscore, passages, preferred_element_type=jnp.float32)
    grad_queries, loss_sum = (
        lax.psum_scatter(query_part, "pa", scatter_dimension=0, tiled=True),
        lax.psum_scatter(loss_part, "pa", scatter_dimension=0, tiled=True),
    )
    row_count = query_count // pa_count
    first_row = lax.axis_index("pa") * row_count
    loss_rows = loss_sum + lax.dynamic_slice_in_dim(lse_student, first_row, row_count)
    grad_passages = lax.psum_scatter(
        lax.dot_general(
            dscore, queries, (((0,), (0,)), ((), ())), preferred_element_type=jnp.float32
        ),
        "pb",
        scatter_dimension=0,
        tiled=True,
    )
    return (loss_rows, grad_queries, grad_passages)


def solution(mesh):
    in_specs = (P("pb", None), P("pa", None), P("pb", "pa"), P("pb", "pa"))
    out_specs = (P(("pb", "pa")), P(("pb", "pa"), None), P(("pa", "pb"), None))
    return jax.shard_map(
        per_device, mesh=mesh, in_specs=in_specs, out_specs=out_specs, check_vma=False
    )
```

profile of v0, /device:TPU:1, one launch (start us, length us, event | category | flops | bytes accessed | tf_op | source)
XLA Modules:
  0.0 791.3 jit_solution(2045358586373505156)
XLA Ops:
  7.2 0.8 copy.31
  8.6 0.6 copy.33
  9.3 8.6 %all-to-all-start = ((s32[32,4,2]{1,2,0:T(2,128)}), s32[32,4,2]{1,2,0:T(2,128)S(1)}, u32[]{:S(2)}, u32[]{:S(2)}) async-start(s32[32,4,2]{1,2,0:T(2,128)} %copy.33), calls=%async_computation | async-start | bytes 65536 | tf_op jit(solution)/shard_map/all_to_all | solution.py:74
  17.9 2.5 reduce_max.18
  20.4 3.3 exponential_reduce_fusion.1
  23.7 15.2 %multiply_reduce_fusion.1 = (f32[2048]{0:T(1024)S(1)}, f32[2048,2048]{0,1:T(8,128)}) fusion(bf16[2048,1024]{1,0:T(8,128)(2,1)} %param.4, bf16[2048,1024]{1,0:T(8,128)(2,1)} %param.5), kind=kOutput, calls=%fused_computation.4 | convolution fusion | flops 8598321152 | bytes 25174016 | tf_op jit(solution)/shard_map/dot_general | solution.py:54
  38.9 123.2 %all-reduce.2 = (f32[2048]{0:T(1024)S(1)}, f32[2048]{0:T(1024)S(1)}) all-reduce(f32[2048]{0:T(1024)S(1)} %reduce_max.18, f32[2048]{0:T(1024)S(1)} %get-tuple-element.11), channel_id=1, replica_groups=mesh['pb'=4,'pa'=32] {'pa'}, use_global_device_ids=true, to_apply=%region_1.0 | all-reduce | flops 4096 | bytes 32768 | tf_op jit(solution)/shard_map/pmax | solution.py:63
  162.1 68.8 %psum.14 = f32[2048]{0:T(1024)S(1)} all-reduce(f32[2048]{0:T(1024)S(1)} %exponential_multiply_fusion.1), channel_id=1, replica_groups=mesh['pb'=4,'pa'=32] {'pa'}, use_global_device_ids=true, to_apply=%region_3.0 | all-reduce | flops 2048 | bytes 16384 | tf_op jit(solution)/shard_map/psum | solution.py:64
  231.0 5.2 subtract_exponential_fusion
  236.2 5.2 reshape.280
  241.4 4.8 copy.35
  246.2 4.9 reshape.284
  251.1 8.8 %fusion.5 = f32[32,4,16384]{2,0,1:T(8,128)} fusion(f32[64,16384,1]{1,0,2:T(8,128)} %reshape.284, s32[32,4]{0,1:T(4,128)S(1)} %multiply_add_fusion.1, s32[64]{0:T(128)S(1)} %multiply_add_fusion.2), kind=kOutput, calls=%fused_computation.15 | convolution fusion | flops 1610620928 | bytes 12583680 | tf_op jit(solution)/shard_map/dot_general | solution.py:32
  259.9 12.0 %copy.36 = f32[32,4,16384]{2,1,0:T(4,128)} copy(f32[32,4,16384]{2,0,1:T(8,128)} %fusion.5) | data formatting | bytes 16777216 | tf_op jit(solution)/shard_map/dot_general | solution.py:32
  271.9 5.2 all-to-all-start.1
  277.5 100.3 %all-to-all-done.1 = f32[32,4,16384]{2,1,0:T(4,128)} async-done(((f32[32,4,16384]{2,1,0:T(4,128)}), f32[32,4,16384]{2,1,0:T(4,128)}, u32[]{:S(2)}, u32[]{:S(2)}) %all-to-all-start.1) | async-done | bytes 8388640 | tf_op jit(solution)/shard_map/all_to_all | solution.py:73
  377.8 10.0 %reshape.282 = f32[128,16384]{1,0:T(8,128)} reshape(f32[32,4,16384]{2,1,0:T(4,128)} %all-to-all-done.1) | data formatting | bytes 16777216 | tf_op jit(solution)/shard_map/reshape | solution.py:77
  387.8 7.5 select_bitcast_fusion
  395.3 9.0 %copy.41 = f32[16384,128]{1,0:T(8,128)} copy(f32[16384,128]{0,1:T(8,128)} %select_bitcast_fusion) | data formatting | bytes 16777216 | tf_op jit(solution)/shard_map/dot_general | solution.py:87
  404.3 9.6 %fusion = f32[16,16,128,128]{3,1,2,0:T(8,128)S(1)} fusion(f32[128,128,128,1]{2,1,0,3:T(8,128)} %bitcast.38, s32[128]{0:T(128)S(1)} %fusion.12, s32[16,16]{1,0:T(8,128)S(1)} %multiply_add_fusion), kind=kOutput, calls=%fused_computation.9 | convolution fusion | flops 6442483712 | bytes 25167360 | tf_op jit(solution)/shard_map/dot_general | solution.py:87
  413.9 11.2 %copy.44 = f32[256,8,16,128]{3,1,2,0:T(8,128)} copy(f32[256,8,16,128]{3,2,1,0:T(8,128)S(1)} %bitcast.36) | data formatting | bytes 33554432
  425.1 17.6 %copy.38 = f32[2048,2048]{0,1:T(8,128)} copy(f32[2048,2048]{1,0:T(8,128)} %bitcast.37) | data formatting | bytes 33554432 | tf_op jit(solution)/shard_map/reshape | solution.py:91
  442.7 12.0 %exponential_reduce_fusion = (f32[2048]{0:T(1024)S(1)}, f32[2048]{0:T(1024)S(1)}) fusion(f32[2048,2048]{0,1:T(8,128)} %get-tuple-element.12, f32[2048]{0:T(1024)S(1)} %get-tuple-element.11, f32[2048,2048]{0,1:T(8,128)} %copy.38), kind=kLoop, calls=%fused_computation.2 | loop fusion | flops 20967424 | bytes 33579008 | tf_op jit(solution)/shard_map/reduce_sum | solution.py:60
  454.7 124.5 %all-reduce.1 = (f32[2048]{0:T(1024)S(1)}, f32[2048]{0:T(1024)S(1)}) all-reduce(f32[2048]{0:T(1024)S(1)} %sub.73, f32[2048]{0:T(1024)S(1)} %exponential_multiply_fusion), channel_id=2, replica_groups=mesh['pb'=4,'pa'=32] {'pa'}, use_global_device_ids=true, to_apply=%region_8.9.clone | all-reduce | flops 4096 | bytes 32768
  579.3 12.3 %multiply_convert_fusion = bf16[2048,2048]{0,1:T(8,128)(2,1)S(1)} fusion(f32[2048,2048]{0,1:T(8,128)} %copy.38, f32[2048,2048]{0,1:T(8,128)} %get-tuple-element.12, f32[2048]{0:T(1024)S(1)} %log_add_fusion), kind=kLoop, calls=%fused_computation.1 | loop fusion | flops 20971520 | bytes 41951232 | tf_op jit(solution)/shard_map/convert_element_type | solution.py:94
  591.6 3.2 copy-done
  594.8 11.5 %fusion.15 = f32[2048,1024]{1,0:T(8,128)} fusion(bf16[2048,2048]{0,1:T(8,128)(2,1)S(1)} %multiply_convert_fusion, bf16[2048,1024]{1,0:T(8,128)(2,1)S(1)} %copy-done.1), kind=kOutput, calls=%fused_computation.51 | convolution fusion | flops 8589934592 | bytes 20971520 | tf_op jit(solution)/shard_map/dot_general | solution.py:96
  606.3 14.4 %fusion.16 = f32[2048,1024]{1,0:T(8,128)} fusion(bf16[2048,2048]{0,1:T(8,128)(2,1)} %copy-done, bf16[2048,1024]{1,0:T(8,128)(2,1)} %param.4), kind=kOutput, calls=%fused_computation.52 | convolution fusion | flops 8589934592 | bytes 20971520 | tf_op jit(solution)/shard_map/dot_general | solution.py:105
  620.8 0.6 copy-done.2
  622.7 0.6 dynamic-slice_add_fusion
  623.3 76.3 %reduce-scatter.3.cloned.1.call-done = f32[64,1024]{1,0:T(8,128)} async-done(((f32[2048,1024]{1,0:T(8,128)}), f32[64,1024]{1,0:T(8,128)}) %reduce-scatter.3.cloned.1.call-update) | async-done | bytes 262160 | tf_op jit(solution)/shard_map/reduce_scatter | solution.py:98
  699.6 84.8 %reduce-scatter.5.cloned.1.call-done = f32[512,1024]{1,0:T(8,128)} async-done(((f32[2048,1024]{1,0:T(8,128)}), f32[512,1024]{1,0:T(8,128)}) %reduce-scatter.5.cloned.1.call-update) | async-done | bytes 2097168 | tf_op jit(solution)/shard_map/reduce_scatter | solution.py:104
  (32 shorter events, 1.8 us)
Async XLA Ops:
  9.3 262.6 %all-to-all-start = ((s32[32,4,2]{1,2,0:T(2,128)}), s32[32,4,2]{1,2,0:T(2,128)S(1)}, u32[]{:S(2)}, u32[]{:S(2)}) async-start(s32[32,4,2]{1,2,0:T(2,128)} %copy.33), calls=%async_computation | async-start | bytes 65536 | tf_op jit(solution)/shard_map/all_to_all | solution.py:74
  271.9 105.9 %all-to-all-start.1 = ((f32[32,4,16384]{2,1,0:T(4,128)}), f32[32,4,16384]{2,1,0:T(4,128)}, u32[]{:S(2)}, u32[]{:S(2)}) async-start(f32[32,4,16384]{2,1,0:T(4,128)} %copy.36), calls=%async_computation.1 | async-start | bytes 16777216 | tf_op jit(solution)/shard_map/all_to_all | solution.py:73
  277.1 422.5 %reduce-scatter.3.cloned.1.call-start = ((), (), s32[]{:S(2)}) async-start(), calls=%async_computation.4 | async-start | bytes 8650752 | tf_op jit(solution)/shard_map/reduce_scatter | solution.py:98
  579.3 15.5 %copy-start.1 = (bf16[2048,1024]{1,0:T(8,128)(2,1)S(1)}, bf16[2048,1024]{1,0:T(8,128)(2,1)}, u32[]{:S(2)}) copy-start(bf16[2048,1024]{1,0:T(8,128)(2,1)} %param.5) | copy-start | bytes 12582916
  591.5 3.2 copy-start
  606.3 178.1 %reduce-scatter.5.cloned.1.call-start = ((), (), s32[]{:S(2)}) async-start(), calls=%async_computation.5 | async-start | bytes 10485760 | tf_op jit(solution)/shard_map/reduce_scatter | solution.py:104
  620.8 0.7 copy-start.2
Sparse Core Ops, SparseCore 0:
  606.4 93.1 reduce-scatter.2
  702.6 81.7 reduce-scatter.4
where the time goes:
time: 793 us; the launch traced here: 791 us
  blocking collectives  317 us (40%)
  waiting for transfers between devices  261 us (33%)
  local copies, waits for them, and re-layouts  80.9 us (10%)
  matrix products  59.4 us (7%)
  other arithmetic  43.9 us (6%)
  between operations  14.9 us (2%)
  starting transfers between devices  14.1 us (2%)
    unnamed x1, blocking collectives  125 us
    pmax x1, blocking collectives, per_device(): whole_max, whole_tmax = lax.pmax((row_max, teacher_max), 'pa')  123 us
    all_to_all x1, waiting for transfers between devices, per_device(): lax.all_to_all(packed, 'pa', split_axis=0, concat_axis=0, tiled=True)  100 us
    reduce_scatter x1, waiting for transfers between devices, per_device(): lax.psum_scatter(lax.dot_general(dscore, queries, (((0,), (0,)), ((), ())...  84.8 us
    reduce_scatter x1, waiting for transfers between devices, per_device(): lax.psum_scatter(query_part, 'pa', scatter_dimension=0, tiled=True)  76.3 us
    psum x1, blocking collectives, per_device(): lax.psum((row_sum * jnp.exp(row_max - whole_max), teacher_sum * jnp.exp(t...  68.8 us
    reshape x1, local copies, waits for them, and re-layouts, per_device(): listed = listed.reshape(query_count, passage_count)  17.6 us
    unnamed x9, local copies, waits for them, and re-layouts  16.4 us
  transfers between devices with their start and end apart: 4, of which 3 were waited for; matrix products, arithmetic and copies ran while one was open for 10% of the time, Pallas kernels for 0%

commit v1 on v0

v1 whole, which is shorter than its diff:
```python
import functools

import jax
import jax.numpy as jnp
from jax import lax
from jax.experimental import pallas as pl
from jax.experimental.pallas import tpu as pltpu
from jax.sharding import Mesh
from jax.sharding import PartitionSpec as P


BLOCK = 128
D = 1024
ROWS = 2048
PBLOCKS_DEV = 16
SLOTS_DEV = 4
CAP = 4
SHARDS = 32
ENTRIES = 64
PACK_STEP = 8
QUARTER = 32
LSE_ROWS = 32
PLANE = ("y", "x", "c")
SCORE_SCALE = 0.0625
GRAD_SCALE = 64.0


def as_row(column):
    n = column.shape[0]
    return jnp.broadcast_to(column, (n, BLOCK)).T[0:1, :]


def as_lanes(row):
    n = row.shape[1]
    return jnp.broadcast_to(row, (BLOCK, n)).T


def pack_kernel(piece, ids_ref, teacher_ref, out_ref, slot_ref, count_ref):
    step = pl.program_id(0)

    @pl.when(step == 0)
    def _():
        for i in range(SHARDS):
            count_ref[i] = 0
        for i in range(SHARDS * CAP):
            slot_ref[i] = -1

        def place(i, carry):
            owner = ids_ref[i] // PBLOCKS_DEV
            rank = count_ref[owner]
            count_ref[owner] = rank + 1
            slot_ref[owner * CAP + jnp.minimum(rank, CAP - 1)] = i
            return carry

        lax.fori_loop(0, ENTRIES, place, 0, unroll=8)

    quarter = lax.broadcasted_iota(jnp.int32, (BLOCK, BLOCK), 1) // QUARTER
    lane = lax.broadcasted_iota(jnp.int32, (8, BLOCK), 1)
    move = lambda t, lanes: t if lanes % BLOCK == 0 else pltpu.roll(t, lanes % BLOCK, 1)
    for j in range(PACK_STEP):
        meta = jnp.zeros((8, BLOCK), jnp.float32)
        tiles = []
        for k in range(CAP):
            slot = slot_ref[(step * PACK_STEP + j) * CAP + k]
            entry = jnp.maximum(slot, 0)
            row = pl.multiple_of((entry // SLOTS_DEV) * BLOCK, BLOCK)
            col = pl.multiple_of((entry % SLOTS_DEV) * BLOCK, BLOCK)
            tiles.append(teacher_ref[pl.ds(row, BLOCK), pl.ds(col, BLOCK)])
            if piece == 0:
                where = jnp.where(slot < 0, -1, entry // SLOTS_DEV).astype(jnp.float32)
                block = (ids_ref[entry] % PBLOCKS_DEV).astype(jnp.float32)
                meta = jnp.where(lane == k, where, meta)
                meta = jnp.where(lane == CAP + k, block, meta)
        if piece < 2:
            moved = [move(t, QUARTER * (k - piece)) for k, t in enumerate(tiles)]
            low = jnp.where(quarter == 0, moved[0], moved[1])
            high = jnp.where(quarter == 2, moved[2], moved[3])
            out_ref[j, :BLOCK, :] = jnp.where(quarter < 2, low, high)
        else:
            for pair in range(CAP // 2):
                first = pltpu.roll(tiles[2 * pair], BLOCK // 2, 1)
                rows = slice(pair * BLOCK, (pair + 1) * BLOCK)
                out_ref[j, rows, :] = jnp.where(quarter < 2, first, tiles[2 * pair + 1])
        if piece == 0:
            out_ref[j, BLOCK:, :] = meta


def pack(piece, ids, teacher):
    rows = (BLOCK + 8, BLOCK, 2 * BLOCK)[piece]
    total = rows + (LSE_ROWS if piece == 1 else 0)
    return pl.pallas_call(
        functools.partial(pack_kernel, piece),
        out_shape=jax.ShapeDtypeStruct((SHARDS, total, BLOCK), jnp.float32),
        grid_spec=pltpu.PrefetchScalarGridSpec(
            num_scalar_prefetch=1,
            grid=(SHARDS // PACK_STEP,),
            in_specs=[pl.BlockSpec((ROWS, SLOTS_DEV * BLOCK), lambda s, ids: (0, 0))],
            out_specs=pl.BlockSpec((PACK_STEP, rows, BLOCK), lambda s, ids: (s, 0, 0)),
            scratch_shapes=[
                pltpu.SMEM((SHARDS * CAP,), jnp.int32),
                pltpu.SMEM((SHARDS,), jnp.int32),
            ],
        ),
        name="pack",
    )(ids, teacher)


def fill_kernel(lse_ref, sent_ref, out_ref):
    out_ref[...] = jnp.broadcast_to(lse_ref[...][None], out_ref.shape)


def fill_lse(sent, lse):
    return pl.pallas_call(
        fill_kernel,
        out_shape=jax.ShapeDtypeStruct(sent.shape, sent.dtype),
        grid=(1,),
        in_specs=[
            pl.BlockSpec((LSE_ROWS, BLOCK), lambda i: (0, 0)),
            pl.BlockSpec(memory_space=pl.ANY),
        ],
        out_specs=pl.BlockSpec((SHARDS, LSE_ROWS, BLOCK), lambda i: (0, BLOCK // LSE_ROWS, 0)),
        input_output_aliases={1: 0},
        name="fill_lse",
    )(lse, sent)


def list_kernel(meta_ref, start_ref, row_ref, block_ref, next_ref):
    blocks = ROWS // BLOCK
    for r in range(blocks):
        next_ref[r] = 0

    def count(n, carry):
        r = meta_ref[(n // CAP) * (2 * CAP) + n % CAP]

        @pl.when(r >= 0)
        def _():
            next_ref[r] = next_ref[r] + 1

        row_ref[n] = 0
        block_ref[n] = 0
        return carry

    lax.fori_loop(0, SHARDS * CAP, count, 0, unroll=4)
    total = 0
    for r in range(blocks):
        start_ref[r] = total
        size = next_ref[r]
        next_ref[r] = total
        total = total + size
    start_ref[blocks] = total

    def place(n, carry):
        src, k = n // CAP, n % CAP
        r = meta_ref[src * (2 * CAP) + k]

        @pl.when(r >= 0)
        def _():
            at = next_ref[r]
            next_ref[r] = at + 1
            row_ref[at] = n
            block_ref[at] = meta_ref[src * (2 * CAP) + CAP + k]

        return carry

    lax.fori_loop(0, SHARDS * CAP, place, 0, unroll=4)


def make_lists(meta):
    smem = pl.BlockSpec(memory_space=pltpu.SMEM)
    ints = lambda n: jax.ShapeDtypeStruct((n,), jnp.int32)
    return pl.pallas_call(
        list_kernel,
        out_shape=(ints(ROWS // BLOCK + 1), ints(SHARDS * CAP), ints(SHARDS * CAP)),
        in_specs=[smem],
        out_specs=(smem, smem, smem),
        scratch_shapes=[pltpu.SMEM((ROWS // BLOCK,), jnp.int32)],
        name="make_lists",
    )(meta)


def score_kernel(q_ref, p_ref, t_ref, s0_ref, s1_ref, lse_ref, p0_ref, p1_ref):
    half = BLOCK // 2

    @pl.when(pl.program_id(0) == 0)
    def _():
        for block in range(PBLOCKS_DEV):
            here = slice(block * half, (block + 1) * half)
            p0_ref[here, :] = p_ref[block * BLOCK : block * BLOCK + half, :]
            p1_ref[here, :] = p_ref[block * BLOCK + half : (block + 1) * BLOCK, :]

    q = q_ref[...]
    nt = (((1,), (1,)), ((), ()))
    s0 = lax.dot_general(q, p0_ref[...], nt, preferred_element_type=jnp.float32) * SCORE_SCALE
    s1 = lax.dot_general(q, p1_ref[...], nt, preferred_element_type=jnp.float32) * SCORE_SCALE
    s0_ref[...] = s0
    s1_ref[...] = s1
    top = jnp.maximum(jnp.max(s0, axis=1, keepdims=True), jnp.max(s1, axis=1, keepdims=True))
    total = jnp.sum(jnp.exp(s0 - top), axis=1, keepdims=True) + jnp.sum(
        jnp.exp(s1 - top), axis=1, keepdims=True
    )
    lse_ref[0, 0:1, :] = as_row(top + jnp.log(total))
    t = t_ref[...]
    ttop = jnp.max(t, axis=1, keepdims=True)
    ttotal = jnp.sum(jnp.exp(t - ttop), axis=1, keepdims=True)
    lse_ref[0, 1:2, :] = as_row(ttop + jnp.log(ttotal))


def score(queries, passages, teacher):
    rb = 256
    block = pl.BlockSpec((rb, D), lambda i: (i, 0))
    whole = pl.BlockSpec((D, D), lambda i: (0, 0))
    scores = jax.ShapeDtypeStruct((ROWS, D), jnp.float32)
    part = jax.ShapeDtypeStruct((D, D), jnp.bfloat16)
    return pl.pallas_call(
        score_kernel,
        out_shape=(
            scores,
            scores,
            jax.ShapeDtypeStruct((ROWS // rb, 2, rb), jnp.float32),
            part,
            part,
        ),
        grid=(ROWS // rb,),
        in_specs=[
            block,
            pl.BlockSpec((ROWS, D), lambda i: (0, 0)),
            pl.BlockSpec((rb, SLOTS_DEV * BLOCK), lambda i: (i, 0)),
        ],
        out_specs=(block, block, pl.BlockSpec((1, 2, rb), lambda i: (i, 0, 0)), whole, whole),
        name="score",
    )(queries, passages, teacher)


def rows_kernel(
    last, pos_ref, start_ref, row_ref, block_ref, s_ref, lse_ref, *refs
):
    if last:
        recv_ref, p_ref, add_ref, ds_ref, loss_ref, own_ref, other_ref, w_ref, lt_ref, acc_ref = refs
    else:
        recv_ref, recv2_ref, p_ref, ds_ref, loss_ref, out_ref, w_ref, lt_ref, acc_ref = refs
    step = pl.program_id(0)
    rb = 256
    half = BLOCK // 2
    ls = as_lanes(lse_ref[0, 0:1, :])
    lt_ref[...] = as_lanes(lse_ref[0, 1:2, :])
    for j in range(D // BLOCK):
        cols = slice(j * BLOCK, (j + 1) * BLOCK)
        w_ref[:, cols] = jnp.exp(s_ref[:, cols] - ls)
    acc_ref[...] = jnp.zeros_like(acc_ref)
    lane = lax.broadcasted_iota(jnp.int32, (BLOCK, BLOCK), 1)
    side = lane // half
    early = lane % half < QUARTER

    def fetch(n):
        slot = row_ref[n]
        block = block_ref[n]
        src, k = slot // CAP, slot % CAP
        shift = (block % 2) * half
        if last:
            at = pl.multiple_of(src * (2 * BLOCK) + (k // 2) * BLOCK, BLOCK)
            x = recv_ref[pl.ds(at, BLOCK), :]
            x = pltpu.roll(x, (shift + (k % 2) * half) % BLOCK, 1)
        else:
            at = pl.multiple_of(src * (BLOCK + 8), 8)
            x = recv_ref[pl.ds(at, BLOCK), :]
            x = pltpu.roll(x, (shift - k * QUARTER + BLOCK) % BLOCK, 1)
            at = pl.multiple_of(src * (BLOCK + LSE_ROWS), 8)
            y = recv2_ref[pl.ds(at, BLOCK), :]
            y = pltpu.roll(y, (shift + QUARTER - k * QUARTER + BLOCK) % BLOCK, 1)
            x = jnp.where(early, x, y)
        return x, block

    for sub in range(rb // BLOCK):
        rows = slice(sub * BLOCK, (sub + 1) * BLOCK)
        r = step * (rb // BLOCK) + sub
        end = start_ref[r + 1]

        def body(n, carry):
            first = start_ref[r] + 2 * n
            parts = []
            for at in (first, first + 1):
                x, block = fetch(jnp.minimum(at, end - 1))
                keep = (side == block % 2) & (at < end)
                centred = x - lt_ref[rows, :]
                prob = jnp.where(keep, jnp.exp(centred), 0.0)
                cols = pl.ds(pl.multiple_of((block // 2) * BLOCK, BLOCK), BLOCK)
                term = jnp.where(keep, prob * (centred - s_ref[rows, cols]), 0.0)
                parts.append((prob, cols, term))
            acc_ref[rows, :] = acc_ref[rows, :] + (parts[0][2] + parts[1][2])
            for prob, cols, _ in parts:
                w_ref[rows, cols] = w_ref[rows, cols] - prob
            return carry

        lax.fori_loop(0, (end - start_ref[r] + 1) // 2, body, 0)
    ds = (w_ref[...] * GRAD_SCALE).astype(jnp.bfloat16)
    ds_ref[...] = ds
    loss_ref[0] = as_row(jnp.sum(acc_ref[...], axis=1, keepdims=True))
    part = jnp.dot(ds, p_ref[...], preferred_element_type=jnp.float32)
    if not last:
        out_ref[...] = part
        return
    part = part + add_ref[...]
    dy = (step // 2 + 4 - pos_ref[1]) % 4
    for j in range(4):
        dx = (2 * step + j // 2 + 4 - pos_ref[2]) % 4
        a = pl.ds(pl.multiple_of(dx * 128 + dy * 32, 32), 32)
        b = pl.ds(pl.multiple_of(512 + dy * 128 + dx * 32, 32), 32)

        @pl.when(pos_ref[3] == j % 2)
        def _():
            own_ref[a, :] = part[64 * j : 64 * j + 32]
            own_ref[b, :] = part[64 * j + 32 : 64 * j + 64]

        @pl.when(pos_ref[3] != j % 2)
        def _():
            other_ref[a, :] = part[64 * j : 64 * j + 32]
            other_ref[b, :] = part[64 * j + 32 : 64 * j + 64]


def rows_call(scalars, scores, lse, recvs, passages, add=None):
    rb = 256
    last = add is not None
    recvs = [r.reshape(-1, BLOCK) for r in recvs]
    block = pl.BlockSpec((rb, D), lambda i, *_: (i, 0))
    full = lambda *shape: pl.BlockSpec(shape, lambda i, *_: (0,) * len(shape))
    grad = jax.ShapeDtypeStruct((ROWS // 2 if last else ROWS, D), jnp.float32)
    return pl.pallas_call(
        functools.partial(rows_kernel, last),
        out_shape=(
            jax.ShapeDtypeStruct((ROWS, D), jnp.bfloat16),
            jax.ShapeDtypeStruct((ROWS // rb, 1, rb), jnp.float32),
        )
        + ((grad, grad) if last else (grad,)),
        grid_spec=pltpu.PrefetchScalarGridSpec(
            num_scalar_prefetch=len(scalars),
            grid=(ROWS // rb,),
            in_specs=[block, pl.BlockSpec((1, 2, rb), lambda i, *_: (i, 0, 0))]
            + [full(*r.shape) for r in recvs]
            + [full(D, D)]
            + ([block] if last else []),
            out_specs=(block, pl.BlockSpec((1, 1, rb), lambda i, *_: (i, 0, 0)))
            + ((full(ROWS // 2, D),) * 2 if last else (block,)),
            scratch_shapes=[
                pltpu.VMEM((rb, D), jnp.float32),
                pltpu.VMEM((rb, BLOCK), jnp.float32),
                pltpu.VMEM((rb, BLOCK), jnp.float32),
            ],
        ),
        name="rows",
    )(*scalars, scores, lse, *recvs, passages, *([add] if last else []))


def columns_kernel(pos_ref, ds_ref, q_ref, *outs):
    groups = {0: outs[:1], 1: outs[1:3], 2: outs[3:5], 3: outs[5:7]}
    for d in (2, 1, 3, 0):
        off = pl.multiple_of(((pos_ref[0] + d) % 4) * (D // 4), D // 4)
        part = lax.dot_general(
            ds_ref[:, pl.ds(off, D // 4)],
            q_ref[...],
            (((0,), (0,)), ((), ())),
            preferred_element_type=jnp.float32,
        )
        size = D // 4 // len(groups[d])
        for i, out in enumerate(groups[d]):
            out[...] = part[size * i : size * (i + 1)]


def columns_call(pos, ds, queries):
    full = lambda *shape: pl.BlockSpec(shape, lambda i, *_: (0,) * len(shape))
    sizes = (D // 4,) + (D // 8,) * 6
    return pl.pallas_call(
        columns_kernel,
        out_shape=tuple(jax.ShapeDtypeStruct((n, D), jnp.float32) for n in sizes),
        grid_spec=pltpu.PrefetchScalarGridSpec(
            num_scalar_prefetch=1,
            grid=(1,),
            in_specs=[full(ROWS, D), full(ROWS, D)],
            out_specs=tuple(full(n, D) for n in sizes),
        ),
        name="columns",
    )(pos, ds, queries)


def ring(d, n=4):
    return [(i, (i + d) % n) for i in range(n)]


def combine_kernel(own_ref, other_ref, *outs):
    for base, group in ((0, outs[:5]), (512, outs[5:])):
        at = lambda lo, n: own_ref[base + lo : base + lo + n] + other_ref[base + lo : base + lo + n]
        group[0][...] = at(0, 128)
        group[1][...] = at(128, 128)
        group[2][...] = at(256, 64)
        group[3][...] = at(320, 64)
        group[4][...] = at(384, 128)


def combine(own, other):
    full = lambda n: pl.BlockSpec((n, D), lambda i: (0, 0))
    sizes = (128, 128, 64, 64, 128) * 2
    return pl.pallas_call(
        combine_kernel,
        out_shape=tuple(jax.ShapeDtypeStruct((n, D), jnp.float32) for n in sizes),
        grid=(1,),
        in_specs=[full(ROWS // 2)] * 2,
        out_specs=tuple(full(n) for n in sizes),
        name="combine",
    )(own, other)


def send(value, axis, d, n=4):
    return lax.ppermute(value, axis, ring(d, n))


def together(*values):
    return lax.optimization_barrier(values)


def near(low, high, axis):
    return [send(low, axis, 1), send(high, axis, -1)]


def far(c1, c3, near_p, near_m, axis):
    h = near_p.shape[0]
    s1 = jnp.concatenate([c1[:h] + near_p, c1[h:]], axis=0)
    s3 = jnp.concatenate([c3[:h], c3[h:] + near_m], axis=0)
    return [send(s1, axis, 1), send(s3, axis, -1)]


def per_device(queries, passages, teacher, block_ids):
    mz, my, mx, mc = (lax.axis_index(a) for a in ("pb", "y", "x", "c"))
    me = my * 8 + mx * 2 + mc
    pos = jnp.stack([mz, my, mx, mc]).astype(jnp.int32)
    flat_ids = block_ids.reshape(-1)
    exchange = functools.partial(
        lax.all_to_all, axis_name=PLANE, split_axis=0, concat_axis=0, tiled=True
    )
    sent0 = pack(0, flat_ids, teacher)
    recv0 = exchange(sent0)
    ids1, _ = together(flat_ids, sent0)
    sent1 = pack(1, ids1, teacher)
    s0, s1, lse, p0, p1 = score(queries, passages, teacher)
    sent1 = fill_lse(sent1, lse.reshape(LSE_ROWS, BLOCK))
    recv1 = exchange(sent1)
    ids2, _ = together(flat_ids, lse)
    sent2 = pack(2, ids2, teacher)
    sent2, _ = together(sent2, recv1[0, 0, 0])
    recv2 = exchange(sent2)
    meta = recv0[:, BLOCK, : 2 * CAP].astype(jnp.int32).reshape(-1)
    scalars = (pos,) + tuple(make_lists(meta))
    every = recv1[:, BLOCK:, :]
    top = jnp.max(every, axis=0)
    lse = top + jnp.log(jnp.sum(jnp.exp(every - top[None]), axis=0))
    lse = lse.reshape(8, 2, 256)
    ds0, loss0, q0 = rows_call(scalars, s0, lse, [recv0, recv1], p0)
    g0 = columns_call(pos, ds0, queries)
    z0 = [g0[0], g0[1:3], g0[3:5], g0[5:7]]
    np0, nm0 = send(z0[2][0], "pb", 1), send(z0[2][1], "pb", -1)
    fp0, fm0 = send(z0[1][1], "pb", 1), send(z0[3][0], "pb", -1)
    sp0 = send(z0[1][0] + np0, "pb", 1)
    sm0 = send(z0[3][1] + nm0, "pb", -1)

    ds1, loss1, own, other = rows_call(scalars, s1, lse, [recv2], p1, q0)
    swapped = send(other, "c", 1, 2)
    g1 = columns_call(pos, ds1, queries)
    z1 = [g1[0], g1[1:3], g1[3:5], g1[5:7]]
    np1, nm1 = send(z1[2][0], "pb", 1), send(z1[2][1], "pb", -1)
    fp1, fm1 = send(z1[1][1], "pb", 1), send(z1[3][0], "pb", -1)
    a0, a1, a2, a3, a4, b0, b1, b2, b3, b4 = combine(own, swapped)
    loss_sum = (loss0 + loss1).reshape(SHARDS, ROWS // SHARDS)
    np1, nm1, apn, anm, bpn, bnm, loss_sum = together(
        np1, nm1, *near(a2, a3, "x"), *near(b2, b3, "y"), loss_sum
    )
    af, bf = far(a1, a4, apn, anm, "x"), far(b1, b4, bpn, bnm, "y")
    sp1 = send(z1[1][0] + np1, "pb", 1)
    sm1 = send(z1[3][1] + nm1, "pb", -1)
    loss_part = exchange(loss_sum)
    af0, af1, bf0, bf1 = together(*af, *bf)
    cut = lambda v: [v[32 * i : 32 * (i + 1)] for i in range(4)]
    a, b = cut(a0 + af0 + af1), cut(b0 + bf0 + bf1)
    apn, anm, bpn, bnm = together(
        *near(a[2][:16], a[2][16:], "y"), *near(b[2][:16], b[2][16:], "x")
    )
    af, bf = far(a[1], a[3], apn, anm, "y"), far(b[1], b[3], bpn, bnm, "x")
    af0, af1, bf0, bf1 = together(*af, *bf)
    grad_queries = jnp.concatenate([a[0] + af0 + af1, b[0] + bf0 + bf1], axis=0)

    h = D // 8
    parts = [
        z0[0][:h] + sp0 + fm0,
        z0[0][h:] + fp0 + sm0,
        z1[0][:h] + sp1 + fm1,
        z1[0][h:] + fp1 + sm1,
    ]
    gp0, gp1 = jnp.concatenate(parts[:2]), jnp.concatenate(parts[2:])
    lse_rows = lax.dynamic_slice_in_dim(
        lse[:, 0, :].reshape(ROWS), me * (ROWS // SHARDS), ROWS // SHARDS
    )
    loss = jnp.sum(loss_part, axis=0) + lse_rows
    grad_passages = jnp.stack(
        [gp0.reshape(4, BLOCK // 2, D), gp1.reshape(4, BLOCK // 2, D)], axis=1
    ).reshape(4 * BLOCK, D)
    return loss, grad_queries, grad_passages


def solution(mesh):
    fine = Mesh(mesh.devices.reshape(4, 4, 4, 2), ("pb",) + PLANE)
    in_specs = (P("pb", None), P(PLANE, None), P("pb", PLANE), P("pb", PLANE))
    out_specs = (P(("pb",) + PLANE), P(("pb",) + PLANE, None), P(PLANE + ("pb",), None))
    return jax.shard_map(
        per_device, mesh=fine, in_specs=in_specs, out_specs=out_specs, check_vma=False
    )
```

time: 793 us -> 293 us (0.37)
  blocking collectives: 317 us -> 0 us
  waiting for transfers between devices: 261 us -> 91.8 us
  Pallas kernels: 0 us -> 110 us
  local copies, waits for them, and re-layouts: 80.9 us -> 7.55 us
  matrix products: 59.4 us -> 0 us
  starting transfers between devices: 14.1 us -> 60.9 us
  other arithmetic: 43.9 us -> 18.5 us
  between operations: 14.9 us -> 1.03 us
    reduce_scatter x2 -> x0, waiting for transfers between devices: 161 us -> none  [the longest x1 84.8 us: per_device(): lax.psum_scatter(lax.dot_general(dscore, queries, (((0,), (0,)), ((), ())...]
    unnamed x1 -> x0, blocking collectives: 125 us -> none
    pmax x1 -> x0, blocking collectives: 123 us -> none  [per_device(): whole_max, whole_tmax = lax.pmax((row_max, teacher_max), 'pa')]
    pallas_call x0 -> x11, Pallas kernels: none -> 110 us  [the longest x2 42.3 us: rows_call(): pl.pallas_call(functools.partial(rows_kernel, last), out_shape=(jax.Shape...]
    psum x1 -> x0, blocking collectives: 68.8 us -> none  [per_device(): lax.psum((row_sum * jnp.exp(row_max - whole_max), teacher_sum * jnp.exp(t...]
    dot_general x5 -> x0, matrix products: 59.4 us -> none  [the longest x1 15.2 us: per_device(): lax.dot_general(queries, passages, (((1,), (1,)), ((), ())), preferred_el...]
    all_to_all x2 -> x4, waiting for transfers between devices: 100 us -> 57.5 us  [the longest x1 28.1 us: per_device(): recv1 = exchange(sent1)]
    reshape x7 -> x3, local copies, waits for them, and re-layouts: 38.1 us -> 2.6 us  [the longest x1 1.33 us: per_device(): sent1 = fill_lse(sent1, lse.reshape(LSE_ROWS, BLOCK))]
  transfers between devices with their start and end apart: 4 -> 33, of which waited for: 3 -> 15; matrix products, arithmetic and copies ran while one was open for 10% -> 8% of each run, Pallas kernels for 0% -> 28%
where the time goes in v1:
time: 293 us; the launch traced here: 289 us
  Pallas kernels  110 us (38%)
  waiting for transfers between devices  91.8 us (31%)
  starting transfers between devices  60.9 us (21%)
  other arithmetic  18.5 us (6%)
  local copies, waits for them, and re-layouts  7.55 us (3%)
    pallas_call x2, Pallas kernels, rows_call(): pl.pallas_call(functools.partial(rows_kernel, last), out_shape=(jax.Shape...  42.3 us
    ppermute x29, waiting for transfers between devices, send(): return lax.ppermute(value, axis, ring(d, n))  34.3 us
    ppermute x29, starting transfers between devices, send(): return lax.ppermute(value, axis, ring(d, n))  31.9 us
    all_to_all x1, waiting for transfers between devices, per_device(): recv1 = exchange(sent1)  28.1 us
    all_to_all x1, waiting for transfers between devices, per_device(): recv2 = exchange(sent2)  23.5 us
    pallas_call x2, Pallas kernels, columns_call(): pl.pallas_call(columns_kernel, out_shape=tuple((jax.ShapeDtypeStruct((n,...  19.4 us
    pallas_call x1, Pallas kernels, score(): pl.pallas_call(score_kernel, out_shape=(scores, scores, jax.ShapeDtypeStr...  18.7 us
    pallas_call x3, Pallas kernels, pack(): pl.pallas_call(functools.partial(pack_kernel, piece), out_shape=jax.Shape...  17.9 us
  transfers between devices with their start and end apart: 33, of which 15 were waited for; matrix products, arithmetic and copies ran while one was open for 8% of the time, Pallas kernels for 28%

profile of v1, /device:TPU:1, one launch (start us, length us, event | category | flops | bytes accessed | tf_op | source)
XLA Modules:
  0.0 289.4 jit_solution(18153235042539429524)
XLA Ops:
  2.0 6.0 %pack.3 = f32[32,136,128]{2,1,0:T(8,128)} custom-call(s32[64]{0:T(128)} %reshape.38.ids_ref, f32[2048,512]{1,0:T(8,128)} %teacher_ref.5), custom_call_target="tpu_custom_call" | custom-call | tf_op jit(solution)/shard_map/pack/pallas_call | solution.py:91
  8.0 8.6 %all-to-all-start = ((f32[32,136,128]{2,1,0:T(8,128)}), f32[32,136,128]{2,1,0:T(8,128)S(1)}, u32[]{:S(2)}, u32[]{:S(2)}) async-start(f32[32,136,128]{2,1,0:T(8,128)} %pack.3), calls=%async_computation | async-start | bytes 4456448 | tf_op jit(solution)/shard_map/all_to_all | solution.py:439
  16.5 18.7 %score.1 = (f32[2048,1024]{1,0:T(8,128)}, f32[2048,1024]{1,0:T(8,128)}, f32[8,2,256]{2,1,0:T(2,128)}, bf16[1024,1024]{1,0:T(8,128)(2,1)}, bf16[1024,1024]{1,0:T(8,128)(2,1)}) custom-call(bf16[2048,1024]{1,0:T(8,128)(2,1)} %q_ref.5, bf16[2048,1024]{1,0:T(8,128)(2,1)} %p_ref.1, f32[2048,512]{1,0:T(8,128)} %teacher_ref.5), custom_call_target="tpu_custom_call" | custom-call | tf_op jit(solution)/shard_map/score/pallas_call | solution.py:214
  36.6 6.0 %pack.4.sent_ref = f32[32,160,128]{2,1,0:T(8,128)} custom-call(s32[64]{0:T(128)} %reshape.38.ids_ref, f32[2048,512]{1,0:T(8,128)} %teacher_ref.5), custom_call_target="tpu_custom_call" | custom-call | tf_op jit(solution)/shard_map/pack/pallas_call | solution.py:91
  44.2 2.5 all-to-all-done
  48.0 5.4 %all-to-all-start.1 = ((f32[32,160,128]{2,1,0:T(8,128)}), f32[32,160,128]{2,1,0:T(8,128)S(1)}, u32[]{:S(2)}, u32[]{:S(2)}) async-start(f32[32,160,128]{2,1,0:T(8,128)} %fill_lse.1), calls=%async_computation.1 | async-start | bytes 5242880 | tf_op jit(solution)/shard_map/all_to_all | solution.py:444
  53.5 5.9 %pack.5 = f32[32,256,128]{2,1,0:T(8,128)} custom-call(s32[64]{0:T(128)} %reshape.38.ids_ref, f32[2048,512]{1,0:T(8,128)} %teacher_ref.5), custom_call_target="tpu_custom_call" | custom-call | tf_op jit(solution)/shard_map/pack/pallas_call | solution.py:91
  59.4 28.1 %all-to-all-done.1 = f32[32,160,128]{2,1,0:T(8,128)S(1)} async-done(((f32[32,160,128]{2,1,0:T(8,128)}), f32[32,160,128]{2,1,0:T(8,128)S(1)}, u32[]{:S(2)}, u32[]{:S(2)}) %all-to-all-start.1) | async-done | bytes 2621472 | tf_op jit(solution)/shard_map/all_to_all | solution.py:444
  87.5 7.0 %all-to-all-start.2 = ((f32[32,256,128]{2,1,0:T(8,128)}), f32[32,256,128]{2,1,0:T(8,128)}, u32[]{:S(2)}, u32[]{:S(2)}) async-start(f32[32,256,128]{2,1,0:T(8,128)} %pack.5), calls=%async_computation.2 | async-start | bytes 8388608 | tf_op jit(solution)/shard_map/all_to_all | solution.py:448
  96.7 4.2 %make_lists.1 = (s32[17]{0:T(128)}, s32[128]{0:T(128)}, s32[128]{0:T(128)}) custom-call(s32[256]{0:T(256)} %convert_element_type.8.meta_ref), custom_call_target="tpu_custom_call" | custom-call | tf_op jit(solution)/shard_map/make_lists/pallas_call | solution.py:171
  101.7 19.9 %rows.2 = (bf16[2048,1024]{1,0:T(8,128)(2,1)}, f32[8,1,256]{2,1,0:T(1,128)}, f32[2048,1024]{1,0:T(8,128)}) custom-call(s32[4]{0:T(128)} %pad_add_fusion.pos_ref, s32[17]{0:T(128)} %get-tuple-element.63.start_ref, s32[128]{0:T(128)} %get-tuple-element.64.row_ref, s32[128]{0:T(128)} %get-tuple-element.65.block_ref, f32[2048,1024]{1,0:T(8,128)} %get-tuple-element.71.s_ref, ...), custom_call_target="tpu_custom_call" | custom-call | tf_op jit(solution)/shard_map/rows/pallas_call | solution.py:327
  121.6 23.5 %all-to-all-done.2 = f32[32,256,128]{2,1,0:T(8,128)} async-done(((f32[32,256,128]{2,1,0:T(8,128)}), f32[32,256,128]{2,1,0:T(8,128)}, u32[]{:S(2)}, u32[]{:S(2)}) %all-to-all-start.2) | async-done | bytes 4194336 | tf_op jit(solution)/shard_map/all_to_all | solution.py:448
  145.1 22.4 %rows.3 = (bf16[2048,1024]{1,0:T(8,128)(2,1)}, f32[8,1,256]{2,1,0:T(1,128)}, f32[1024,1024]{1,0:T(8,128)}, f32[1024,1024]{1,0:T(8,128)}) custom-call(s32[4]{0:T(128)} %pad_add_fusion.pos_ref, s32[17]{0:T(128)} %get-tuple-element.63.start_ref, s32[128]{0:T(128)} %get-tuple-element.64.row_ref, s32[128]{0:T(128)} %get-tuple-element.65.block_ref, ...), custom_call_target="tpu_custom_call" | custom-call | tf_op jit(solution)/shard_map/rows/pallas_call | solution.py:327
  167.6 3.4 %collective-permute-start.2 = (f32[1024,1024]{1,0:T(8,128)}, f32[1024,1024]{1,0:T(8,128)}, u32[]{:S(2)}, u32[]{:S(2)}) collective-permute-start(f32[1024,1024]{1,0:T(8,128)} %get-tuple-element.78), channel_id=1, source_target_pairs={{0,1},{1,0},{2,3},{3,2},{4,5},{5,4},{6,7},{7,6},{8,9},{9,8},{10,11... | collective-permute-start | bytes 12582920 | tf_op jit(solution)/shard_map/ppermute | solution.py:412
  170.9 9.7 %columns.3 = (f32[256,1024]{1,0:T(8,128)}, f32[128,1024]{1,0:T(8,128)}, f32[128,1024]{1,0:T(8,128)}, f32[128,1024]{1,0:T(8,128)}, f32[128,1024]{1,0:T(8,128)}, /*index=5*/f32[128,1024]{1,0:T(8,128)}, f32[128,1024]{1,0:T(8,128)}) custom-call(s32[4]{0:T(128)} %pad_add_fusion.pos_ref, bf16[2048,1024]{1,0:T(8,128)(2,1)} %get-tuple-element.108.ds_ref, ...), custom_call_target="tpu_custom_call" | custom-call | tf_op jit(solution)/shard_map/columns/pallas_call | solution.py:371
  180.6 2.3 collective-permute-start.23
  183.6 9.7 %columns.2 = (f32[256,1024]{1,0:T(8,128)}, f32[128,1024]{1,0:T(8,128)}, f32[128,1024]{1,0:T(8,128)}, f32[128,1024]{1,0:T(8,128)}, f32[128,1024]{1,0:T(8,128)}, /*index=5*/f32[128,1024]{1,0:T(8,128)}, f32[128,1024]{1,0:T(8,128)}) custom-call(s32[4]{0:T(128)} %pad_add_fusion.pos_ref, bf16[2048,1024]{1,0:T(8,128)(2,1)} %get-tuple-element.74.ds_ref, ...), custom_call_target="tpu_custom_call" | custom-call | tf_op jit(solution)/shard_map/columns/pallas_call | solution.py:371
  195.9 5.6 %combine.1 = (f32[128,1024]{1,0:T(8,128)}, f32[128,1024]{1,0:T(8,128)}, f32[64,1024]{1,0:T(8,128)}, f32[64,1024]{1,0:T(8,128)}, f32[128,1024]{1,0:T(8,128)}, /*i...) custom-call(f32[1024,1024]{1,0:T(8,128)} %get-tuple-element.77.own_r, ...), custom_call_target="tpu_custom_call" | custom-call | tf_op jit(solution)/shard_map/combine/pallas_call | solution.py:401
  201.6 2.7 collective-permute-start.4
  205.9 2.8 collective-permute-done
  225.7 10.1 %collective-permute-done.24 = f32[128,1024]{1,0:T(8,128)S(1)} collective-permute-done((f32[128,1024]{1,0:T(8,128)S(1)}, f32[128,1024]{1,0:T(8,128)S(1)}, u32[]{:S(2)}, u32[]{:S(2)}) %collective-permute-start.24) | collective-permute-done | bytes 524320 | tf_op jit(solution)/shard_map/ppermute | solution.py:412
  237.3 8.0 %all-to-all-start.3 = ((f32[32,1,64]{2,1,0:T(1,128)}), f32[32,1,64]{2,1,0:T(1,128)S(1)}, u32[]{:S(2)}, u32[]{:S(2)}) async-start(f32[32,1,64]{2,1,0:T(1,128)} %bitcast.7), calls=%async_computation.3 | async-start | bytes 32768 | tf_op jit(solution)/shard_map/all_to_all | solution.py:477
  246.8 1.9 add.139
  249.8 3.5 %all-to-all-done.3 = f32[32,1,64]{2,1,0:T(1,128)S(1)} async-done(((f32[32,1,64]{2,1,0:T(1,128)}), f32[32,1,64]{2,1,0:T(1,128)S(1)}, u32[]{:S(2)}, u32[]{:S(2)}) %all-to-all-start.3) | async-done | bytes 8224 | tf_op jit(solution)/shard_map/all_to_all | solution.py:477
  253.9 2.7 collective-permute-start.28
  256.6 2.1 add_add_fusion.4
  259.1 2.5 collective-permute-start.12
  261.6 6.5 %collective-permute-done.27 = f32[128,1024]{1,0:T(8,128)S(1)} collective-permute-done((f32[128,1024]{1,0:T(8,128)}, f32[128,1024]{1,0:T(8,128)S(1)}, u32[]{:S(2)}, u32[]{:S(2)}) %collective-permute-start.27) | collective-permute-done | bytes 524320 | tf_op jit(solution)/shard_map/ppermute | solution.py:412
  268.1 2.2 collective-permute-done.28
  270.2 2.4 collective-permute-start.14
  272.6 6.7 %collective-permute-done.25 = f32[128,1024]{1,0:T(8,128)S(1)} collective-permute-done((f32[128,1024]{1,0:T(8,128)S(1)}, f32[128,1024]{1,0:T(8,128)S(1)}, u32[]{:S(2)}, u32[]{:S(2)}) %collective-permute-start.25) | collective-permute-done | bytes 524320 | tf_op jit(solution)/shard_map/ppermute | solution.py:412
  286.7 2.0 collective-permute-done.15
  (121 shorter events, 43.7 us)
Async XLA Ops:
  8.0 38.7 %all-to-all-start = ((f32[32,136,128]{2,1,0:T(8,128)}), f32[32,136,128]{2,1,0:T(8,128)S(1)}, u32[]{:S(2)}, u32[]{:S(2)}) async-start(f32[32,136,128]{2,1,0:T(8,128)} %pack.3), calls=%async_computation | async-start | bytes 4456448 | tf_op jit(solution)/shard_map/all_to_all | solution.py:439
  48.0 39.4 %all-to-all-start.1 = ((f32[32,160,128]{2,1,0:T(8,128)}), f32[32,160,128]{2,1,0:T(8,128)S(1)}, u32[]{:S(2)}, u32[]{:S(2)}) async-start(f32[32,160,128]{2,1,0:T(8,128)} %fill_lse.1), calls=%async_computation.1 | async-start | bytes 5242880 | tf_op jit(solution)/shard_map/all_to_all | solution.py:444
  87.5 57.7 %all-to-all-start.2 = ((f32[32,256,128]{2,1,0:T(8,128)}), f32[32,256,128]{2,1,0:T(8,128)}, u32[]{:S(2)}, u32[]{:S(2)}) async-start(f32[32,256,128]{2,1,0:T(8,128)} %pack.5), calls=%async_computation.2 | async-start | bytes 8388608 | tf_op jit(solution)/shard_map/all_to_all | solution.py:448
  167.6 28.3 %collective-permute-start.2 = (f32[1024,1024]{1,0:T(8,128)}, f32[1024,1024]{1,0:T(8,128)}, u32[]{:S(2)}, u32[]{:S(2)}) collective-permute-start(f32[1024,1024]{1,0:T(8,128)} %get-tuple-element.78), channel_id=1, source_target_pairs={{0,1},{1,0},{2,3},{3,2},{4,5},{5,4},{6,7},{7,6},{8,9},{9,8},{10,11... | collective-permute-start | bytes 12582920 | tf_op jit(solution)/shard_map/ppermute | solution.py:412
  180.6 21.0 %collective-permute-start.23 = (f32[128,1024]{1,0:T(8,128)}, f32[128,1024]{1,0:T(8,128)S(1)}, u32[]{:S(2)}, u32[]{:S(2)}) collective-permute-start(f32[128,1024]{1,0:T(8,128)} %get-tuple-element.115), channel_id=1, source_target_pairs={{0,96},{32,0},{64,32},{96,64},{1,97},{33,1},{65,33},{97,65},{2,98}... | collective-permute-start | bytes 1572872 | tf_op jit(solution)/shard_map/ppermute | solution.py:412
  182.9 21.4 %collective-permute-start.19 = (f32[128,1024]{1,0:T(8,128)}, f32[128,1024]{1,0:T(8,128)S(1)}, u32[]{:S(2)}, u32[]{:S(2)}) collective-permute-start(f32[128,1024]{1,0:T(8,128)} %get-tuple-element.111), channel_id=1, source_target_pairs={{0,32},{32,64},{64,96},{96,0},{1,33},{33,65},{65,97},{97,1},{2,34}... | collective-permute-start | bytes 1572872 | tf_op jit(solution)/shard_map/ppermute | solution.py:412
  193.2 15.5 %collective-permute-start = (f32[128,1024]{1,0:T(8,128)}, f32[128,1024]{1,0:T(8,128)S(1)}, u32[]{:S(2)}, u32[]{:S(2)}) collective-permute-start(f32[128,1024]{1,0:T(8,128)} %get-tuple-element.75), channel_id=1, source_target_pairs={{0,32},{32,64},{64,96},{96,0},{1,33},{33,65},{65,97},{97,1},{2,34}... | collective-permute-start | bytes 1572872 | tf_op jit(solution)/shard_map/ppermute | solution.py:412
  194.6 17.6 %collective-permute-start.1 = (f32[128,1024]{1,0:T(8,128)}, f32[128,1024]{1,0:T(8,128)S(1)}, u32[]{:S(2)}, u32[]{:S(2)}) collective-permute-start(f32[128,1024]{1,0:T(8,128)} %get-tuple-element.76), channel_id=1, source_target_pairs={{0,96},{32,0},{64,32},{96,64},{1,97},{33,1},{65,33},{97,65},{2,98}... | collective-permute-start | bytes 1572872 | tf_op jit(solution)/shard_map/ppermute | solution.py:412
  201.5 10.7 %collective-permute-start.3 = (f32[64,1024]{1,0:T(8,128)}, f32[64,1024]{1,0:T(8,128)S(1)}, u32[]{:S(2)}, u32[]{:S(2)}) collective-permute-start(f32[64,1024]{1,0:T(8,128)} %get-tuple-element.79), channel_id=1, source_target_pairs={{0,2},{2,4},{4,6},{6,0},{1,3},{3,5},{5,7},{7,1},{8,10},{10,12},{12... | collective-permute-start | bytes 786440 | tf_op jit(solution)/shard_map/ppermute | solution.py:412
  201.6 12.1 %collective-permute-start.4 = (f32[64,1024]{1,0:T(8,128)}, f32[64,1024]{1,0:T(8,128)}, u32[]{:S(2)}, u32[]{:S(2)}) collective-permute-start(f32[64,1024]{1,0:T(8,128)} %get-tuple-element.80), channel_id=1, source_target_pairs={{0,6},{2,0},{4,2},{6,4},{1,7},{3,1},{5,3},{7,5},{8,14},{10,8},{12,... | collective-permute-start | bytes 786440 | tf_op jit(solution)/shard_map/ppermute | solution.py:412
  204.3 10.7 %collective-permute-start.5 = (f32[64,1024]{1,0:T(8,128)}, f32[64,1024]{1,0:T(8,128)}, u32[]{:S(2)}, u32[]{:S(2)}) collective-permute-start(f32[64,1024]{1,0:T(8,128)} %get-tuple-element.81), channel_id=1, source_target_pairs={{0,8},{8,16},{16,24},{24,0},{1,9},{9,17},{17,25},{25,1},{2,10},{10... | collective-permute-start | bytes 786440 | tf_op jit(solution)/shard_map/ppermute | solution.py:412
  208.7 8.0 %collective-permute-start.6 = (f32[64,1024]{1,0:T(8,128)}, f32[64,1024]{1,0:T(8,128)}, u32[]{:S(2)}, u32[]{:S(2)}) collective-permute-start(f32[64,1024]{1,0:T(8,128)} %get-tuple-element.82), channel_id=1, source_target_pairs={{0,24},{8,0},{16,8},{24,16},{1,25},{9,1},{17,9},{25,17},{2,26},{10... | collective-permute-start | bytes 786440 | tf_op jit(solution)/shard_map/ppermute | solution.py:412
  212.2 13.1 %collective-permute-start.21 = (f32[128,1024]{1,0:T(8,128)}, f32[128,1024]{1,0:T(8,128)S(1)}, u32[]{:S(2)}, u32[]{:S(2)}) collective-permute-start(f32[128,1024]{1,0:T(8,128)} %get-tuple-element.112), channel_id=1, source_target_pairs={{0,96},{32,0},{64,32},{96,64},{1,97},{33,1},{65,33},{97,65},{2,98}... | collective-permute-start | bytes 1572872 | tf_op jit(solution)/shard_map/ppermute | solution.py:412
  212.3 13.4 %collective-permute-start.22 = (f32[128,1024]{1,0:T(8,128)}, f32[128,1024]{1,0:T(8,128)S(1)}, u32[]{:S(2)}, u32[]{:S(2)}) collective-permute-start(f32[128,1024]{1,0:T(8,128)} %get-tuple-element.113), channel_id=1, source_target_pairs={{0,32},{32,64},{64,96},{96,0},{1,33},{33,65},{65,97},{97,1},{2,34}... | collective-permute-start | bytes 1572872 | tf_op jit(solution)/shard_map/ppermute | solution.py:412
  213.7 22.1 %collective-permute-start.24 = (f32[128,1024]{1,0:T(8,128)S(1)}, f32[128,1024]{1,0:T(8,128)S(1)}, u32[]{:S(2)}, u32[]{:S(2)}) collective-permute-start(f32[128,1024]{1,0:T(8,128)S(1)} %add.133), channel_id=1, source_target_pairs={{0,96},{32,0},{64,32},{96,64},{1,97},{33,1},{65,33},{97,65},{2,98}... | collective-permute-start | bytes 1572872 | tf_op jit(solution)/shard_map/ppermute | solution.py:412
  215.0 22.0 %collective-permute-start.20 = (f32[128,1024]{1,0:T(8,128)S(1)}, f32[128,1024]{1,0:T(8,128)S(1)}, u32[]{:S(2)}, u32[]{:S(2)}) collective-permute-start(f32[128,1024]{1,0:T(8,128)S(1)} %add.129), channel_id=1, source_target_pairs={{0,32},{32,64},{64,96},{96,0},{1,33},{33,65},{65,97},{97,1},{2,34}... | collective-permute-start | bytes 1572872 | tf_op jit(solution)/shard_map/ppermute | solution.py:412
  218.8 35.1 %collective-permute-start.10 = (f32[128,1024]{1,0:T(8,128)}, f32[128,1024]{1,0:T(8,128)}, u32[]{:S(2)}, u32[]{:S(2)}) collective-permute-start(f32[128,1024]{1,0:T(8,128)} %pad_maximum_fusion.6), channel_id=1, source_target_pairs={{0,24},{8,0},{16,8},{24,16},{1,25},{9,1},{17,9},{25,17},{2,26},{10... | collective-permute-start | bytes 1572872 | tf_op jit(solution)/shard_map/ppermute | solution.py:412
  225.3 28.6 %collective-permute-start.9 = (f32[128,1024]{1,0:T(8,128)}, f32[128,1024]{1,0:T(8,128)}, u32[]{:S(2)}, u32[]{:S(2)}) collective-permute-start(f32[128,1024]{1,0:T(8,128)} %pad_maximum_fusion.5), channel_id=1, source_target_pairs={{0,8},{8,16},{16,24},{24,0},{1,9},{9,17},{17,25},{25,1},{2,10},{10... | collective-permute-start | bytes 1572872 | tf_op jit(solution)/shard_map/ppermute | solution.py:412
  225.7 30.9 %collective-permute-start.8 = (f32[128,1024]{1,0:T(8,128)}, f32[128,1024]{1,0:T(8,128)}, u32[]{:S(2)}, u32[]{:S(2)}) collective-permute-start(f32[128,1024]{1,0:T(8,128)} %pad_maximum_fusion.4), channel_id=1, source_target_pairs={{0,6},{2,0},{4,2},{6,4},{1,7},{3,1},{5,3},{7,5},{8,14},{10,8},{12,... | collective-permute-start | bytes 1572872 | tf_op jit(solution)/shard_map/ppermute | solution.py:412
  235.8 20.7 %collective-permute-start.7 = (f32[128,1024]{1,0:T(8,128)}, f32[128,1024]{1,0:T(8,128)}, u32[]{:S(2)}, u32[]{:S(2)}) collective-permute-start(f32[128,1024]{1,0:T(8,128)} %pad_maximum_fusion.3), channel_id=1, source_target_pairs={{0,2},{2,4},{4,6},{6,0},{1,3},{3,5},{5,7},{7,1},{8,10},{10,12},{12... | collective-permute-start | bytes 1572872 | tf_op jit(solution)/shard_map/ppermute | solution.py:412
  237.3 15.9 %all-to-all-start.3 = ((f32[32,1,64]{2,1,0:T(1,128)}), f32[32,1,64]{2,1,0:T(1,128)S(1)}, u32[]{:S(2)}, u32[]{:S(2)}) async-start(f32[32,1,64]{2,1,0:T(1,128)} %bitcast.7), calls=%async_computation.3 | async-start | bytes 32768 | tf_op jit(solution)/shard_map/all_to_all | solution.py:477
  245.5 13.6 %collective-permute-start.26 = (f32[128,1024]{1,0:T(8,128)}, f32[128,1024]{1,0:T(8,128)}, u32[]{:S(2)}, u32[]{:S(2)}) collective-permute-start(f32[128,1024]{1,0:T(8,128)} %get-tuple-element.119), channel_id=1, source_target_pairs={{0,96},{32,0},{64,32},{96,64},{1,97},{33,1},{65,33},{97,65},{2,98}... | collective-permute-start | bytes 1572872 | tf_op jit(solution)/shard_map/ppermute | solution.py:412
  253.9 14.2 %collective-permute-start.27 = (f32[128,1024]{1,0:T(8,128)}, f32[128,1024]{1,0:T(8,128)S(1)}, u32[]{:S(2)}, u32[]{:S(2)}) collective-permute-start(f32[128,1024]{1,0:T(8,128)} %get-tuple-element.120), channel_id=1, source_target_pairs={{0,32},{32,64},{64,96},{96,0},{1,33},{33,65},{65,97},{97,1},{2,34}... | collective-permute-start | bytes 1572872 | tf_op jit(solution)/shard_map/ppermute | solution.py:412
  253.9 16.4 %collective-permute-start.28 = (f32[128,1024]{1,0:T(8,128)}, f32[128,1024]{1,0:T(8,128)S(1)}, u32[]{:S(2)}, u32[]{:S(2)}) collective-permute-start(f32[128,1024]{1,0:T(8,128)} %add.139), channel_id=1, source_target_pairs={{0,96},{32,0},{64,32},{96,64},{1,97},{33,1},{65,33},{97,65},{2,98}... | collective-permute-start | bytes 1572872 | tf_op jit(solution)/shard_map/ppermute | solution.py:412
  256.6 22.7 %collective-permute-start.25 = (f32[128,1024]{1,0:T(8,128)S(1)}, f32[128,1024]{1,0:T(8,128)S(1)}, u32[]{:S(2)}, u32[]{:S(2)}) collective-permute-start(f32[128,1024]{1,0:T(8,128)S(1)} %add.135), channel_id=1, source_target_pairs={{0,32},{32,64},{64,96},{96,0},{1,33},{33,65},{65,97},{97,1},{2,34}... | collective-permute-start | bytes 1572872 | tf_op jit(solution)/shard_map/ppermute | solution.py:412
  258.7 22.1 %collective-permute-start.11 = (f32[16,1024]{1,0:T(8,128)S(1)}, f32[16,1024]{1,0:T(8,128)S(1)}, u32[]{:S(2)}, u32[]{:S(2)}) collective-permute-start(f32[16,1024]{1,0:T(8,128)S(1)} %get-tuple-element.138), channel_id=1, source_target_pairs={{0,8},{8,16},{16,24},{24,0},{1,9},{9,17},{17,25},{25,1},{2,10},{10... | collective-permute-start | bytes 196616 | tf_op jit(solution)/shard_map/ppermute | solution.py:412
  259.1 21.7 %collective-permute-start.12 = (f32[16,1024]{1,0:T(8,128)S(1)}, f32[16,1024]{1,0:T(8,128)S(1)}, u32[]{:S(2)}, u32[]{:S(2)}) collective-permute-start(f32[16,1024]{1,0:T(8,128)S(1)} %get-tuple-element.137), channel_id=1, source_target_pairs={{0,24},{8,0},{16,8},{24,16},{1,25},{9,1},{17,9},{25,17},{2,26},{10... | collective-permute-start | bytes 196616 | tf_op jit(solution)/shard_map/ppermute | solution.py:412
  268.1 12.7 %collective-permute-start.13 = (f32[16,1024]{1,0:T(8,128)S(1)}, f32[16,1024]{1,0:T(8,128)S(1)}, u32[]{:S(2)}, u32[]{:S(2)}) collective-permute-start(f32[16,1024]{1,0:T(8,128)S(1)} %get-tuple-element.136), channel_id=1, source_target_pairs={{0,2},{2,4},{4,6},{6,0},{1,3},{3,5},{5,7},{7,1},{8,10},{10,12},{12... | collective-permute-start | bytes 196616 | tf_op jit(solution)/shard_map/ppermute | solution.py:412
  270.2 10.6 %collective-permute-start.14 = (f32[16,1024]{1,0:T(8,128)S(1)}, f32[16,1024]{1,0:T(8,128)S(1)}, u32[]{:S(2)}, u32[]{:S(2)}) collective-permute-start(f32[16,1024]{1,0:T(8,128)S(1)} %get-tuple-element.135), channel_id=1, source_target_pairs={{0,6},{2,0},{4,2},{6,4},{1,7},{3,1},{5,3},{7,5},{8,14},{10,8},{12,... | collective-permute-start | bytes 196616 | tf_op jit(solution)/shard_map/ppermute | solution.py:412
  280.9 5.0 %collective-permute-start.18 = (f32[32,1024]{1,0:T(8,128)S(1)}, f32[32,1024]{1,0:T(8,128)S(1)}, u32[]{:S(2)}, u32[]{:S(2)}) collective-permute-start(f32[32,1024]{1,0:T(8,128)S(1)} %pad_maximum_fusion.11), channel_id=1, source_target_pairs={{0,6},{2,0},{4,2},{6,4},{1,7},{3,1},{5,3},{7,5},{8,14},{10,8},{12,... | collective-permute-start | bytes 393224 | tf_op jit(solution)/shard_map/ppermute | solution.py:412
  281.0 5.1 %collective-permute-start.17 = (f32[32,1024]{1,0:T(8,128)S(1)}, f32[32,1024]{1,0:T(8,128)S(1)}, u32[]{:S(2)}, u32[]{:S(2)}) collective-permute-start(f32[32,1024]{1,0:T(8,128)S(1)} %pad_maximum_fusion.10), channel_id=1, source_target_pairs={{0,2},{2,4},{4,6},{6,0},{1,3},{3,5},{5,7},{7,1},{8,10},{10,12},{12... | collective-permute-start | bytes 393224 | tf_op jit(solution)/shard_map/ppermute | solution.py:412
  283.6 5.1 %collective-permute-start.15 = (f32[32,1024]{1,0:T(8,128)S(1)}, f32[32,1024]{1,0:T(8,128)S(1)}, u32[]{:S(2)}, u32[]{:S(2)}) collective-permute-start(f32[32,1024]{1,0:T(8,128)S(1)} %pad_maximum_fusion.8), channel_id=1, source_target_pairs={{0,8},{8,16},{16,24},{24,0},{1,9},{9,17},{17,25},{25,1},{2,10},{10... | collective-permute-start | bytes 393224 | tf_op jit(solution)/shard_map/ppermute | solution.py:412
  (17 other events, 186.1 us)

commit v2 on v1

--- a/solution.py
+++ b/solution.py
@@ -79,14 +79,17 @@
         else:
             for pair in range(CAP // 2):
                 first = pltpu.roll(tiles[2 * pair], BLOCK // 2, 1)
-                rows = slice(pair * BLOCK, (pair + 1) * BLOCK)
-                out_ref[j, rows, :] = jnp.where(quarter < 2, first, tiles[2 * pair + 1])
+                both = jnp.where(quarter < 2, first, tiles[2 * pair + 1])
+                for end in range(2):
+                    at = 2 * QUARTER * end + QUARTER * (piece - 2)
+                    out = QUARTER * (2 * pair + end)
+                    out_ref[j, out : out + QUARTER, :] = both[at : at + QUARTER]
         if piece == 0:
             out_ref[j, BLOCK:, :] = meta
 
 
 def pack(piece, ids, teacher):
-    rows = (BLOCK + 8, BLOCK, 2 * BLOCK)[piece]
+    rows = BLOCK + (8 if piece == 0 else 0)
     total = rows + (LSE_ROWS if piece == 1 else 0)
     return pl.pallas_call(
         functools.partial(pack_kernel, piece),
@@ -231,13 +234,36 @@
     )(queries, passages, teacher)
 
 
-def rows_kernel(
-    last, pos_ref, start_ref, row_ref, block_ref, s_ref, lse_ref, *refs
+def subtract_tiles(
+    fetch, sub_rows, first, end, block_ref, s_cols, lt_ref, rows, w_ref, acc_ref
 ):
-    if last:
-        recv_ref, p_ref, add_ref, ds_ref, loss_ref, own_ref, other_ref, w_ref, lt_ref, acc_ref = refs
-    else:
-        recv_ref, recv2_ref, p_ref, ds_ref, loss_ref, out_ref, w_ref, lt_ref, acc_ref = refs
+    lane = lax.broadcasted_iota(jnp.int32, (sub_rows, BLOCK), 1)
+    side = lane // (BLOCK // 2)
+
+    def body(n, carry):
+        parts = []
+        for at in (first + 2 * n, first + 2 * n + 1):
+            here = jnp.minimum(at, end - 1)
+            block = block_ref[here]
+            x = fetch(here, block)
+            keep = (side == block % 2) & (at < end)
+            centred = x - lt_ref[rows, :]
+            prob = jnp.where(keep, jnp.exp(centred), 0.0)
+            cols = pl.ds(pl.multiple_of((block // 2) * BLOCK, BLOCK), BLOCK)
+            term = jnp.where(keep, prob * (centred - s_cols(cols)), 0.0)
+            parts.append((prob, cols, term))
+        acc_ref[rows, :] = acc_ref[rows, :] + (parts[0][2] + parts[1][2])
+        for prob, cols, _ in parts:
+            w_ref[rows, cols] = w_ref[rows, cols] - prob
+        return carry
+
+    lax.fori_loop(0, (end - first + 1) // 2, body, 0)
+
+
+def rows0_kernel(
+    start_ref, row_ref, block_ref, s_ref, lse_ref, recv0_ref, recv1_ref,
+    ds_ref, loss_ref, w_ref, lt_ref, acc_ref,
+):
     step = pl.program_id(0)
     rb = 256
     half = BLOCK // 2
@@ -247,107 +273,147 @@
         cols = slice(j * BLOCK, (j + 1) * BLOCK)
         w_ref[:, cols] = jnp.exp(s_ref[:, cols] - ls)
     acc_ref[...] = jnp.zeros_like(acc_ref)
-    lane = lax.broadcasted_iota(jnp.int32, (BLOCK, BLOCK), 1)
-    side = lane // half
-    early = lane % half < QUARTER
-
-    def fetch(n):
+    early = lax.broadcasted_iota(jnp.int32, (BLOCK, BLOCK), 1) % half < QUARTER
+
+    def fetch(n, block):
         slot = row_ref[n]
-        block = block_ref[n]
         src, k = slot // CAP, slot % CAP
         shift = (block % 2) * half
-        if last:
-            at = pl.multiple_of(src * (2 * BLOCK) + (k // 2) * BLOCK, BLOCK)
-            x = recv_ref[pl.ds(at, BLOCK), :]
-            x = pltpu.roll(x, (shift + (k % 2) * half) % BLOCK, 1)
-        else:
-            at = pl.multiple_of(src * (BLOCK + 8), 8)
-            x = recv_ref[pl.ds(at, BLOCK), :]
-            x = pltpu.roll(x, (shift - k * QUARTER + BLOCK) % BLOCK, 1)
-            at = pl.multiple_of(src * (BLOCK + LSE_ROWS), 8)
-            y = recv2_ref[pl.ds(at, BLOCK), :]
-            y = pltpu.roll(y, (shift + QUARTER - k * QUARTER + BLOCK) % BLOCK, 1)
-            x = jnp.where(early, x, y)
-        return x, block
+        at = pl.multiple_of(src * (BLOCK + 8), 8)
+        x = recv0_ref[pl.ds(at, BLOCK), :]
+        x = pltpu.roll(x, (shift - k * QUARTER + BLOCK) % BLOCK, 1)
+        at = pl.multiple_of(src * (BLOCK + LSE_ROWS), 8)
+        y = recv1_ref[pl.ds(at, BLOCK), :]
+        y = pltpu.roll(y, (shift + QUARTER - k * QUARTER + BLOCK) % BLOCK, 1)
+        return jnp.where(early, x, y)
 
     for sub in range(rb // BLOCK):
         rows = slice(sub * BLOCK, (sub + 1) * BLOCK)
         r = step * (rb // BLOCK) + sub
-        end = start_ref[r + 1]
-
-        def body(n, carry):
-            first = start_ref[r] + 2 * n
-            parts = []
-            for at in (first, first + 1):
-                x, block = fetch(jnp.minimum(at, end - 1))
-                keep = (side == block % 2) & (at < end)
-                centred = x - lt_ref[rows, :]
-                prob = jnp.where(keep, jnp.exp(centred), 0.0)
-                cols = pl.ds(pl.multiple_of((block // 2) * BLOCK, BLOCK), BLOCK)
-                term = jnp.where(keep, prob * (centred - s_ref[rows, cols]), 0.0)
-                parts.append((prob, cols, term))
-            acc_ref[rows, :] = acc_ref[rows, :] + (parts[0][2] + parts[1][2])
-            for prob, cols, _ in parts:
-                w_ref[rows, cols] = w_ref[rows, cols] - prob
-            return carry
-
-        lax.fori_loop(0, (end - start_ref[r] + 1) // 2, body, 0)
-    ds = (w_ref[...] * GRAD_SCALE).astype(jnp.bfloat16)
-    ds_ref[...] = ds
+        subtract_tiles(
+            fetch, BLOCK, start_ref[r], start_ref[r + 1], block_ref,
+            lambda cols: s_ref[rows, cols], lt_ref, rows, w_ref, acc_ref,
+        )
+    ds_ref[...] = (w_ref[...] * GRAD_SCALE).astype(jnp.bfloat16)
     loss_ref[0] = as_row(jnp.sum(acc_ref[...], axis=1, keepdims=True))
-    part = jnp.dot(ds, p_ref[...], preferred_element_type=jnp.float32)
-    if not last:
-        out_ref[...] = part
-        return
-    part = part + add_ref[...]
-    dy = (step // 2 + 4 - pos_ref[1]) % 4
-    for j in range(4):
-        dx = (2 * step + j // 2 + 4 - pos_ref[2]) % 4
-        a = pl.ds(pl.multiple_of(dx * 128 + dy * 32, 32), 32)
-        b = pl.ds(pl.multiple_of(512 + dy * 128 + dx * 32, 32), 32)
-
-        @pl.when(pos_ref[3] == j % 2)
-        def _():
-            own_ref[a, :] = part[64 * j : 64 * j + 32]
-            own_ref[b, :] = part[64 * j + 32 : 64 * j + 64]
-
-        @pl.when(pos_ref[3] != j % 2)
-        def _():
-            other_ref[a, :] = part[64 * j : 64 * j + 32]
-            other_ref[b, :] = part[64 * j + 32 : 64 * j + 64]
-
-
-def rows_call(scalars, scores, lse, recvs, passages, add=None):
+
+
+ROW_SCRATCH = [
+    pltpu.VMEM((256, D), jnp.float32),
+    pltpu.VMEM((256, BLOCK), jnp.float32),
+    pltpu.VMEM((256, BLOCK), jnp.float32),
+]
+
+
+def full_spec(*shape):
+    return pl.BlockSpec(shape, lambda i, *_: (0,) * len(shape))
+
+
+def rows0_call(lists, scores, lse, recvs):
     rb = 256
-    last = add is not None
     recvs = [r.reshape(-1, BLOCK) for r in recvs]
     block = pl.BlockSpec((rb, D), lambda i, *_: (i, 0))
-    full = lambda *shape: pl.BlockSpec(shape, lambda i, *_: (0,) * len(shape))
-    grad = jax.ShapeDtypeStruct((ROWS // 2 if last else ROWS, D), jnp.float32)
-    return pl.pallas_call(
-        functools.partial(rows_kernel, last),
+    return pl.pallas_call(
+        rows0_kernel,
         out_shape=(
             jax.ShapeDtypeStruct((ROWS, D), jnp.bfloat16),
             jax.ShapeDtypeStruct((ROWS // rb, 1, rb), jnp.float32),
+        ),
+        grid_spec=pltpu.PrefetchScalarGridSpec(
+            num_scalar_prefetch=len(lists),
+            grid=(ROWS // rb,),
+            in_specs=[block, pl.BlockSpec((1, 2, rb), lambda i, *_: (i, 0, 0))]
+            + [full_spec(*r.shape) for r in recvs],
+            out_specs=(block, pl.BlockSpec((1, 1, rb), lambda i, *_: (i, 0, 0))),
+            scratch_shapes=ROW_SCRATCH,
+        ),
+        name="rows0",
+    )(*lists, scores, lse, *recvs)
+
+
+def rows1_kernel(
+    pos_ref, start_ref, row_ref, block_ref, s_ref, lse_ref, recv_ref, ds0_ref, p0_ref, p1_ref,
+    *refs,
+):
+    ds_ref, loss_ref, own_ref, other_ref, w_ref, lt_ref, acc_ref = refs[-7:]
+    step = pl.program_id(0)
+    rb = 256
+    half = BLOCK // 2
+    ls = as_lanes(lse_ref[0, 0:1, :])
+    lt_ref[...] = as_lanes(lse_ref[0, 1:2, :])
+    for j in range(D // BLOCK):
+        cols = slice(j * BLOCK, (j + 1) * BLOCK)
+        w_ref[:, cols] = jnp.exp(s_ref[:, 0, :, cols].reshape(rb, BLOCK) - ls)
+    acc_ref[...] = jnp.zeros_like(acc_ref)
+
+    def fetch(n, block):
+        slot = row_ref[n]
+        k = slot % CAP
+        at = pl.multiple_of((slot // 2) * half, half)
+        x = recv_ref[pl.ds(at, half), :]
+        return pltpu.roll(x, ((block + k) % 2) * half, 1)
+
+    for sub in range(rb // half):
+        rows = slice(sub * half, (sub + 1) * half)
+        r = step * (rb // half) + sub
+        subtract_tiles(
+            fetch, half, start_ref[r], start_ref[r + 1], block_ref,
+            lambda cols: s_ref[2 * sub : 2 * sub + 2, 0, :, cols].reshape(half, BLOCK),
+            lt_ref, rows, w_ref, acc_ref,
         )
-        + ((grad, grad) if last else (grad,)),
+    ds = (w_ref[...] * GRAD_SCALE).astype(jnp.bfloat16)
+    ds_ref[...] = ds.reshape(ds_ref.shape)
+    loss_ref[0] = as_row(jnp.sum(acc_ref[...], axis=1, keepdims=True))
+    part = jnp.dot(ds, p1_ref[...], preferred_element_type=jnp.float32)
+    ds0 = ds0_ref[...].reshape(rb, D)
+    part = part + jnp.dot(ds0, p0_ref[...], preferred_element_type=jnp.float32)
+    part = part.reshape(rb // QUARTER, 2, QUARTER // 2, D)
+
+    @pl.when(pos_ref[3] == 0)
+    def _():
+        own_ref[...] = part[:, 0]
+        other_ref[...] = part[:, 1]
+
+    @pl.when(pos_ref[3] != 0)
+    def _():
+        own_ref[...] = part[:, 1]
+        other_ref[...] = part[:, 0]
+
+
+def rows1_call(h, scalars, scores, lse, recv, ds0, p0, p1, ds=None):
+    rb = 256
+    view = (SHARDS, 2, QUARTER, D)
+    recv = recv.reshape(-1, BLOCK)
+    group = pl.BlockSpec((rb // QUARTER, 1, QUARTER, D), lambda i, *_: (i, h, 0, 0))
+    out = pl.BlockSpec((rb // QUARTER, QUARTER // 2, D), lambda i, *_: (i, 0, 0))
+    out_type = jax.ShapeDtypeStruct((SHARDS, QUARTER // 2, D), jnp.float32)
+    again = [] if ds is None else [ds]
+    return pl.pallas_call(
+        rows1_kernel,
+        out_shape=(
+            jax.ShapeDtypeStruct(view, jnp.bfloat16),
+            jax.ShapeDtypeStruct((ROWS // 2 // rb, 1, rb), jnp.float32),
+            out_type,
+            out_type,
+        ),
         grid_spec=pltpu.PrefetchScalarGridSpec(
             num_scalar_prefetch=len(scalars),
-            grid=(ROWS // rb,),
-            in_specs=[block, pl.BlockSpec((1, 2, rb), lambda i, *_: (i, 0, 0))]
-            + [full(*r.shape) for r in recvs]
-            + [full(D, D)]
-            + ([block] if last else []),
-            out_specs=(block, pl.BlockSpec((1, 1, rb), lambda i, *_: (i, 0, 0)))
-            + ((full(ROWS // 2, D),) * 2 if last else (block,)),
-            scratch_shapes=[
-                pltpu.VMEM((rb, D), jnp.float32),
-                pltpu.VMEM((rb, BLOCK), jnp.float32),
-                pltpu.VMEM((rb, BLOCK), jnp.float32),
-            ],
-        ),
-        name="rows",
-    )(*scalars, scores, lse, *recvs, passages, *([add] if last else []))
+            grid=(ROWS // 2 // rb,),
+            in_specs=[
+                group,
+                pl.BlockSpec((1, 2, rb), lambda i, *_: (i, 0, 0)),
+                full_spec(*recv.shape),
+                group,
+                full_spec(D, D),
+                full_spec(D, D),
+            ]
+            + [pl.BlockSpec(memory_space=pl.ANY)] * len(again),
+            out_specs=(group, pl.BlockSpec((1, 1, rb), lambda i, *_: (i, 0, 0)), out, out),
+            scratch_shapes=ROW_SCRATCH,
+        ),
+        input_output_aliases={len(scalars) + 6: 0} if again else {},
+        name="rows1",
+    )(*scalars, scores.reshape(view), lse, recv, ds0.reshape(view), p0, p1, *again)
 
 
 def columns_kernel(pos_ref, ds_ref, q_ref, *outs):
@@ -385,27 +451,26 @@
     return [(i, (i + d) % n) for i in range(n)]
 
 
-def combine_kernel(own_ref, other_ref, *outs):
-    for base, group in ((0, outs[:5]), (512, outs[5:])):
-        at = lambda lo, n: own_ref[base + lo : base + lo + n] + other_ref[base + lo : base + lo + n]
-        group[0][...] = at(0, 128)
-        group[1][...] = at(128, 128)
-        group[2][...] = at(256, 64)
-        group[3][...] = at(320, 64)
-        group[4][...] = at(384, 128)
-
-
-def combine(own, other):
-    full = lambda n: pl.BlockSpec((n, D), lambda i: (0, 0))
-    sizes = (128, 128, 64, 64, 128) * 2
+def combine_kernel(own_ref, other_ref, *refs):
+    out_ref = refs[-1]
+    out_ref[:, :, :D] = own_ref[...] + other_ref[...]
+    if len(refs) == 2:
+        loss = refs[0][...]
+        out_ref[:, :, D:] = jnp.broadcast_to(loss[:, None, :], (*out_ref.shape[:2], BLOCK))
+
+
+def combine(own, other, *loss):
+    step = 8
+    width = D + BLOCK * len(loss)
+    block = lambda w: pl.BlockSpec((step, QUARTER // 2, w), lambda i: (i, 0, 0))
     return pl.pallas_call(
         combine_kernel,
-        out_shape=tuple(jax.ShapeDtypeStruct((n, D), jnp.float32) for n in sizes),
-        grid=(1,),
-        in_specs=[full(ROWS // 2)] * 2,
-        out_specs=tuple(full(n) for n in sizes),
+        out_shape=jax.ShapeDtypeStruct((SHARDS, QUARTER // 2, width), jnp.float32),
+        grid=(SHARDS // step,),
+        in_specs=[block(D), block(D)] + [pl.BlockSpec((step, BLOCK), lambda i: (i, 0))] * len(loss),
+        out_specs=block(width),
         name="combine",
-    )(own, other)
+    )(own, other, *loss)
 
 
 def send(value, axis, d, n=4):
@@ -414,17 +479,6 @@
 
 def together(*values):
     return lax.optimization_barrier(values)
-
-
-def near(low, high, axis):
-    return [send(low, axis, 1), send(high, axis, -1)]
-
-
-def far(c1, c3, near_p, near_m, axis):
-    h = near_p.shape[0]
-    s1 = jnp.concatenate([c1[:h] + near_p, c1[h:]], axis=0)
-    s3 = jnp.concatenate([c3[:h], c3[h:] + near_m], axis=0)
-    return [send(s1, axis, 1), send(s3, axis, -1)]
 
 
 def per_device(queries, passages, teacher, block_ids):
@@ -432,9 +486,10 @@
     me = my * 8 + mx * 2 + mc
     pos = jnp.stack([mz, my, mx, mc]).astype(jnp.int32)
     flat_ids = block_ids.reshape(-1)
-    exchange = functools.partial(
-        lax.all_to_all, axis_name=PLANE, split_axis=0, concat_axis=0, tiled=True
-    )
+
+    def exchange(value):
+        return lax.all_to_all(value, PLANE, split_axis=0, concat_axis=0, tiled=True)
+
     sent0 = pack(0, flat_ids, teacher)
     recv0 = exchange(sent0)
     ids1, _ = together(flat_ids, sent0)
@@ -444,46 +499,46 @@
     recv1 = exchange(sent1)
     ids2, _ = together(flat_ids, lse)
     sent2 = pack(2, ids2, teacher)
+    sent3 = pack(3, ids2, teacher)
     sent2, _ = together(sent2, recv1[0, 0, 0])
     recv2 = exchange(sent2)
     meta = recv0[:, BLOCK, : 2 * CAP].astype(jnp.int32).reshape(-1)
-    scalars = (pos,) + tuple(make_lists(meta))
+    lists = tuple(make_lists(meta))
     every = recv1[:, BLOCK:, :]
     top = jnp.max(every, axis=0)
-    lse = top + jnp.log(jnp.sum(jnp.exp(every - top[None]), axis=0))
-    lse = lse.reshape(8, 2, 256)
-    ds0, loss0, q0 = rows_call(scalars, s0, lse, [recv0, recv1], p0)
+    lse = (top + jnp.log(jnp.sum(jnp.exp(every - top[None]), axis=0))).reshape(8, 2, 256)
+    split = lse.transpose(1, 0, 2).reshape(2, SHARDS, 2, QUARTER)
+    lse_half = [split[:, :, h].reshape(2, 4, 256).transpose(1, 0, 2) for h in range(2)]
+    ds0, loss0 = rows0_call(lists, s0, lse, [recv0, recv1])
     g0 = columns_call(pos, ds0, queries)
     z0 = [g0[0], g0[1:3], g0[3:5], g0[5:7]]
     np0, nm0 = send(z0[2][0], "pb", 1), send(z0[2][1], "pb", -1)
     fp0, fm0 = send(z0[1][1], "pb", 1), send(z0[3][0], "pb", -1)
+
+    sent3, _ = together(sent3, recv2[0, 0, 0])
+    recv3 = exchange(sent3)
+    scalars = (pos,) + lists
+    ds1, loss_a, own_a, other_a = rows1_call(0, scalars, s1, lse_half[0], recv2, ds0, p0, p1)
+    swap_a = send(other_a, "c", 1, 2)
     sp0 = send(z0[1][0] + np0, "pb", 1)
     sm0 = send(z0[3][1] + nm0, "pb", -1)
-
-    ds1, loss1, own, other = rows_call(scalars, s1, lse, [recv2], p1, q0)
-    swapped = send(other, "c", 1, 2)
-    g1 = columns_call(pos, ds1, queries)
+    both_a = combine(own_a, swap_a)
+    both_a, _ = together(both_a, recv3[0, 0, 0])
+    got_a = exchange(both_a)
+    ds1, loss_b, own_b, other_b = rows1_call(1, scalars, s1, lse_half[1], recv3, ds0, p0, p1, ds1)
+    swap_b = send(other_b, "c", 1, 2)
+    g1 = columns_call(pos, ds1.reshape(ROWS, D), queries)
     z1 = [g1[0], g1[1:3], g1[3:5], g1[5:7]]
     np1, nm1 = send(z1[2][0], "pb", 1), send(z1[2][1], "pb", -1)
     fp1, fm1 = send(z1[1][1], "pb", 1), send(z1[3][0], "pb", -1)
-    a0, a1, a2, a3, a4, b0, b1, b2, b3, b4 = combine(own, swapped)
-    loss_sum = (loss0 + loss1).reshape(SHARDS, ROWS // SHARDS)
-    np1, nm1, apn, anm, bpn, bnm, loss_sum = together(
-        np1, nm1, *near(a2, a3, "x"), *near(b2, b3, "y"), loss_sum
-    )
-    af, bf = far(a1, a4, apn, anm, "x"), far(b1, b4, bpn, bnm, "y")
+    loss_ab = jnp.stack([loss_a.reshape(SHARDS, QUARTER), loss_b.reshape(SHARDS, QUARTER)], axis=1)
+    loss_sum = loss0.reshape(SHARDS, 2 * QUARTER) + loss_ab.reshape(SHARDS, 2 * QUARTER)
+    loss_sum = jnp.pad(loss_sum, ((0, 0), (0, BLOCK - 2 * QUARTER)))
+    both_b = combine(own_b, swap_b, loss_sum)
+    both_b, _ = together(both_b, got_a[0, 0, 0])
+    got_b = exchange(both_b)
     sp1 = send(z1[1][0] + np1, "pb", 1)
     sm1 = send(z1[3][1] + nm1, "pb", -1)
-    loss_part = exchange(loss_sum)
-    af0, af1, bf0, bf1 = together(*af, *bf)
-    cut = lambda v: [v[32 * i : 32 * (i + 1)] for i in range(4)]
-    a, b = cut(a0 + af0 + af1), cut(b0 + bf0 + bf1)
-    apn, anm, bpn, bnm = together(
-        *near(a[2][:16], a[2][16:], "y"), *near(b[2][:16], b[2][16:], "x")
-    )
-    af, bf = far(a[1], a[3], apn, anm, "y"), far(b[1], b[3], bpn, bnm, "x")
-    af0, af1, bf0, bf1 = together(*af, *bf)
-    grad_queries = jnp.concatenate([a[0] + af0 + af1, b[0] + bf0 + bf1], axis=0)
 
     h = D // 8
     parts = [
@@ -493,13 +548,17 @@
         z1[0][h:] + fp1 + sm1,
     ]
     gp0, gp1 = jnp.concatenate(parts[:2]), jnp.concatenate(parts[2:])
+    grad_passages = jnp.stack(
+        [gp0.reshape(4, BLOCK // 2, D), gp1.reshape(4, BLOCK // 2, D)], axis=1
+    ).reshape(4 * BLOCK, D)
+    chips = SHARDS // 2
+    sum_a = jnp.sum(got_a.reshape(chips, QUARTER, D), axis=0)
+    sum_b = jnp.sum(got_b[:, :, :D].reshape(chips, QUARTER, D), axis=0)
+    grad_queries = jnp.concatenate([sum_a, sum_b], axis=0)
     lse_rows = lax.dynamic_slice_in_dim(
         lse[:, 0, :].reshape(ROWS), me * (ROWS // SHARDS), ROWS // SHARDS
     )
-    loss = jnp.sum(loss_part, axis=0) + lse_rows
-    grad_passages = jnp.stack(
-        [gp0.reshape(4, BLOCK // 2, D), gp1.reshape(4, BLOCK // 2, D)], axis=1
-    ).reshape(4 * BLOCK, D)
+    loss = jnp.sum(got_b[:, 0, D : D + 2 * QUARTER], axis=0) + lse_rows
     return loss, grad_queries, grad_passages
 
 

time: 293 us -> 292 us (level)
  Pallas kernels: 110 us -> 121 us
  waiting for transfers between devices: 91.8 us -> 80.9 us
  local copies, waits for them, and re-layouts: 7.55 us -> 14.3 us
  other arithmetic: 18.5 us -> 13.6 us
    all_to_all x4 -> x6, waiting for transfers between devices: 57.5 us -> 43.7 us  [exchange(): return lax.all_to_all(value, PLANE, split_axis=0, concat_axis=0, tiled=True)]
    ppermute x29 -> x14, starting transfers between devices: 31.9 us -> 18.8 us  [send(): return lax.ppermute(value, axis, ring(d, n))]
    all_to_all x4 -> x6, starting transfers between devices: 29 us -> 40.2 us  [exchange(): return lax.all_to_all(value, PLANE, split_axis=0, concat_axis=0, tiled=True)]
    pallas_call x3 -> x5, Pallas kernels: 47.9 us -> 55.1 us  [the longest x2 31.6 us: rows1_call(): pl.pallas_call(rows1_kernel, out_shape=(jax.ShapeDtypeStruct(view, jnp.bf...]
    unnamed x31 -> x39, local copies, waits for them, and re-layouts: 2.2 us -> 7.38 us
    pallas_call x3 -> x4, Pallas kernels: 17.9 us -> 22.3 us  [pack(): pl.pallas_call(functools.partial(pack_kernel, piece), out_shape=jax.Shape...]
    add x8 -> x3, other arithmetic: 3.99 us -> 0.6 us  [the longest x1 0.59 us: per_device(): loss = jnp.sum(got_b[:, 0, D:D + 2 * QUARTER], axis=0) + lse_rows]
    concatenate x9 -> x1, other arithmetic: 4.09 us -> 0.72 us  [per_device(): grad_queries = jnp.concatenate([sum_a, sum_b], axis=0)]
  transfers between devices with their start and end apart: 33 -> 20, of which waited for: 15 -> 12; matrix products, arithmetic and copies ran while one was open for 8% -> 6% of each run, Pallas kernels for 28% -> 40%
where the time goes in v2:
time: 292 us; the launch traced here: 290 us
  Pallas kernels  121 us (41%)
  waiting for transfers between devices  80.9 us (28%)
  starting transfers between devices  59 us (20%)
  local copies, waits for them, and re-layouts  14.3 us (5%)
  other arithmetic  13.6 us (5%)
    all_to_all x6, waiting for transfers between devices, exchange(): return lax.all_to_all(value, PLANE, split_axis=0, concat_axis=0, tiled=True)  43.7 us
    all_to_all x6, starting transfers between devices, exchange(): return lax.all_to_all(value, PLANE, split_axis=0, concat_axis=0, tiled=True)  40.2 us
    ppermute x14, waiting for transfers between devices, send(): return lax.ppermute(value, axis, ring(d, n))  37.3 us
    pallas_call x2, Pallas kernels, rows1_call(): pl.pallas_call(rows1_kernel, out_shape=(jax.ShapeDtypeStruct(view, jnp.bf...  31.6 us
    pallas_call x4, Pallas kernels, pack(): pl.pallas_call(functools.partial(pack_kernel, piece), out_shape=jax.Shape...  22.3 us
    pallas_call x2, Pallas kernels, columns_call(): pl.pallas_call(columns_kernel, out_shape=tuple((jax.ShapeDtypeStruct((n,...  19.6 us
    ppermute x14, starting transfers between devices, send(): return lax.ppermute(value, axis, ring(d, n))  18.8 us
    pallas_call x1, Pallas kernels, score(): pl.pallas_call(score_kernel, out_shape=(scores, scores, jax.ShapeDtypeStr...  18.7 us
  transfers between devices with their start and end apart: 20, of which 12 were waited for; matrix products, arithmetic and copies ran while one was open for 6% of the time, Pallas kernels for 40%

profile of v2, /device:TPU:1, one launch (start us, length us, event | category | flops | bytes accessed | tf_op | source)
XLA Modules:
  0.0 290.2 jit_solution(5717805692357883663)
XLA Ops:
  2.0 6.0 %pack.4 = f32[32,136,128]{2,1,0:T(8,128)} custom-call(s32[64]{0:T(128)} %reshape.62.ids_ref, f32[2048,512]{1,0:T(8,128)} %teacher_ref.7), custom_call_target="tpu_custom_call" | custom-call | tf_op jit(solution)/shard_map/pack/pallas_call | solution.py:94
  8.0 8.6 %all-to-all-start = ((f32[32,136,128]{2,1,0:T(8,128)}), f32[32,136,128]{2,1,0:T(8,128)S(1)}, u32[]{:S(2)}, u32[]{:S(2)}) async-start(f32[32,136,128]{2,1,0:T(8,128)} %pack.4), calls=%async_computation | async-start | bytes 4456448 | tf_op jit(solution)/shard_map/all_to_all | solution.py:491
  16.6 18.7 %score.1 = (f32[2048,1024]{1,0:T(8,128)}, f32[2048,1024]{1,0:T(8,128)}, f32[8,2,256]{2,1,0:T(2,128)}, bf16[1024,1024]{1,0:T(8,128)(2,1)}, bf16[1024,1024]{1,0:T(8,128)(2,1)}) custom-call(bf16[2048,1024]{1,0:T(8,128)(2,1)} %q_ref.5, bf16[2048,1024]{1,0:T(8,128)(2,1)} %p_ref.1, f32[2048,512]{1,0:T(8,128)} %teacher_ref.7), custom_call_target="tpu_custom_call" | custom-call | tf_op jit(solution)/shard_map/score/pallas_call | solution.py:217
  36.6 5.9 %pack.5.sent_ref = f32[32,160,128]{2,1,0:T(8,128)} custom-call(s32[64]{0:T(128)} %reshape.62.ids_ref, f32[2048,512]{1,0:T(8,128)} %teacher_ref.7), custom_call_target="tpu_custom_call" | custom-call | tf_op jit(solution)/shard_map/pack/pallas_call | solution.py:94
  44.1 2.5 all-to-all-done
  48.1 5.4 %all-to-all-start.1 = ((f32[32,160,128]{2,1,0:T(8,128)}), f32[32,160,128]{2,1,0:T(8,128)S(1)}, u32[]{:S(2)}, u32[]{:S(2)}) async-start(f32[32,160,128]{2,1,0:T(8,128)} %fill_lse.1), calls=%async_computation.1 | async-start | bytes 5242880 | tf_op jit(solution)/shard_map/all_to_all | solution.py:491
  53.5 5.1 %pack.7 = f32[32,128,128]{2,1,0:T(8,128)} custom-call(s32[64]{0:T(128)} %reshape.62.ids_ref, f32[2048,512]{1,0:T(8,128)} %teacher_ref.7), custom_call_target="tpu_custom_call" | custom-call | tf_op jit(solution)/shard_map/pack/pallas_call | solution.py:94
  58.7 28.8 %all-to-all-done.1 = f32[32,160,128]{2,1,0:T(8,128)S(1)} async-done(((f32[32,160,128]{2,1,0:T(8,128)}), f32[32,160,128]{2,1,0:T(8,128)S(1)}, u32[]{:S(2)}, u32[]{:S(2)}) %all-to-all-start.1) | async-done | bytes 2621472 | tf_op jit(solution)/shard_map/all_to_all | solution.py:491
  87.5 6.9 %all-to-all-start.3 = ((f32[32,128,128]{2,1,0:T(8,128)}), f32[32,128,128]{2,1,0:T(8,128)}, u32[]{:S(2)}, u32[]{:S(2)}) async-start(f32[32,128,128]{2,1,0:T(8,128)} %pack.7), calls=%async_computation.3 | async-start | bytes 4194304 | tf_op jit(solution)/shard_map/all_to_all | solution.py:491
  94.4 5.2 %pack.6 = f32[32,128,128]{2,1,0:T(8,128)} custom-call(s32[64]{0:T(128)} %reshape.62.ids_ref, f32[2048,512]{1,0:T(8,128)} %teacher_ref.7), custom_call_target="tpu_custom_call" | custom-call | tf_op jit(solution)/shard_map/pack/pallas_call | solution.py:94
  101.8 4.2 %make_lists.1 = (s32[17]{0:T(128)}, s32[128]{0:T(128)}, s32[128]{0:T(128)}) custom-call(s32[256]{0:T(256)} %convert_element_type.10.meta_ref), custom_call_target="tpu_custom_call" | custom-call | tf_op jit(solution)/shard_map/make_lists/pallas_call | solution.py:174
  107.3 15.1 %rows0.1 = (bf16[2048,1024]{1,0:T(8,128)(2,1)}, f32[8,1,256]{2,1,0:T(1,128)}) custom-call(s32[17]{0:T(128)} %get-tuple-element.37.start_ref, s32[128]{0:T(128)} %get-tuple-element.38.row_ref, s32[128]{0:T(128)} %get-tuple-element.39.block_ref, f32[2048,1024]{1,0:T(8,128)} %get-tuple-element.44.s_ref, f32[8,2,256]{2,1,0:T(2,128)} %copy-done.14, ...), custom_call_target="tpu_custom_call" | custom-call | tf_op jit(solution)/shard_map/rows0/pallas_call | solution.py:316
  122.8 7.7 %all-to-all-start.2 = ((f32[32,128,128]{2,1,0:T(8,128)}), f32[32,128,128]{2,1,0:T(8,128)S(1)}, u32[]{:S(2)}, u32[]{:S(2)}) async-start(f32[32,128,128]{2,1,0:T(8,128)} %pack.6), calls=%async_computation.2 | async-start | bytes 4194304 | tf_op jit(solution)/shard_map/all_to_all | solution.py:491
  130.5 15.8 %rows1.2 = (bf16[32,2,32,1024]{3,2,1,0:T(8,128)(2,1)}, f32[4,1,256]{2,1,0:T(1,128)}, f32[32,16,1024]{2,1,0:T(8,128)}, f32[32,16,1024]{2,1,0:T(8,128)}) custom-call(s32[4]{0:T(128)} %pad_add_fusion.pos_ref, s32[17]{0:T(128)} %get-tuple-element.37.start_ref, s32[128]{0:T(128)} %get-tuple-element.38.row_ref, s32[128]{0:T(128)} %get-tuple-element.39.block_ref, ...), custom_call_target="tpu_custom_call" | custom-call | tf_op jit(solution)/shard_map/rows1/pallas_call | solution.py:391
  147.2 11.9 %all-to-all-done.2 = f32[32,128,128]{2,1,0:T(8,128)S(1)} async-done(((f32[32,128,128]{2,1,0:T(8,128)}), f32[32,128,128]{2,1,0:T(8,128)S(1)}, u32[]{:S(2)}, u32[]{:S(2)}) %all-to-all-start.2) | async-done | bytes 2097184 | tf_op jit(solution)/shard_map/all_to_all | solution.py:491
  160.5 15.8 %rows1.3 = (bf16[32,2,32,1024]{3,2,1,0:T(8,128)(2,1)}, f32[4,1,256]{2,1,0:T(1,128)}, f32[32,16,1024]{2,1,0:T(8,128)}, f32[32,16,1024]{2,1,0:T(8,128)}) custom-call(s32[4]{0:T(128)} %pad_add_fusion.pos_ref, s32[17]{0:T(128)} %get-tuple-element.37.start_ref, s32[128]{0:T(128)} %get-tuple-element.38.row_ref, ...), custom_call_target="tpu_custom_call", output_to_operand_aliasing={{0}: (10, {})} | custom-call | tf_op jit(solution)/shard_map/rows1/pallas_call | solution.py:391
  178.0 4.2 %combine.3 = f32[32,16,1024]{2,1,0:T(8,128)} custom-call(f32[32,16,1024]{2,1,0:T(8,128)} %get-tuple-element.54.own_ref, f32[32,16,1024]{2,1,0:T(8,128)} %collective-permute-done.1.other_ref), custom_call_target="tpu_custom_call" | custom-call | tf_op jit(solution)/shard_map/combine/pallas_call | solution.py:466
  182.2 4.0 %all-to-all-start.5 = ((f32[32,16,1024]{2,1,0:T(8,128)}), f32[32,16,1024]{2,1,0:T(8,128)S(1)}, u32[]{:S(2)}, u32[]{:S(2)}) async-start(f32[32,16,1024]{2,1,0:T(8,128)} %combine.3), calls=%async_computation.5 | async-start | bytes 4194304 | tf_op jit(solution)/shard_map/all_to_all | solution.py:491
  186.2 9.7 %columns.2 = (f32[256,1024]{1,0:T(8,128)}, f32[128,1024]{1,0:T(8,128)}, f32[128,1024]{1,0:T(8,128)}, f32[128,1024]{1,0:T(8,128)}, f32[128,1024]{1,0:T(8,128)}, /*index=5*/f32[128,1024]{1,0:T(8,128)}, f32[128,1024]{1,0:T(8,128)}) custom-call(s32[4]{0:T(128)} %pad_add_fusion.pos_ref, bf16[2048,1024]{1,0:T(8,128)(2,1)} %get-tuple-element.45.ds_ref, ...), custom_call_target="tpu_custom_call" | custom-call | tf_op jit(solution)/shard_map/columns/pallas_call | solution.py:437
  196.1 9.8 %columns.3 = (f32[256,1024]{1,0:T(8,128)}, f32[128,1024]{1,0:T(8,128)}, f32[128,1024]{1,0:T(8,128)}, f32[128,1024]{1,0:T(8,128)}, f32[128,1024]{1,0:T(8,128)}, /*index=5*/f32[128,1024]{1,0:T(8,128)}, f32[128,1024]{1,0:T(8,128)}) custom-call(s32[4]{0:T(128)} %pad_add_fusion.pos_ref, bf16[2048,1024]{1,0:T(8,128)(2,1)} %bitcast.34, bf16[2048,1024]{1,0:T(8,128)(2,1)} %q_ref.5), custom_call_target="tpu_custom_call" | custom-call | tf_op jit(solution)/shard_map/columns/pallas_call | solution.py:437
  205.9 2.5 collective-permute-start.8
  211.2 4.2 %combine.2 = f32[32,16,1152]{2,1,0:T(8,128)} custom-call(f32[32,16,1024]{2,1,0:T(8,128)} %get-tuple-element.49.own_ref, f32[32,16,1024]{2,1,0:T(8,128)} %collective-permute-done.other_ref, f32[32,128]{1,0:T(8,128)} %pad.4.refs_0_), custom_call_target="tpu_custom_call" | custom-call | tf_op jit(solution)/shard_map/combine/pallas_call | solution.py:466
  216.8 7.7 %all-to-all-start.4 = ((f32[32,16,1152]{2,1,0:T(8,128)}), f32[32,16,1152]{2,1,0:T(8,128)S(1)}, u32[]{:S(2)}, u32[]{:S(2)}) async-start(f32[32,16,1152]{2,1,0:T(8,128)} %combine.2), calls=%async_computation.4 | async-start | bytes 4718592 | tf_op jit(solution)/shard_map/all_to_all | solution.py:491
  224.5 3.0 %collective-permute-start.6 = (f32[128,1024]{1,0:T(8,128)}, f32[128,1024]{1,0:T(8,128)S(1)}, u32[]{:S(2)}, u32[]{:S(2)}) collective-permute-start(f32[128,1024]{1,0:T(8,128)} %get-tuple-element.62), channel_id=1, source_target_pairs={{0,96},{32,0},{64,32},{96,64},{1,97},{33,1},{65,33},{97,65},{2,98}... | collective-permute-start | bytes 1572872 | tf_op jit(solution)/shard_map/ppermute | solution.py:477
  230.9 2.2 add.77
  238.8 3.3 %collective-permute-start.4 = (f32[128,1024]{1,0:T(8,128)}, f32[128,1024]{1,0:T(8,128)}, u32[]{:S(2)}, u32[]{:S(2)}) collective-permute-start(f32[128,1024]{1,0:T(8,128)} %get-tuple-element.59), channel_id=1, source_target_pairs={{0,96},{32,0},{64,32},{96,64},{1,97},{33,1},{65,33},{97,65},{2,98}... | collective-permute-start | bytes 1572872 | tf_op jit(solution)/shard_map/ppermute | solution.py:477
  243.1 7.0 %collective-permute-done.10 = f32[128,1024]{1,0:T(8,128)S(1)} collective-permute-done((f32[128,1024]{1,0:T(8,128)}, f32[128,1024]{1,0:T(8,128)S(1)}, u32[]{:S(2)}, u32[]{:S(2)}) %collective-permute-start.10) | collective-permute-done | bytes 524320 | tf_op jit(solution)/shard_map/ppermute | solution.py:477
  252.0 4.0 %collective-permute-done.9 = f32[128,1024]{1,0:T(8,128)S(1)} collective-permute-done((f32[128,1024]{1,0:T(8,128)S(1)}, f32[128,1024]{1,0:T(8,128)S(1)}, u32[]{:S(2)}, u32[]{:S(2)}) %collective-permute-start.9) | collective-permute-done | bytes 524320 | tf_op jit(solution)/shard_map/ppermute | solution.py:477
  258.2 3.1 %collective-permute-done.13 = f32[128,1024]{1,0:T(8,128)} collective-permute-done((f32[128,1024]{1,0:T(8,128)}, f32[128,1024]{1,0:T(8,128)}, u32[]{:S(2)}, u32[]{:S(2)}) %collective-permute-start.13) | collective-permute-done | bytes 524320 | tf_op jit(solution)/shard_map/ppermute | solution.py:477
  263.2 9.3 %collective-permute-done.4 = f32[128,1024]{1,0:T(8,128)} collective-permute-done((f32[128,1024]{1,0:T(8,128)}, f32[128,1024]{1,0:T(8,128)}, u32[]{:S(2)}, u32[]{:S(2)}) %collective-permute-start.4) | collective-permute-done | bytes 524320 | tf_op jit(solution)/shard_map/ppermute | solution.py:477
  272.6 6.1 %collective-permute-done.3 = f32[128,1024]{1,0:T(8,128)} collective-permute-done((f32[128,1024]{1,0:T(8,128)}, f32[128,1024]{1,0:T(8,128)}, u32[]{:S(2)}, u32[]{:S(2)}) %collective-permute-start.3) | collective-permute-done | bytes 524320 | tf_op jit(solution)/shard_map/ppermute | solution.py:477
  278.7 5.1 %collective-permute-done.7 = f32[128,1024]{1,0:T(8,128)} collective-permute-done((f32[128,1024]{1,0:T(8,128)}, f32[128,1024]{1,0:T(8,128)}, u32[]{:S(2)}, u32[]{:S(2)}) %collective-permute-start.7) | collective-permute-done | bytes 524320 | tf_op jit(solution)/shard_map/ppermute | solution.py:477
  (104 shorter events, 40.1 us)
Async XLA Ops:
  8.0 38.7 %all-to-all-start = ((f32[32,136,128]{2,1,0:T(8,128)}), f32[32,136,128]{2,1,0:T(8,128)S(1)}, u32[]{:S(2)}, u32[]{:S(2)}) async-start(f32[32,136,128]{2,1,0:T(8,128)} %pack.4), calls=%async_computation | async-start | bytes 4456448 | tf_op jit(solution)/shard_map/all_to_all | solution.py:491
  48.1 39.4 %all-to-all-start.1 = ((f32[32,160,128]{2,1,0:T(8,128)}), f32[32,160,128]{2,1,0:T(8,128)S(1)}, u32[]{:S(2)}, u32[]{:S(2)}) async-start(f32[32,160,128]{2,1,0:T(8,128)} %fill_lse.1), calls=%async_computation.1 | async-start | bytes 5242880 | tf_op jit(solution)/shard_map/all_to_all | solution.py:491
  87.5 18.6 %copy-start = (f32[32,160,128]{2,1,0:T(8,128)}, f32[32,160,128]{2,1,0:T(8,128)S(1)}, u32[]{:S(2)}) copy-start(f32[32,160,128]{2,1,0:T(8,128)S(1)} %all-to-all-done.1) | copy-start | bytes 7864324
  87.5 35.3 %all-to-all-start.3 = ((f32[32,128,128]{2,1,0:T(8,128)}), f32[32,128,128]{2,1,0:T(8,128)}, u32[]{:S(2)}, u32[]{:S(2)}) async-start(f32[32,128,128]{2,1,0:T(8,128)} %pack.7), calls=%async_computation.3 | async-start | bytes 4194304 | tf_op jit(solution)/shard_map/all_to_all | solution.py:491
  122.8 36.3 %all-to-all-start.2 = ((f32[32,128,128]{2,1,0:T(8,128)}), f32[32,128,128]{2,1,0:T(8,128)S(1)}, u32[]{:S(2)}, u32[]{:S(2)}) async-start(f32[32,128,128]{2,1,0:T(8,128)} %pack.6), calls=%async_computation.2 | async-start | bytes 4194304 | tf_op jit(solution)/shard_map/all_to_all | solution.py:491
  146.3 31.7 %collective-permute-start.1 = (f32[32,16,1024]{2,1,0:T(8,128)}, f32[32,16,1024]{2,1,0:T(8,128)}, u32[]{:S(2)}, u32[]{:S(2)}) collective-permute-start(f32[32,16,1024]{2,1,0:T(8,128)} %get-tuple-element.55), channel_id=1, source_target_pairs={{0,1},{1,0},{2,3},{3,2},{4,5},{5,4},{6,7},{7,6},{8,9},{9,8},{10,11... | collective-permute-start | bytes 6291464 | tf_op jit(solution)/shard_map/ppermute | solution.py:477
  176.3 34.9 %collective-permute-start = (f32[32,16,1024]{2,1,0:T(8,128)}, f32[32,16,1024]{2,1,0:T(8,128)}, u32[]{:S(2)}, u32[]{:S(2)}) collective-permute-start(f32[32,16,1024]{2,1,0:T(8,128)} %get-tuple-element.50), channel_id=1, source_target_pairs={{0,1},{1,0},{2,3},{3,2},{4,5},{5,4},{6,7},{7,6},{8,9},{9,8},{10,11... | collective-permute-start | bytes 6291464 | tf_op jit(solution)/shard_map/ppermute | solution.py:477
  182.2 33.3 %all-to-all-start.5 = ((f32[32,16,1024]{2,1,0:T(8,128)}), f32[32,16,1024]{2,1,0:T(8,128)S(1)}, u32[]{:S(2)}, u32[]{:S(2)}) async-start(f32[32,16,1024]{2,1,0:T(8,128)} %combine.3), calls=%async_computation.5 | async-start | bytes 4194304 | tf_op jit(solution)/shard_map/all_to_all | solution.py:491
  186.2 9.7 %copy-start.18 = (f32[4,1,256]{2,1,0:T(1,128)S(1)}, f32[4,1,256]{2,1,0:T(1,128)}, u32[]{:S(2)}) copy-start(f32[4,1,256]{2,1,0:T(1,128)} %get-tuple-element.53) | copy-start | bytes 12292
  186.2 9.8 %copy-start.17 = (f32[4,1,256]{2,1,0:T(1,128)S(1)}, f32[4,1,256]{2,1,0:T(1,128)}, u32[]{:S(2)}) copy-start(f32[4,1,256]{2,1,0:T(1,128)} %get-tuple-element.52) | copy-start | bytes 12292
  196.1 14.3 %copy-start.16 = (f32[8,1,256]{2,1,0:T(1,128)S(1)}, f32[8,1,256]{2,1,0:T(1,128)}, u32[]{:S(2)}) copy-start(f32[8,1,256]{2,1,0:T(1,128)} %get-tuple-element.51) | copy-start | bytes 24580
  205.9 22.0 %collective-permute-start.8 = (f32[128,1024]{1,0:T(8,128)}, f32[128,1024]{1,0:T(8,128)}, u32[]{:S(2)}, u32[]{:S(2)}) collective-permute-start(f32[128,1024]{1,0:T(8,128)} %get-tuple-element.66), channel_id=1, source_target_pairs={{0,32},{32,64},{64,96},{96,0},{1,33},{33,65},{65,97},{97,1},{2,34}... | collective-permute-start | bytes 1572872 | tf_op jit(solution)/shard_map/ppermute | solution.py:477
  208.5 21.6 %collective-permute-start.12 = (f32[128,1024]{1,0:T(8,128)}, f32[128,1024]{1,0:T(8,128)S(1)}, u32[]{:S(2)}, u32[]{:S(2)}) collective-permute-start(f32[128,1024]{1,0:T(8,128)} %get-tuple-element.70), channel_id=1, source_target_pairs={{0,96},{32,0},{64,32},{96,64},{1,97},{33,1},{65,33},{97,65},{2,98}... | collective-permute-start | bytes 1572872 | tf_op jit(solution)/shard_map/ppermute | solution.py:477
  210.3 23.4 %collective-permute-start.2 = (f32[128,1024]{1,0:T(8,128)}, f32[128,1024]{1,0:T(8,128)}, u32[]{:S(2)}, u32[]{:S(2)}) collective-permute-start(f32[128,1024]{1,0:T(8,128)} %get-tuple-element.58), channel_id=1, source_target_pairs={{0,32},{32,64},{64,96},{96,0},{1,33},{33,65},{65,97},{97,1},{2,34}... | collective-permute-start | bytes 1572872 | tf_op jit(solution)/shard_map/ppermute | solution.py:477
  215.5 13.5 %copy-start.9 = (f32[128,1024]{1,0:T(8,128)S(1)}, f32[128,1024]{1,0:T(8,128)}, u32[]{:S(2)}) copy-start(f32[128,1024]{1,0:T(8,128)} %get-tuple-element.65) | copy-start | bytes 1572868
  216.8 71.7 %all-to-all-start.4 = ((f32[32,16,1152]{2,1,0:T(8,128)}), f32[32,16,1152]{2,1,0:T(8,128)S(1)}, u32[]{:S(2)}, u32[]{:S(2)}) async-start(f32[32,16,1152]{2,1,0:T(8,128)} %combine.2), calls=%async_computation.4 | async-start | bytes 4718592 | tf_op jit(solution)/shard_map/all_to_all | solution.py:491
  224.5 10.6 %copy-start.8 = (f32[128,1024]{1,0:T(8,128)S(1)}, f32[128,1024]{1,0:T(8,128)}, u32[]{:S(2)}) copy-start(f32[128,1024]{1,0:T(8,128)} %get-tuple-element.57) | copy-start | bytes 1572868
  224.5 14.4 %collective-permute-start.6 = (f32[128,1024]{1,0:T(8,128)}, f32[128,1024]{1,0:T(8,128)S(1)}, u32[]{:S(2)}, u32[]{:S(2)}) collective-permute-start(f32[128,1024]{1,0:T(8,128)} %get-tuple-element.62), channel_id=1, source_target_pairs={{0,96},{32,0},{64,32},{96,64},{1,97},{33,1},{65,33},{97,65},{2,98}... | collective-permute-start | bytes 1572872 | tf_op jit(solution)/shard_map/ppermute | solution.py:477
  227.5 22.6 %collective-permute-start.10 = (f32[128,1024]{1,0:T(8,128)}, f32[128,1024]{1,0:T(8,128)S(1)}, u32[]{:S(2)}, u32[]{:S(2)}) collective-permute-start(f32[128,1024]{1,0:T(8,128)} %get-tuple-element.67), channel_id=1, source_target_pairs={{0,96},{32,0},{64,32},{96,64},{1,97},{33,1},{65,33},{97,65},{2,98}... | collective-permute-start | bytes 1572872 | tf_op jit(solution)/shard_map/ppermute | solution.py:477
  228.0 22.9 %collective-permute-start.11 = (f32[128,1024]{1,0:T(8,128)}, f32[128,1024]{1,0:T(8,128)S(1)}, u32[]{:S(2)}, u32[]{:S(2)}) collective-permute-start(f32[128,1024]{1,0:T(8,128)} %get-tuple-element.68), channel_id=1, source_target_pairs={{0,32},{32,64},{64,96},{96,0},{1,33},{33,65},{65,97},{97,1},{2,34}... | collective-permute-start | bytes 1572872 | tf_op jit(solution)/shard_map/ppermute | solution.py:477
  229.0 13.2 %copy-start.7 = (f32[128,1024]{1,0:T(8,128)S(1)}, f32[128,1024]{1,0:T(8,128)}, u32[]{:S(2)}) copy-start(f32[128,1024]{1,0:T(8,128)} %get-tuple-element.61) | copy-start | bytes 1572868
  230.1 25.9 %collective-permute-start.9 = (f32[128,1024]{1,0:T(8,128)S(1)}, f32[128,1024]{1,0:T(8,128)S(1)}, u32[]{:S(2)}, u32[]{:S(2)}) collective-permute-start(f32[128,1024]{1,0:T(8,128)S(1)} %add.73), channel_id=1, source_target_pairs={{0,32},{32,64},{64,96},{96,0},{1,33},{33,65},{65,97},{97,1},{2,34}... | collective-permute-start | bytes 1572872 | tf_op jit(solution)/shard_map/ppermute | solution.py:477
  230.9 27.2 %copy-start.15 = (f32[8,2,256]{2,1,0:T(2,128)S(1)}, f32[8,2,256]{2,1,0:T(2,128)}, u32[]{:S(2)}) copy-start(f32[8,2,256]{2,1,0:T(2,128)} %copy-done.14) | copy-start | bytes 49156
  230.9 30.4 %copy-start.6 = (f32[256,1024]{1,0:T(8,128)S(1)}, f32[256,1024]{1,0:T(8,128)}, u32[]{:S(2)}) copy-start(f32[256,1024]{1,0:T(8,128)} %get-tuple-element.64) | copy-start | bytes 3145732
  233.7 27.6 %collective-permute-start.13 = (f32[128,1024]{1,0:T(8,128)}, f32[128,1024]{1,0:T(8,128)}, u32[]{:S(2)}, u32[]{:S(2)}) collective-permute-start(f32[128,1024]{1,0:T(8,128)} %add.77), channel_id=1, source_target_pairs={{0,96},{32,0},{64,32},{96,64},{1,97},{33,1},{65,33},{97,65},{2,98}... | collective-permute-start | bytes 1572872 | tf_op jit(solution)/shard_map/ppermute | solution.py:477
  238.8 33.7 %collective-permute-start.4 = (f32[128,1024]{1,0:T(8,128)}, f32[128,1024]{1,0:T(8,128)}, u32[]{:S(2)}, u32[]{:S(2)}) collective-permute-start(f32[128,1024]{1,0:T(8,128)} %get-tuple-element.59), channel_id=1, source_target_pairs={{0,96},{32,0},{64,32},{96,64},{1,97},{33,1},{65,33},{97,65},{2,98}... | collective-permute-start | bytes 1572872 | tf_op jit(solution)/shard_map/ppermute | solution.py:477
  250.1 6.0 %copy-start.11 = (f32[128,1024]{1,0:T(8,128)}, f32[128,1024]{1,0:T(8,128)S(1)}, u32[]{:S(2)}) copy-start(f32[128,1024]{1,0:T(8,128)S(1)} %collective-permute-done.10) | copy-start | bytes 1572868
  250.1 22.5 %collective-permute-start.5 = (f32[128,1024]{1,0:T(8,128)}, f32[128,1024]{1,0:T(8,128)}, u32[]{:S(2)}, u32[]{:S(2)}) collective-permute-start(f32[128,1024]{1,0:T(8,128)} %get-tuple-element.60), channel_id=1, source_target_pairs={{0,32},{32,64},{64,96},{96,0},{1,33},{33,65},{65,97},{97,1},{2,34}... | collective-permute-start | bytes 1572872 | tf_op jit(solution)/shard_map/ppermute | solution.py:477
  250.9 5.2 %copy-start.12 = (f32[128,1024]{1,0:T(8,128)}, f32[128,1024]{1,0:T(8,128)S(1)}, u32[]{:S(2)}) copy-start(f32[128,1024]{1,0:T(8,128)S(1)} %collective-permute-done.11) | copy-start | bytes 1572868
  250.9 27.8 %collective-permute-start.3 = (f32[128,1024]{1,0:T(8,128)}, f32[128,1024]{1,0:T(8,128)}, u32[]{:S(2)}, u32[]{:S(2)}) collective-permute-start(f32[128,1024]{1,0:T(8,128)} %add.67), channel_id=1, source_target_pairs={{0,32},{32,64},{64,96},{96,0},{1,33},{33,65},{65,97},{97,1},{2,34}... | collective-permute-start | bytes 1572872 | tf_op jit(solution)/shard_map/ppermute | solution.py:477
  256.9 26.9 %collective-permute-start.7 = (f32[128,1024]{1,0:T(8,128)}, f32[128,1024]{1,0:T(8,128)}, u32[]{:S(2)}, u32[]{:S(2)}) collective-permute-start(f32[128,1024]{1,0:T(8,128)} %add.71), channel_id=1, source_target_pairs={{0,96},{32,0},{64,32},{96,64},{1,97},{33,1},{65,33},{97,65},{2,98}... | collective-permute-start | bytes 1572872 | tf_op jit(solution)/shard_map/ppermute | solution.py:477
  263.1 20.7 %copy-start.5 = (f32[256,1024]{1,0:T(8,128)S(1)}, f32[256,1024]{1,0:T(8,128)}, u32[]{:S(2)}) copy-start(f32[256,1024]{1,0:T(8,128)} %get-tuple-element.56) | copy-start | bytes 3145732
  (7 other events, 9.1 us)

commit v3 on v2

--- a/solution.py
+++ b/solution.py
@@ -20,6 +20,7 @@
 PACK_STEP = 8
 QUARTER = 32
 LSE_ROWS = 32
+SUM_ROWS = 256
 PLANE = ("y", "x", "c")
 SCORE_SCALE = 0.0625
 GRAD_SCALE = 64.0
@@ -79,17 +80,14 @@
         else:
             for pair in range(CAP // 2):
                 first = pltpu.roll(tiles[2 * pair], BLOCK // 2, 1)
-                both = jnp.where(quarter < 2, first, tiles[2 * pair + 1])
-                for end in range(2):
-                    at = 2 * QUARTER * end + QUARTER * (piece - 2)
-                    out = QUARTER * (2 * pair + end)
-                    out_ref[j, out : out + QUARTER, :] = both[at : at + QUARTER]
+                rows = slice(pair * BLOCK, (pair + 1) * BLOCK)
+                out_ref[j, rows, :] = jnp.where(quarter < 2, first, tiles[2 * pair + 1])
         if piece == 0:
             out_ref[j, BLOCK:, :] = meta
 
 
 def pack(piece, ids, teacher):
-    rows = BLOCK + (8 if piece == 0 else 0)
+    rows = (BLOCK + 8, BLOCK, 2 * BLOCK)[piece]
     total = rows + (LSE_ROWS if piece == 1 else 0)
     return pl.pallas_call(
         functools.partial(pack_kernel, piece),
@@ -332,88 +330,94 @@
 
 
 def rows1_kernel(
-    pos_ref, start_ref, row_ref, block_ref, s_ref, lse_ref, recv_ref, ds0_ref, p0_ref, p1_ref,
-    *refs,
+    pos_ref, start_ref, row_ref, block_ref, s_ref, lse_ref, recv_ref, add_ref, p_ref,
+    ds_ref, loss_ref, own_ref, other_ref, w_ref, lt_ref, acc_ref, past_ref,
 ):
-    ds_ref, loss_ref, own_ref, other_ref, w_ref, lt_ref, acc_ref = refs[-7:]
     step = pl.program_id(0)
+    steps = pl.num_programs(0) - 1
     rb = 256
     half = BLOCK // 2
+    part = add_ref[...] + jnp.dot(past_ref[...], p_ref[...], preferred_element_type=jnp.float32)
     ls = as_lanes(lse_ref[0, 0:1, :])
     lt_ref[...] = as_lanes(lse_ref[0, 1:2, :])
     for j in range(D // BLOCK):
         cols = slice(j * BLOCK, (j + 1) * BLOCK)
-        w_ref[:, cols] = jnp.exp(s_ref[:, 0, :, cols].reshape(rb, BLOCK) - ls)
+        w_ref[:, cols] = jnp.exp(s_ref[:, cols] - ls)
     acc_ref[...] = jnp.zeros_like(acc_ref)
+    part = part.reshape(rb // (2 * QUARTER), 2, QUARTER, D)
+    first = pos_ref[3] == 0
+    own_ref[...] = jnp.where(first, part[:, 0], part[:, 1])
+    other_ref[...] = jnp.where(first, part[:, 1], part[:, 0])
 
     def fetch(n, block):
         slot = row_ref[n]
-        k = slot % CAP
-        at = pl.multiple_of((slot // 2) * half, half)
-        x = recv_ref[pl.ds(at, half), :]
-        return pltpu.roll(x, ((block + k) % 2) * half, 1)
-
-    for sub in range(rb // half):
-        rows = slice(sub * half, (sub + 1) * half)
-        r = step * (rb // half) + sub
-        subtract_tiles(
-            fetch, half, start_ref[r], start_ref[r + 1], block_ref,
-            lambda cols: s_ref[2 * sub : 2 * sub + 2, 0, :, cols].reshape(half, BLOCK),
-            lt_ref, rows, w_ref, acc_ref,
-        )
-    ds = (w_ref[...] * GRAD_SCALE).astype(jnp.bfloat16)
-    ds_ref[...] = ds.reshape(ds_ref.shape)
-    loss_ref[0] = as_row(jnp.sum(acc_ref[...], axis=1, keepdims=True))
-    part = jnp.dot(ds, p1_ref[...], preferred_element_type=jnp.float32)
-    ds0 = ds0_ref[...].reshape(rb, D)
-    part = part + jnp.dot(ds0, p0_ref[...], preferred_element_type=jnp.float32)
-    part = part.reshape(rb // QUARTER, 2, QUARTER // 2, D)
-
-    @pl.when(pos_ref[3] == 0)
+        at = pl.multiple_of((slot // 2) * BLOCK, BLOCK)
+        return pltpu.roll(recv_ref[pl.ds(at, BLOCK), :], ((block + slot) % 2) * half, 1)
+
+    @pl.when(step < steps)
     def _():
-        own_ref[...] = part[:, 0]
-        other_ref[...] = part[:, 1]
-
-    @pl.when(pos_ref[3] != 0)
-    def _():
-        own_ref[...] = part[:, 1]
-        other_ref[...] = part[:, 0]
-
-
-def rows1_call(h, scalars, scores, lse, recv, ds0, p0, p1, ds=None):
+        for sub in range(rb // BLOCK):
+            rows = slice(sub * BLOCK, (sub + 1) * BLOCK)
+            r = step * (rb // BLOCK) + sub
+            subtract_tiles(
+                fetch, BLOCK, start_ref[r], start_ref[r + 1], block_ref,
+                lambda cols: s_ref[rows, cols], lt_ref, rows, w_ref, acc_ref,
+            )
+        ds = (w_ref[...] * GRAD_SCALE).astype(jnp.bfloat16)
+        ds_ref[...] = ds
+        past_ref[...] = ds
+        loss_ref[0] = as_row(jnp.sum(acc_ref[...], axis=1, keepdims=True))
+
+
+def rows1_call(scalars, scores, lse, recv, add, passages):
     rb = 256
-    view = (SHARDS, 2, QUARTER, D)
+    steps = ROWS // rb
     recv = recv.reshape(-1, BLOCK)
-    group = pl.BlockSpec((rb // QUARTER, 1, QUARTER, D), lambda i, *_: (i, h, 0, 0))
-    out = pl.BlockSpec((rb // QUARTER, QUARTER // 2, D), lambda i, *_: (i, 0, 0))
-    out_type = jax.ShapeDtypeStruct((SHARDS, QUARTER // 2, D), jnp.float32)
-    again = [] if ds is None else [ds]
+    now = lambda i, *_: (jnp.minimum(i, steps - 1), 0)
+    now3 = lambda i, *_: (jnp.minimum(i, steps - 1), 0, 0)
+    past = lambda i, *_: (jnp.maximum(i - 1, 0), 0)
+    past3 = lambda i, *_: (jnp.maximum(i - 1, 0), 0, 0)
+    out = pl.BlockSpec((rb // (2 * QUARTER), QUARTER, D), past3)
+    out_type = jax.ShapeDtypeStruct((SHARDS, QUARTER, D), jnp.float32)
     return pl.pallas_call(
         rows1_kernel,
         out_shape=(
-            jax.ShapeDtypeStruct(view, jnp.bfloat16),
-            jax.ShapeDtypeStruct((ROWS // 2 // rb, 1, rb), jnp.float32),
+            jax.ShapeDtypeStruct((ROWS, D), jnp.bfloat16),
+            jax.ShapeDtypeStruct((steps, 1, rb), jnp.float32),
             out_type,
             out_type,
         ),
         grid_spec=pltpu.PrefetchScalarGridSpec(
             num_scalar_prefetch=len(scalars),
-            grid=(ROWS // 2 // rb,),
+            grid=(steps + 1,),
             in_specs=[
-                group,
-                pl.BlockSpec((1, 2, rb), lambda i, *_: (i, 0, 0)),
+                pl.BlockSpec((rb, D), now),
+                pl.BlockSpec((1, 2, rb), now3),
                 full_spec(*recv.shape),
-                group,
+                pl.BlockSpec((rb, D), past),
                 full_spec(D, D),
-                full_spec(D, D),
-            ]
-            + [pl.BlockSpec(memory_space=pl.ANY)] * len(again),
-            out_specs=(group, pl.BlockSpec((1, 1, rb), lambda i, *_: (i, 0, 0)), out, out),
-            scratch_shapes=ROW_SCRATCH,
-        ),
-        input_output_aliases={len(scalars) + 6: 0} if again else {},
+            ],
+            out_specs=(pl.BlockSpec((rb, D), now), pl.BlockSpec((1, 1, rb), now3), out, out),
+            scratch_shapes=ROW_SCRATCH + [pltpu.VMEM((rb, D), jnp.bfloat16)],
+        ),
         name="rows1",
-    )(*scalars, scores.reshape(view), lse, recv, ds0.reshape(view), p0, p1, *again)
+    )(*scalars, scores, lse, recv, add, passages)
+
+
+def query_kernel(ds_ref, p_ref, out_ref):
+    out_ref[...] = jnp.dot(ds_ref[...], p_ref[...], preferred_element_type=jnp.float32)
+
+
+def query_call(ds, passages):
+    rb = 512
+    return pl.pallas_call(
+        query_kernel,
+        out_shape=jax.ShapeDtypeStruct((ROWS, D), jnp.float32),
+        grid=(ROWS // rb,),
+        in_specs=[pl.BlockSpec((rb, D), lambda i: (i, 0)), full_spec(D, D)],
+        out_specs=pl.BlockSpec((rb, D), lambda i: (i, 0)),
+        name="query",
+    )(ds, passages)
 
 
 def columns_kernel(pos_ref, ds_ref, q_ref, *outs):
@@ -451,26 +455,73 @@
     return [(i, (i + d) % n) for i in range(n)]
 
 
-def combine_kernel(own_ref, other_ref, *refs):
-    out_ref = refs[-1]
-    out_ref[:, :, :D] = own_ref[...] + other_ref[...]
-    if len(refs) == 2:
-        loss = refs[0][...]
-        out_ref[:, :, D:] = jnp.broadcast_to(loss[:, None, :], (*out_ref.shape[:2], BLOCK))
-
-
-def combine(own, other, *loss):
+def combine_kernel(own_ref, other_ref, loss_ref, out_ref):
+    for j in range(D // BLOCK):
+        cols = slice(j * BLOCK, (j + 1) * BLOCK)
+        rows = slice(j * QUARTER, (j + 1) * QUARTER)
+        out_ref[:, rows, :] = own_ref[:, :, cols] + other_ref[:, :, cols]
+    shape = (out_ref.shape[0], 8, BLOCK)
+    out_ref[:, SUM_ROWS:, :] = jnp.broadcast_to(loss_ref[...][:, None, :], shape)
+
+
+def combine(own, other, loss):
     step = 8
-    width = D + BLOCK * len(loss)
-    block = lambda w: pl.BlockSpec((step, QUARTER // 2, w), lambda i: (i, 0, 0))
+    block = pl.BlockSpec((step, QUARTER, D), lambda i: (i, 0, 0))
     return pl.pallas_call(
         combine_kernel,
-        out_shape=jax.ShapeDtypeStruct((SHARDS, QUARTER // 2, width), jnp.float32),
+        out_shape=jax.ShapeDtypeStruct((SHARDS, SUM_ROWS + 8, BLOCK), jnp.float32),
         grid=(SHARDS // step,),
-        in_specs=[block(D), block(D)] + [pl.BlockSpec((step, BLOCK), lambda i: (i, 0))] * len(loss),
-        out_specs=block(width),
+        in_specs=[block, block, pl.BlockSpec((step, BLOCK), lambda i: (i, 0))],
+        out_specs=pl.BlockSpec((step, SUM_ROWS + 8, BLOCK), lambda i: (i, 0, 0)),
         name="combine",
-    )(own, other, *loss)
+    )(own, other, loss)
+
+
+def total_kernel(got_ref, lse_ref, grad_ref, loss_ref):
+    step = pl.program_id(0)
+    loss = jnp.sum(got_ref[:, SUM_ROWS:, :], axis=0)
+
+    @pl.when(step == 0)
+    def _():
+        loss_ref[...] = lse_ref[...] + loss
+
+    @pl.when(step > 0)
+    def _():
+        loss_ref[...] = loss_ref[...] + loss
+
+    for core in range(2):
+        for j in range(D // BLOCK):
+            rows = slice(j * QUARTER, (j + 1) * QUARTER)
+            to = (slice(core * QUARTER, (core + 1) * QUARTER), slice(j * BLOCK, (j + 1) * BLOCK))
+            part = got_ref[core, rows, :]
+            for chip in range(1, got_ref.shape[0] // 2):
+                part = part + got_ref[2 * chip + core, rows, :]
+
+            @pl.when(step == 0)
+            def _(part=part, to=to):
+                grad_ref[to] = part
+
+            @pl.when(step > 0)
+            def _(part=part, to=to):
+                grad_ref[to] = grad_ref[to] + part
+
+
+def total(got, lse_rows):
+    step = 8
+    return pl.pallas_call(
+        total_kernel,
+        out_shape=(
+            jax.ShapeDtypeStruct((2 * QUARTER, D), jnp.float32),
+            jax.ShapeDtypeStruct((8, BLOCK), jnp.float32),
+        ),
+        grid=(SHARDS // step,),
+        in_specs=[
+            pl.BlockSpec((step, SUM_ROWS + 8, BLOCK), lambda i: (i, 0, 0)),
+            full_spec(8, BLOCK),
+        ],
+        out_specs=(full_spec(2 * QUARTER, D), full_spec(8, BLOCK)),
+        name="total",
+    )(got, lse_rows)
 
 
 def send(value, axis, d, n=4):
@@ -499,7 +550,6 @@
     recv1 = exchange(sent1)
     ids2, _ = together(flat_ids, lse)
     sent2 = pack(2, ids2, teacher)
-    sent3 = pack(3, ids2, teacher)
     sent2, _ = together(sent2, recv1[0, 0, 0])
     recv2 = exchange(sent2)
     meta = recv0[:, BLOCK, : 2 * CAP].astype(jnp.int32).reshape(-1)
@@ -507,36 +557,25 @@
     every = recv1[:, BLOCK:, :]
     top = jnp.max(every, axis=0)
     lse = (top + jnp.log(jnp.sum(jnp.exp(every - top[None]), axis=0))).reshape(8, 2, 256)
-    split = lse.transpose(1, 0, 2).reshape(2, SHARDS, 2, QUARTER)
-    lse_half = [split[:, :, h].reshape(2, 4, 256).transpose(1, 0, 2) for h in range(2)]
     ds0, loss0 = rows0_call(lists, s0, lse, [recv0, recv1])
     g0 = columns_call(pos, ds0, queries)
     z0 = [g0[0], g0[1:3], g0[3:5], g0[5:7]]
     np0, nm0 = send(z0[2][0], "pb", 1), send(z0[2][1], "pb", -1)
     fp0, fm0 = send(z0[1][1], "pb", 1), send(z0[3][0], "pb", -1)
-
-    sent3, _ = together(sent3, recv2[0, 0, 0])
-    recv3 = exchange(sent3)
-    scalars = (pos,) + lists
-    ds1, loss_a, own_a, other_a = rows1_call(0, scalars, s1, lse_half[0], recv2, ds0, p0, p1)
-    swap_a = send(other_a, "c", 1, 2)
+    q0 = query_call(ds0, p0)
     sp0 = send(z0[1][0] + np0, "pb", 1)
     sm0 = send(z0[3][1] + nm0, "pb", -1)
-    both_a = combine(own_a, swap_a)
-    both_a, _ = together(both_a, recv3[0, 0, 0])
-    got_a = exchange(both_a)
-    ds1, loss_b, own_b, other_b = rows1_call(1, scalars, s1, lse_half[1], recv3, ds0, p0, p1, ds1)
-    swap_b = send(other_b, "c", 1, 2)
-    g1 = columns_call(pos, ds1.reshape(ROWS, D), queries)
+
+    ds1, loss1, own, other = rows1_call((pos,) + lists, s1, lse, recv2, q0, p1)
+    swapped = send(other, "c", 1, 2)
+    loss_sum = (loss0 + loss1).reshape(SHARDS, 2 * QUARTER)
+    loss_sum = jnp.pad(loss_sum, ((0, 0), (0, BLOCK - 2 * QUARTER)))
+    both = combine(own, swapped, loss_sum)
+    got = exchange(both)
+    g1 = columns_call(pos, ds1, queries)
     z1 = [g1[0], g1[1:3], g1[3:5], g1[5:7]]
     np1, nm1 = send(z1[2][0], "pb", 1), send(z1[2][1], "pb", -1)
     fp1, fm1 = send(z1[1][1], "pb", 1), send(z1[3][0], "pb", -1)
-    loss_ab = jnp.stack([loss_a.reshape(SHARDS, QUARTER), loss_b.reshape(SHARDS, QUARTER)], axis=1)
-    loss_sum = loss0.reshape(SHARDS, 2 * QUARTER) + loss_ab.reshape(SHARDS, 2 * QUARTER)
-    loss_sum = jnp.pad(loss_sum, ((0, 0), (0, BLOCK - 2 * QUARTER)))
-    both_b = combine(own_b, swap_b, loss_sum)
-    both_b, _ = together(both_b, got_a[0, 0, 0])
-    got_b = exchange(both_b)
     sp1 = send(z1[1][0] + np1, "pb", 1)
     sm1 = send(z1[3][1] + nm1, "pb", -1)
 
@@ -551,15 +590,12 @@
     grad_passages = jnp.stack(
         [gp0.reshape(4, BLOCK // 2, D), gp1.reshape(4, BLOCK // 2, D)], axis=1
     ).reshape(4 * BLOCK, D)
-    chips = SHARDS // 2
-    sum_a = jnp.sum(got_a.reshape(chips, QUARTER, D), axis=0)
-    sum_b = jnp.sum(got_b[:, :, :D].reshape(chips, QUARTER, D), axis=0)
-    grad_queries = jnp.concatenate([sum_a, sum_b], axis=0)
     lse_rows = lax.dynamic_slice_in_dim(
         lse[:, 0, :].reshape(ROWS), me * (ROWS // SHARDS), ROWS // SHARDS
     )
-    loss = jnp.sum(got_b[:, 0, D : D + 2 * QUARTER], axis=0) + lse_rows
-    return loss, grad_queries, grad_passages
+    lse_rows = jnp.broadcast_to(jnp.pad(lse_rows, (0, BLOCK - 2 * QUARTER)), (8, BLOCK))
+    grad_queries, loss = total(got, lse_rows)
+    return loss[0, : 2 * QUARTER], grad_queries, grad_passages
 
 
 def solution(mesh):

time: 292 us -> 283 us (0.969)
  waiting for transfers between devices: 80.9 us -> 99.6 us
  starting transfers between devices: 59 us -> 44.1 us
  other arithmetic: 13.6 us -> 8.63 us
  local copies, waits for them, and re-layouts: 14.3 us -> 10.2 us
  Pallas kernels: 121 us -> 117 us
    all_to_all x6 -> x4, starting transfers between devices: 40.2 us -> 25.8 us  [exchange(): return lax.all_to_all(value, PLANE, split_axis=0, concat_axis=0, tiled=True)]
    ppermute x14 -> x13, waiting for transfers between devices: 37.3 us -> 50 us  [send(): return lax.ppermute(value, axis, ring(d, n))]
    all_to_all x6 -> x4, waiting for transfers between devices: 43.7 us -> 49.7 us  [exchange(): return lax.all_to_all(value, PLANE, split_axis=0, concat_axis=0, tiled=True)]
    unnamed x39 -> x23, local copies, waits for them, and re-layouts: 7.38 us -> 2.94 us
    pallas_call x4 -> x3, Pallas kernels: 22.3 us -> 17.9 us  [pack(): pl.pallas_call(functools.partial(pack_kernel, piece), out_shape=jax.Shape...]
    ppermute x14 -> x13, starting transfers between devices: 18.8 us -> 18.2 us  [send(): return lax.ppermute(value, axis, ring(d, n))]
  transfers between devices with their start and end apart: 20 -> 17, of which waited for: 12 -> 12; matrix products, arithmetic and copies ran while one was open for 6% -> 5% of each run, Pallas kernels for 40% -> 29%
where the time goes in v3:
time: 283 us; the launch traced here: 280 us
  Pallas kernels  117 us (41%)
  waiting for transfers between devices  99.6 us (35%)
  starting transfers between devices  44.1 us (16%)
  local copies, waits for them, and re-layouts  10.2 us (4%)
  other arithmetic  8.63 us (3%)
    ppermute x13, waiting for transfers between devices, send(): return lax.ppermute(value, axis, ring(d, n))  50 us
    all_to_all x4, waiting for transfers between devices, exchange(): return lax.all_to_all(value, PLANE, split_axis=0, concat_axis=0, tiled=True)  49.7 us
    all_to_all x4, starting transfers between devices, exchange(): return lax.all_to_all(value, PLANE, split_axis=0, concat_axis=0, tiled=True)  25.8 us
    pallas_call x1, Pallas kernels, rows1_call(): pl.pallas_call(rows1_kernel, out_shape=(jax.ShapeDtypeStruct((ROWS, D), j...  21.1 us
    pallas_call x2, Pallas kernels, columns_call(): pl.pallas_call(columns_kernel, out_shape=tuple((jax.ShapeDtypeStruct((n,...  19.5 us
    pallas_call x1, Pallas kernels, score(): pl.pallas_call(score_kernel, out_shape=(scores, scores, jax.ShapeDtypeStr...  18.7 us
    ppermute x13, starting transfers between devices, send(): return lax.ppermute(value, axis, ring(d, n))  18.2 us
    pallas_call x3, Pallas kernels, pack(): pl.pallas_call(functools.partial(pack_kernel, piece), out_shape=jax.Shape...  17.9 us
  transfers between devices with their start and end apart: 17, of which 12 were waited for; matrix products, arithmetic and copies ran while one was open for 5% of the time, Pallas kernels for 29%

profile of v3, /device:TPU:1, one launch (start us, length us, event | category | flops | bytes accessed | tf_op | source)
XLA Modules:
  0.0 280.5 jit_solution(14463240010972663938)
XLA Ops:
  2.0 6.0 %pack.3 = f32[32,136,128]{2,1,0:T(8,128)} custom-call(s32[64]{0:T(128)} %reshape.36.ids_ref, f32[2048,512]{1,0:T(8,128)} %teacher_ref.5), custom_call_target="tpu_custom_call" | custom-call | tf_op jit(solution)/shard_map/pack/pallas_call | solution.py:92
  8.0 8.6 %all-to-all-start = ((f32[32,136,128]{2,1,0:T(8,128)}), f32[32,136,128]{2,1,0:T(8,128)S(1)}, u32[]{:S(2)}, u32[]{:S(2)}) async-start(f32[32,136,128]{2,1,0:T(8,128)} %pack.3), calls=%async_computation | async-start | bytes 4456448 | tf_op jit(solution)/shard_map/all_to_all | solution.py:542
  16.5 18.7 %score.1 = (f32[2048,1024]{1,0:T(8,128)}, f32[2048,1024]{1,0:T(8,128)}, f32[8,2,256]{2,1,0:T(2,128)}, bf16[1024,1024]{1,0:T(8,128)(2,1)}, bf16[1024,1024]{1,0:T(8,128)(2,1)}) custom-call(bf16[2048,1024]{1,0:T(8,128)(2,1)} %q_ref.5, bf16[2048,1024]{1,0:T(8,128)(2,1)} %p_ref.1, f32[2048,512]{1,0:T(8,128)} %teacher_ref.5), custom_call_target="tpu_custom_call" | custom-call | tf_op jit(solution)/shard_map/score/pallas_call | solution.py:215
  36.6 5.9 %pack.4.sent_ref = f32[32,160,128]{2,1,0:T(8,128)} custom-call(s32[64]{0:T(128)} %reshape.36.ids_ref, f32[2048,512]{1,0:T(8,128)} %teacher_ref.5), custom_call_target="tpu_custom_call" | custom-call | tf_op jit(solution)/shard_map/pack/pallas_call | solution.py:92
  44.1 2.5 all-to-all-done
  47.9 5.4 %all-to-all-start.1 = ((f32[32,160,128]{2,1,0:T(8,128)}), f32[32,160,128]{2,1,0:T(8,128)S(1)}, u32[]{:S(2)}, u32[]{:S(2)}) async-start(f32[32,160,128]{2,1,0:T(8,128)} %fill_lse.1), calls=%async_computation.1 | async-start | bytes 5242880 | tf_op jit(solution)/shard_map/all_to_all | solution.py:542
  53.4 6.0 %pack.5 = f32[32,256,128]{2,1,0:T(8,128)} custom-call(s32[64]{0:T(128)} %reshape.36.ids_ref, f32[2048,512]{1,0:T(8,128)} %teacher_ref.5), custom_call_target="tpu_custom_call" | custom-call | tf_op jit(solution)/shard_map/pack/pallas_call | solution.py:92
  59.4 28.0 %all-to-all-done.1 = f32[32,160,128]{2,1,0:T(8,128)S(1)} async-done(((f32[32,160,128]{2,1,0:T(8,128)}), f32[32,160,128]{2,1,0:T(8,128)S(1)}, u32[]{:S(2)}, u32[]{:S(2)}) %all-to-all-start.1) | async-done | bytes 2621472 | tf_op jit(solution)/shard_map/all_to_all | solution.py:542
  87.4 7.0 %all-to-all-start.2 = ((f32[32,256,128]{2,1,0:T(8,128)}), f32[32,256,128]{2,1,0:T(8,128)}, u32[]{:S(2)}, u32[]{:S(2)}) async-start(f32[32,256,128]{2,1,0:T(8,128)} %pack.5), calls=%async_computation.2 | async-start | bytes 8388608 | tf_op jit(solution)/shard_map/all_to_all | solution.py:542
  96.7 4.2 %make_lists.1 = (s32[17]{0:T(128)}, s32[128]{0:T(128)}, s32[128]{0:T(128)}) custom-call(s32[256]{0:T(256)} %convert_element_type.12.meta_ref), custom_call_target="tpu_custom_call" | custom-call | tf_op jit(solution)/shard_map/make_lists/pallas_call | solution.py:172
  101.7 15.1 %rows0.1 = (bf16[2048,1024]{1,0:T(8,128)(2,1)}, f32[8,1,256]{2,1,0:T(1,128)}) custom-call(s32[17]{0:T(128)} %get-tuple-element.35.start_ref, s32[128]{0:T(128)} %get-tuple-element.36.row_ref, s32[128]{0:T(128)} %get-tuple-element.37.block_ref, f32[2048,1024]{1,0:T(8,128)} %get-tuple-element.42.s_ref, f32[8,2,256]{2,1,0:T(2,128)} %add.60.lse_ref, ...), custom_call_target="tpu_custom_call" | custom-call | tf_op jit(solution)/shard_map/rows0/pallas_call | solution.py:314
  116.8 9.1 %query.1.add_ref = f32[2048,1024]{1,0:T(8,128)} custom-call(bf16[2048,1024]{1,0:T(8,128)(2,1)} %get-tuple-element.43.ds_ref, bf16[1024,1024]{1,0:T(8,128)(2,1)} %get-tuple-element.44.p_ref), custom_call_target="tpu_custom_call" | custom-call | tf_op jit(solution)/shard_map/query/pallas_call | solution.py:413
  125.9 19.2 %all-to-all-done.2 = f32[32,256,128]{2,1,0:T(8,128)} async-done(((f32[32,256,128]{2,1,0:T(8,128)}), f32[32,256,128]{2,1,0:T(8,128)}, u32[]{:S(2)}, u32[]{:S(2)}) %all-to-all-start.2) | async-done | bytes 4194336 | tf_op jit(solution)/shard_map/all_to_all | solution.py:542
  145.1 21.1 %rows1.1 = (bf16[2048,1024]{1,0:T(8,128)(2,1)}, f32[8,1,256]{2,1,0:T(1,128)}, f32[32,32,1024]{2,1,0:T(8,128)}, f32[32,32,1024]{2,1,0:T(8,128)}) custom-call(s32[4]{0:T(128)} %pad_add_fusion.pos_ref, s32[17]{0:T(128)} %get-tuple-element.35.start_ref, s32[128]{0:T(128)} %get-tuple-element.36.row_ref, s32[128]{0:T(128)} %get-tuple-element.37.block_ref, ...), custom_call_target="tpu_custom_call" | custom-call | tf_op jit(solution)/shard_map/rows1/pallas_call | solution.py:382
  166.2 3.3 %collective-permute-start = (f32[32,32,1024]{2,1,0:T(8,128)}, f32[32,32,1024]{2,1,0:T(8,128)}, u32[]{:S(2)}, u32[]{:S(2)}) collective-permute-start(f32[32,32,1024]{2,1,0:T(8,128)} %get-tuple-element.47), channel_id=1, source_target_pairs={{0,1},{1,0},{2,3},{3,2},{4,5},{5,4},{6,7},{7,6},{8,9},{9,8},{10,11... | collective-permute-start | bytes 12582920 | tf_op jit(solution)/shard_map/ppermute | solution.py:528
  170.9 5.7 %collective-permute-done.other_ref = f32[32,32,1024]{2,1,0:T(8,128)} collective-permute-done((f32[32,32,1024]{2,1,0:T(8,128)}, f32[32,32,1024]{2,1,0:T(8,128)}, u32[]{:S(2)}, u32[]{:S(2)}) %collective-permute-start) | collective-permute-done | bytes 4194336 | tf_op jit(solution)/shard_map/ppermute | solution.py:528
  176.6 6.0 %combine.1 = f32[32,264,128]{2,1,0:T(8,128)} custom-call(f32[32,32,1024]{2,1,0:T(8,128)} %get-tuple-element.46.own_ref, f32[32,32,1024]{2,1,0:T(8,128)} %collective-permute-done.other_ref, f32[32,128]{1,0:T(8,128)} %pad.8.loss_ref), custom_call_target="tpu_custom_call" | custom-call | tf_op jit(solution)/shard_map/combine/pallas_call | solution.py:470
  182.6 4.8 %all-to-all-start.3 = ((f32[32,264,128]{2,1,0:T(8,128)}), f32[32,264,128]{2,1,0:T(8,128)}, u32[]{:S(2)}, u32[]{:S(2)}) async-start(f32[32,264,128]{2,1,0:T(8,128)} %combine.1), calls=%async_computation.3 | async-start | bytes 8650752 | tf_op jit(solution)/shard_map/all_to_all | solution.py:542
  187.4 9.7 %columns.2 = (f32[256,1024]{1,0:T(8,128)}, f32[128,1024]{1,0:T(8,128)}, f32[128,1024]{1,0:T(8,128)}, f32[128,1024]{1,0:T(8,128)}, f32[128,1024]{1,0:T(8,128)}, /*index=5*/f32[128,1024]{1,0:T(8,128)}, f32[128,1024]{1,0:T(8,128)}) custom-call(s32[4]{0:T(128)} %pad_add_fusion.pos_ref, bf16[2048,1024]{1,0:T(8,128)(2,1)} %get-tuple-element.43.ds_ref, ...), custom_call_target="tpu_custom_call" | custom-call | tf_op jit(solution)/shard_map/columns/pallas_call | solution.py:441
  197.1 2.8 %collective-permute-start.5 = (f32[128,1024]{1,0:T(8,128)}, f32[128,1024]{1,0:T(8,128)S(1)}, u32[]{:S(2)}, u32[]{:S(2)}) collective-permute-start(f32[128,1024]{1,0:T(8,128)} %get-tuple-element.58), channel_id=1, source_target_pairs={{0,96},{32,0},{64,32},{96,64},{1,97},{33,1},{65,33},{97,65},{2,98}... | collective-permute-start | bytes 1572872 | tf_op jit(solution)/shard_map/ppermute | solution.py:528
  199.9 9.8 %columns.3 = (f32[256,1024]{1,0:T(8,128)}, f32[128,1024]{1,0:T(8,128)}, f32[128,1024]{1,0:T(8,128)}, f32[128,1024]{1,0:T(8,128)}, f32[128,1024]{1,0:T(8,128)}, /*index=5*/f32[128,1024]{1,0:T(8,128)}, f32[128,1024]{1,0:T(8,128)}) custom-call(s32[4]{0:T(128)} %pad_add_fusion.pos_ref, bf16[2048,1024]{1,0:T(8,128)(2,1)} %get-tuple-element.59.ds_ref, ...), custom_call_target="tpu_custom_call" | custom-call | tf_op jit(solution)/shard_map/columns/pallas_call | solution.py:441
  209.8 2.7 collective-permute-start.11
  212.5 2.7 collective-permute-start.3
  215.3 2.7 collective-permute-start.6
  218.9 4.2 %collective-permute-done.11 = f32[128,1024]{1,0:T(8,128)S(1)} collective-permute-done((f32[128,1024]{1,0:T(8,128)}, f32[128,1024]{1,0:T(8,128)S(1)}, u32[]{:S(2)}, u32[]{:S(2)}) %collective-permute-start.11) | collective-permute-done | bytes 524320 | tf_op jit(solution)/shard_map/ppermute | solution.py:528
  226.3 8.0 %collective-permute-done.3 = f32[128,1024]{1,0:T(8,128)S(1)} collective-permute-done((f32[128,1024]{1,0:T(8,128)}, f32[128,1024]{1,0:T(8,128)S(1)}, u32[]{:S(2)}, u32[]{:S(2)}) %collective-permute-start.3) | collective-permute-done | bytes 524320 | tf_op jit(solution)/shard_map/ppermute | solution.py:528
  234.3 3.4 %collective-permute-start.9 = (f32[128,1024]{1,0:T(8,128)}, f32[128,1024]{1,0:T(8,128)}, u32[]{:S(2)}, u32[]{:S(2)}) collective-permute-start(f32[128,1024]{1,0:T(8,128)} %get-tuple-element.63), channel_id=1, source_target_pairs={{0,96},{32,0},{64,32},{96,64},{1,97},{33,1},{65,33},{97,65},{2,98}... | collective-permute-start | bytes 1572872 | tf_op jit(solution)/shard_map/ppermute | solution.py:528
  237.8 7.6 %collective-permute-done.6 = f32[128,1024]{1,0:T(8,128)S(1)} collective-permute-done((f32[128,1024]{1,0:T(8,128)S(1)}, f32[128,1024]{1,0:T(8,128)S(1)}, u32[]{:S(2)}, u32[]{:S(2)}) %collective-permute-start.6) | collective-permute-done | bytes 524320 | tf_op jit(solution)/shard_map/ppermute | solution.py:528
  250.6 9.3 %collective-permute-done.10 = f32[128,1024]{1,0:T(8,128)} collective-permute-done((f32[128,1024]{1,0:T(8,128)}, f32[128,1024]{1,0:T(8,128)}, u32[]{:S(2)}, u32[]{:S(2)}) %collective-permute-start.10) | collective-permute-done | bytes 524320 | tf_op jit(solution)/shard_map/ppermute | solution.py:528
  259.9 8.0 %collective-permute-done.12 = f32[128,1024]{1,0:T(8,128)} collective-permute-done((f32[128,1024]{1,0:T(8,128)S(1)}, f32[128,1024]{1,0:T(8,128)}, u32[]{:S(2)}, u32[]{:S(2)}) %collective-permute-start.12) | collective-permute-done | bytes 524320 | tf_op jit(solution)/shard_map/ppermute | solution.py:528
  267.9 3.2 %collective-permute-done.8 = f32[128,1024]{1,0:T(8,128)} collective-permute-done((f32[128,1024]{1,0:T(8,128)S(1)}, f32[128,1024]{1,0:T(8,128)}, u32[]{:S(2)}, u32[]{:S(2)}) %collective-permute-start.8) | collective-permute-done | bytes 524320 | tf_op jit(solution)/shard_map/ppermute | solution.py:528
  275.3 4.0 %total.1 = (f32[64,1024]{1,0:T(8,128)}, f32[8,128]{1,0:T(8,128)}) custom-call(f32[32,264,128]{2,1,0:T(8,128)} %all-to-all-done.3.got_ref, f32[8,128]{1,0:T(8,128)} %broadcast_in_dim.4.lse_ref), custom_call_target="tpu_custom_call" | custom-call | tf_op jit(solution)/shard_map/total/pallas_call | solution.py:511
  (66 shorter events, 24.8 us)
Async XLA Ops:
  8.0 38.7 %all-to-all-start = ((f32[32,136,128]{2,1,0:T(8,128)}), f32[32,136,128]{2,1,0:T(8,128)S(1)}, u32[]{:S(2)}, u32[]{:S(2)}) async-start(f32[32,136,128]{2,1,0:T(8,128)} %pack.3), calls=%async_computation | async-start | bytes 4456448 | tf_op jit(solution)/shard_map/all_to_all | solution.py:542
  46.6 1.3 copy-start.1
  47.9 39.4 %all-to-all-start.1 = ((f32[32,160,128]{2,1,0:T(8,128)}), f32[32,160,128]{2,1,0:T(8,128)S(1)}, u32[]{:S(2)}, u32[]{:S(2)}) async-start(f32[32,160,128]{2,1,0:T(8,128)} %fill_lse.1), calls=%async_computation.1 | async-start | bytes 5242880 | tf_op jit(solution)/shard_map/all_to_all | solution.py:542
  87.4 13.6 %copy-start = (f32[32,160,128]{2,1,0:T(8,128)}, f32[32,160,128]{2,1,0:T(8,128)S(1)}, u32[]{:S(2)}) copy-start(f32[32,160,128]{2,1,0:T(8,128)S(1)} %all-to-all-done.1) | copy-start | bytes 7864324
  87.4 57.7 %all-to-all-start.2 = ((f32[32,256,128]{2,1,0:T(8,128)}), f32[32,256,128]{2,1,0:T(8,128)}, u32[]{:S(2)}, u32[]{:S(2)}) async-start(f32[32,256,128]{2,1,0:T(8,128)} %pack.5), calls=%async_computation.2 | async-start | bytes 8388608 | tf_op jit(solution)/shard_map/all_to_all | solution.py:542
  145.1 24.4 %copy-start.10 = (f32[8,1,256]{2,1,0:T(1,128)S(1)}, f32[8,1,256]{2,1,0:T(1,128)}, u32[]{:S(2)}) copy-start(f32[8,1,256]{2,1,0:T(1,128)} %get-tuple-element.48) | copy-start | bytes 24580
  166.2 10.4 %collective-permute-start = (f32[32,32,1024]{2,1,0:T(8,128)}, f32[32,32,1024]{2,1,0:T(8,128)}, u32[]{:S(2)}, u32[]{:S(2)}) collective-permute-start(f32[32,32,1024]{2,1,0:T(8,128)} %get-tuple-element.47), channel_id=1, source_target_pairs={{0,1},{1,0},{2,3},{3,2},{4,5},{5,4},{6,7},{7,6},{8,9},{9,8},{10,11... | collective-permute-start | bytes 12582920 | tf_op jit(solution)/shard_map/ppermute | solution.py:528
  182.6 92.2 %all-to-all-start.3 = ((f32[32,264,128]{2,1,0:T(8,128)}), f32[32,264,128]{2,1,0:T(8,128)}, u32[]{:S(2)}, u32[]{:S(2)}) async-start(f32[32,264,128]{2,1,0:T(8,128)} %combine.1), calls=%async_computation.3 | async-start | bytes 8650752 | tf_op jit(solution)/shard_map/all_to_all | solution.py:542
  197.1 18.1 %collective-permute-start.5 = (f32[128,1024]{1,0:T(8,128)}, f32[128,1024]{1,0:T(8,128)S(1)}, u32[]{:S(2)}, u32[]{:S(2)}) collective-permute-start(f32[128,1024]{1,0:T(8,128)} %get-tuple-element.58), channel_id=1, source_target_pairs={{0,96},{32,0},{64,32},{96,64},{1,97},{33,1},{65,33},{97,65},{2,98}... | collective-permute-start | bytes 1572872 | tf_op jit(solution)/shard_map/ppermute | solution.py:528
  199.9 15.3 %collective-permute-start.1 = (f32[128,1024]{1,0:T(8,128)}, f32[128,1024]{1,0:T(8,128)S(1)}, u32[]{:S(2)}, u32[]{:S(2)}) collective-permute-start(f32[128,1024]{1,0:T(8,128)} %get-tuple-element.54), channel_id=1, source_target_pairs={{0,32},{32,64},{64,96},{96,0},{1,33},{33,65},{65,97},{97,1},{2,34}... | collective-permute-start | bytes 1572872 | tf_op jit(solution)/shard_map/ppermute | solution.py:528
  199.9 15.3 %copy-start.6 = (f32[128,1024]{1,0:T(8,128)S(1)}, f32[128,1024]{1,0:T(8,128)}, u32[]{:S(2)}) copy-start(f32[128,1024]{1,0:T(8,128)} %get-tuple-element.57) | copy-start | bytes 1572868
  199.9 18.1 %copy-start.5 = (f32[128,1024]{1,0:T(8,128)S(1)}, f32[128,1024]{1,0:T(8,128)}, u32[]{:S(2)}) copy-start(f32[128,1024]{1,0:T(8,128)} %get-tuple-element.53) | copy-start | bytes 1572868
  209.7 16.5 %copy-start.4 = (f32[128,1024]{1,0:T(8,128)S(1)}, f32[128,1024]{1,0:T(8,128)}, u32[]{:S(2)}) copy-start(f32[128,1024]{1,0:T(8,128)} %get-tuple-element.61) | copy-start | bytes 1572868
  209.7 36.8 %slice-start = ((f32[8,2,256]{2,1,0:T(2,128)}), f32[8,1,256]{2,1,0:T(1,128)S(1)}, s32[]{:S(2)}) async-start(f32[8,2,256]{2,1,0:T(2,128)} %add.60.lse_ref), calls=%async_computation.4 | async-start | bytes 16384 | tf_op jit(solution)/shard_map/slice | solution.py:594
  209.7 38.9 %copy-start.3 = (f32[256,1024]{1,0:T(8,128)S(1)}, f32[256,1024]{1,0:T(8,128)}, u32[]{:S(2)}) copy-start(f32[256,1024]{1,0:T(8,128)} %get-tuple-element.52) | copy-start | bytes 3145732
  209.8 13.3 %collective-permute-start.11 = (f32[128,1024]{1,0:T(8,128)}, f32[128,1024]{1,0:T(8,128)S(1)}, u32[]{:S(2)}, u32[]{:S(2)}) collective-permute-start(f32[128,1024]{1,0:T(8,128)} %get-tuple-element.66), channel_id=1, source_target_pairs={{0,96},{32,0},{64,32},{96,64},{1,97},{33,1},{65,33},{97,65},{2,98}... | collective-permute-start | bytes 1572872 | tf_op jit(solution)/shard_map/ppermute | solution.py:528
  212.5 13.7 %collective-permute-start.7 = (f32[128,1024]{1,0:T(8,128)}, f32[128,1024]{1,0:T(8,128)S(1)}, u32[]{:S(2)}, u32[]{:S(2)}) collective-permute-start(f32[128,1024]{1,0:T(8,128)} %get-tuple-element.62), channel_id=1, source_target_pairs={{0,32},{32,64},{64,96},{96,0},{1,33},{33,65},{65,97},{97,1},{2,34}... | collective-permute-start | bytes 1572872 | tf_op jit(solution)/shard_map/ppermute | solution.py:528
  212.5 21.8 %collective-permute-start.3 = (f32[128,1024]{1,0:T(8,128)}, f32[128,1024]{1,0:T(8,128)S(1)}, u32[]{:S(2)}, u32[]{:S(2)}) collective-permute-start(f32[128,1024]{1,0:T(8,128)} %get-tuple-element.55), channel_id=1, source_target_pairs={{0,96},{32,0},{64,32},{96,64},{1,97},{33,1},{65,33},{97,65},{2,98}... | collective-permute-start | bytes 1572872 | tf_op jit(solution)/shard_map/ppermute | solution.py:528
  215.2 22.5 %collective-permute-start.4 = (f32[128,1024]{1,0:T(8,128)}, f32[128,1024]{1,0:T(8,128)S(1)}, u32[]{:S(2)}, u32[]{:S(2)}) collective-permute-start(f32[128,1024]{1,0:T(8,128)} %get-tuple-element.56), channel_id=1, source_target_pairs={{0,32},{32,64},{64,96},{96,0},{1,33},{33,65},{65,97},{97,1},{2,34}... | collective-permute-start | bytes 1572872 | tf_op jit(solution)/shard_map/ppermute | solution.py:528
  215.3 30.2 %collective-permute-start.6 = (f32[128,1024]{1,0:T(8,128)S(1)}, f32[128,1024]{1,0:T(8,128)S(1)}, u32[]{:S(2)}, u32[]{:S(2)}) collective-permute-start(f32[128,1024]{1,0:T(8,128)S(1)} %add.69), channel_id=1, source_target_pairs={{0,96},{32,0},{64,32},{96,64},{1,97},{33,1},{65,33},{97,65},{2,98}... | collective-permute-start | bytes 1572872 | tf_op jit(solution)/shard_map/ppermute | solution.py:528
  223.1 25.6 %collective-permute-start.2 = (f32[128,1024]{1,0:T(8,128)}, f32[128,1024]{1,0:T(8,128)}, u32[]{:S(2)}, u32[]{:S(2)}) collective-permute-start(f32[128,1024]{1,0:T(8,128)} %add.65), channel_id=1, source_target_pairs={{0,32},{32,64},{64,96},{96,0},{1,33},{33,65},{65,97},{97,1},{2,34}... | collective-permute-start | bytes 1572872 | tf_op jit(solution)/shard_map/ppermute | solution.py:528
  224.4 46.8 %copy-start.2 = (f32[256,1024]{1,0:T(8,128)S(1)}, f32[256,1024]{1,0:T(8,128)}, u32[]{:S(2)}) copy-start(f32[256,1024]{1,0:T(8,128)} %get-tuple-element.60) | copy-start | bytes 3145732
  226.2 33.7 %collective-permute-start.10 = (f32[128,1024]{1,0:T(8,128)}, f32[128,1024]{1,0:T(8,128)}, u32[]{:S(2)}, u32[]{:S(2)}) collective-permute-start(f32[128,1024]{1,0:T(8,128)} %get-tuple-element.64), channel_id=1, source_target_pairs={{0,32},{32,64},{64,96},{96,0},{1,33},{33,65},{65,97},{97,1},{2,34}... | collective-permute-start | bytes 1572872 | tf_op jit(solution)/shard_map/ppermute | solution.py:528
  234.3 11.1 %copy-start.7 = (f32[128,1024]{1,0:T(8,128)}, f32[128,1024]{1,0:T(8,128)S(1)}, u32[]{:S(2)}) copy-start(f32[128,1024]{1,0:T(8,128)S(1)} %collective-permute-done.3) | copy-start | bytes 1572868
  234.3 25.6 %collective-permute-start.9 = (f32[128,1024]{1,0:T(8,128)}, f32[128,1024]{1,0:T(8,128)}, u32[]{:S(2)}, u32[]{:S(2)}) collective-permute-start(f32[128,1024]{1,0:T(8,128)} %get-tuple-element.63), channel_id=1, source_target_pairs={{0,96},{32,0},{64,32},{96,64},{1,97},{33,1},{65,33},{97,65},{2,98}... | collective-permute-start | bytes 1572872 | tf_op jit(solution)/shard_map/ppermute | solution.py:528
  237.7 7.7 %copy-start.8 = (f32[128,1024]{1,0:T(8,128)}, f32[128,1024]{1,0:T(8,128)S(1)}, u32[]{:S(2)}) copy-start(f32[128,1024]{1,0:T(8,128)S(1)} %collective-permute-done.4) | copy-start | bytes 1572868
  237.7 30.2 %collective-permute-start.12 = (f32[128,1024]{1,0:T(8,128)S(1)}, f32[128,1024]{1,0:T(8,128)}, u32[]{:S(2)}, u32[]{:S(2)}) collective-permute-start(f32[128,1024]{1,0:T(8,128)S(1)} %add.75), channel_id=1, source_target_pairs={{0,96},{32,0},{64,32},{96,64},{1,97},{33,1},{65,33},{97,65},{2,98}... | collective-permute-start | bytes 1572872 | tf_op jit(solution)/shard_map/ppermute | solution.py:528
  245.4 0.8 copy-start.9
  246.2 24.9 %collective-permute-start.8 = (f32[128,1024]{1,0:T(8,128)S(1)}, f32[128,1024]{1,0:T(8,128)}, u32[]{:S(2)}, u32[]{:S(2)}) collective-permute-start(f32[128,1024]{1,0:T(8,128)S(1)} %add.71), channel_id=1, source_target_pairs={{0,32},{32,64},{64,96},{96,0},{1,33},{33,65},{65,97},{97,1},{2,34}... | collective-permute-start | bytes 1572872 | tf_op jit(solution)/shard_map/ppermute | solution.py:528

commit v4 on v3

--- a/solution.py
+++ b/solution.py
@@ -47,7 +47,7 @@
             slot_ref[i] = -1
 
         def place(i, carry):
-            owner = ids_ref[i] // PBLOCKS_DEV
+            owner = ids_ref[i // SLOTS_DEV, i % SLOTS_DEV] // PBLOCKS_DEV
             rank = count_ref[owner]
             count_ref[owner] = rank + 1
             slot_ref[owner * CAP + jnp.minimum(rank, CAP - 1)] = i
@@ -69,7 +69,8 @@
             tiles.append(teacher_ref[pl.ds(row, BLOCK), pl.ds(col, BLOCK)])
             if piece == 0:
                 where = jnp.where(slot < 0, -1, entry // SLOTS_DEV).astype(jnp.float32)
-                block = (ids_ref[entry] % PBLOCKS_DEV).astype(jnp.float32)
+                block = ids_ref[entry // SLOTS_DEV, entry % SLOTS_DEV] % PBLOCKS_DEV
+                block = block.astype(jnp.float32)
                 meta = jnp.where(lane == k, where, meta)
                 meta = jnp.where(lane == CAP + k, block, meta)
         if piece < 2:
@@ -330,78 +331,85 @@
 
 
 def rows1_kernel(
-    pos_ref, start_ref, row_ref, block_ref, s_ref, lse_ref, recv_ref, add_ref, p_ref,
-    ds_ref, loss_ref, own_ref, other_ref, w_ref, lt_ref, acc_ref, past_ref,
+    side_ref, start_ref, row_ref, block_ref, s_ref, lse_ref, recv_ref, add_ref, p_ref, *refs
 ):
+    ds_ref, loss_ref, grad_ref, w_ref, lt_ref, acc_ref, past_ref = refs[-7:]
     step = pl.program_id(0)
     steps = pl.num_programs(0) - 1
     rb = 256
     half = BLOCK // 2
-    part = add_ref[...] + jnp.dot(past_ref[...], p_ref[...], preferred_element_type=jnp.float32)
-    ls = as_lanes(lse_ref[0, 0:1, :])
-    lt_ref[...] = as_lanes(lse_ref[0, 1:2, :])
+    part = add_ref[...].reshape(rb, D) + jnp.dot(
+        past_ref[...], p_ref[...], preferred_element_type=jnp.float32
+    )
+    ls = as_lanes(lse_ref[0, 0, 0:1, :])
+    lt_ref[...] = as_lanes(lse_ref[0, 0, 1:2, :])
     for j in range(D // BLOCK):
         cols = slice(j * BLOCK, (j + 1) * BLOCK)
-        w_ref[:, cols] = jnp.exp(s_ref[:, cols] - ls)
+        w_ref[:, cols] = jnp.exp(s_ref[:, 0, :, cols].reshape(rb, BLOCK) - ls)
     acc_ref[...] = jnp.zeros_like(acc_ref)
-    part = part.reshape(rb // (2 * QUARTER), 2, QUARTER, D)
-    first = pos_ref[3] == 0
-    own_ref[...] = jnp.where(first, part[:, 0], part[:, 1])
-    other_ref[...] = jnp.where(first, part[:, 1], part[:, 0])
+    grad_ref[...] = part.reshape(grad_ref.shape)
 
     def fetch(n, block):
         slot = row_ref[n]
-        at = pl.multiple_of((slot // 2) * BLOCK, BLOCK)
-        return pltpu.roll(recv_ref[pl.ds(at, BLOCK), :], ((block + slot) % 2) * half, 1)
+        x = recv_ref[pl.ds((slot // 2) * 2, 2), 0, :, :].reshape(half, BLOCK)
+        return pltpu.roll(x, ((block + slot) % 2) * half, 1)
 
     @pl.when(step < steps)
     def _():
-        for sub in range(rb // BLOCK):
-            rows = slice(sub * BLOCK, (sub + 1) * BLOCK)
-            r = step * (rb // BLOCK) + sub
+        for sub in range(rb // half):
+            rows = slice(sub * half, (sub + 1) * half)
+            r = step * (rb // half) + sub
             subtract_tiles(
-                fetch, BLOCK, start_ref[r], start_ref[r + 1], block_ref,
-                lambda cols: s_ref[rows, cols], lt_ref, rows, w_ref, acc_ref,
+                fetch, half, start_ref[r], start_ref[r + 1], block_ref,
+                lambda cols: s_ref[2 * sub : 2 * sub + 2, 0, :, cols].reshape(half, BLOCK),
+                lt_ref, rows, w_ref, acc_ref,
             )
         ds = (w_ref[...] * GRAD_SCALE).astype(jnp.bfloat16)
-        ds_ref[...] = ds
+        ds_ref[...] = ds.reshape(ds_ref.shape)
         past_ref[...] = ds
         loss_ref[0] = as_row(jnp.sum(acc_ref[...], axis=1, keepdims=True))
 
 
-def rows1_call(scalars, scores, lse, recv, add, passages):
+def rows1_call(side, lists, scores, lse, recv, add, passages, ds=None):
     rb = 256
-    steps = ROWS // rb
-    recv = recv.reshape(-1, BLOCK)
-    now = lambda i, *_: (jnp.minimum(i, steps - 1), 0)
-    now3 = lambda i, *_: (jnp.minimum(i, steps - 1), 0, 0)
-    past = lambda i, *_: (jnp.maximum(i - 1, 0), 0)
-    past3 = lambda i, *_: (jnp.maximum(i - 1, 0), 0, 0)
-    out = pl.BlockSpec((rb // (2 * QUARTER), QUARTER, D), past3)
-    out_type = jax.ShapeDtypeStruct((SHARDS, QUARTER, D), jnp.float32)
+    steps = ROWS // 2 // rb
+    view = (SHARDS, 2, QUARTER, D)
+    scalars = (side,) + lists
+    now = lambda i: jnp.minimum(i, steps - 1)
+    past = lambda i: jnp.maximum(i - 1, 0)
+    group = (rb // QUARTER, 1, QUARTER, D)
+    again = [] if ds is None else [ds]
     return pl.pallas_call(
         rows1_kernel,
         out_shape=(
-            jax.ShapeDtypeStruct((ROWS, D), jnp.bfloat16),
+            jax.ShapeDtypeStruct(view, jnp.bfloat16),
             jax.ShapeDtypeStruct((steps, 1, rb), jnp.float32),
-            out_type,
-            out_type,
+            jax.ShapeDtypeStruct((SHARDS, QUARTER, D), jnp.float32),
         ),
         grid_spec=pltpu.PrefetchScalarGridSpec(
             num_scalar_prefetch=len(scalars),
             grid=(steps + 1,),
             in_specs=[
-                pl.BlockSpec((rb, D), now),
-                pl.BlockSpec((1, 2, rb), now3),
-                full_spec(*recv.shape),
-                pl.BlockSpec((rb, D), past),
+                pl.BlockSpec(group, lambda i, h, *_: (now(i), h[0], 0, 0)),
+                pl.BlockSpec((1, 1, 2, rb), lambda i, h, *_: (h[0], now(i), 0, 0)),
+                pl.BlockSpec((4 * SHARDS, 1, QUARTER, BLOCK), lambda i, h, *_: (0, h[0], 0, 0)),
+                pl.BlockSpec(group, lambda i, h, *_: (past(i), h[0], 0, 0)),
                 full_spec(D, D),
-            ],
-            out_specs=(pl.BlockSpec((rb, D), now), pl.BlockSpec((1, 1, rb), now3), out, out),
+            ]
+            + [pl.BlockSpec(memory_space=pl.ANY)] * len(again),
+            out_specs=(
+                pl.BlockSpec(group, lambda i, h, *_: (now(i), h[0], 0, 0)),
+                pl.BlockSpec((1, 1, rb), lambda i, *_: (now(i), 0, 0)),
+                pl.BlockSpec((rb // QUARTER, QUARTER, D), lambda i, *_: (past(i), 0, 0)),
+            ),
             scratch_shapes=ROW_SCRATCH + [pltpu.VMEM((rb, D), jnp.bfloat16)],
         ),
+        input_output_aliases={len(scalars) + 5: 0} if again else {},
         name="rows1",
-    )(*scalars, scores, lse, recv, add, passages)
+    )(
+        *scalars, scores.reshape(view), lse, recv.reshape(4 * SHARDS, 2, QUARTER, BLOCK),
+        add.reshape(view), passages, *again,
+    )
 
 
 def query_kernel(ds_ref, p_ref, out_ref):
@@ -455,73 +463,92 @@
     return [(i, (i + d) % n) for i in range(n)]
 
 
-def combine_kernel(own_ref, other_ref, loss_ref, out_ref):
+def combine_kernel(pos_ref, own_ref, other_ref, loss0_ref, mine_ref, partner_ref, out_ref):
     for j in range(D // BLOCK):
         cols = slice(j * BLOCK, (j + 1) * BLOCK)
         rows = slice(j * QUARTER, (j + 1) * QUARTER)
         out_ref[:, rows, :] = own_ref[:, :, cols] + other_ref[:, :, cols]
-    shape = (out_ref.shape[0], 8, BLOCK)
-    out_ref[:, SUM_ROWS:, :] = jnp.broadcast_to(loss_ref[...][:, None, :], shape)
-
-
-def combine(own, other, loss):
-    step = 8
-    block = pl.BlockSpec((step, QUARTER, D), lambda i: (i, 0, 0))
+    first = pos_ref[3] == 0
+    for i in range(2):
+        cols = slice(i * BLOCK, (i + 1) * BLOCK)
+        mine, partner = mine_ref[0, :, cols], partner_ref[0, :, cols]
+        lines = {
+            i: jnp.where(first, mine, partner),
+            2 + i: jnp.where(first, partner, mine),
+            4 + i: loss0_ref[0, :, cols],
+            6 + i: loss0_ref[1, :, cols],
+        }
+        for at, line in lines.items():
+            shape = (out_ref.shape[0], 1, BLOCK)
+            out_ref[:, SUM_ROWS + at : SUM_ROWS + at + 1, :] = jnp.broadcast_to(line[None], shape)
+
+
+def combine(pos, own, other, loss0, mine, partner):
+    step = 4
+    block = pl.BlockSpec((step, QUARTER, D), lambda i, *_: (i, 0, 0))
+    group = lambda n: pl.BlockSpec((n, 1, 256), lambda i, *_: (i // (8 // step), 0, 0))
     return pl.pallas_call(
         combine_kernel,
         out_shape=jax.ShapeDtypeStruct((SHARDS, SUM_ROWS + 8, BLOCK), jnp.float32),
-        grid=(SHARDS // step,),
-        in_specs=[block, block, pl.BlockSpec((step, BLOCK), lambda i: (i, 0))],
-        out_specs=pl.BlockSpec((step, SUM_ROWS + 8, BLOCK), lambda i: (i, 0, 0)),
+        grid_spec=pltpu.PrefetchScalarGridSpec(
+            num_scalar_prefetch=1,
+            grid=(SHARDS // step,),
+            in_specs=[block, block, group(2), group(1), group(1)],
+            out_specs=pl.BlockSpec((step, SUM_ROWS + 8, BLOCK), lambda i, *_: (i, 0, 0)),
+        ),
         name="combine",
-    )(own, other, loss)
-
-
-def total_kernel(got_ref, lse_ref, grad_ref, loss_ref):
-    step = pl.program_id(0)
-    loss = jnp.sum(got_ref[:, SUM_ROWS:, :], axis=0)
-
-    @pl.when(step == 0)
+    )(pos, own, other, loss0, mine, partner)
+
+
+def total_kernel(me_ref, got_ref, lines_ref, lse_ref, grad_ref, loss_ref, sum_ref):
+    chips = SHARDS // 2
+    for core in range(2):
+        for j in range(got_ref.shape[1] // QUARTER):
+            rows = slice(j * QUARTER, (j + 1) * QUARTER)
+            part = got_ref[core, rows, :]
+            for chip in range(1, chips):
+                part = part + got_ref[2 * chip + core, rows, :]
+            to = slice(core * QUARTER, (core + 1) * QUARTER)
+            grad_ref[to, j * BLOCK : (j + 1) * BLOCK] = part
+
+    @pl.when(pl.program_id(0) == 0)
     def _():
-        loss_ref[...] = lse_ref[...] + loss
-
-    @pl.when(step > 0)
-    def _():
-        loss_ref[...] = loss_ref[...] + loss
-
-    for core in range(2):
-        for j in range(D // BLOCK):
-            rows = slice(j * QUARTER, (j + 1) * QUARTER)
-            to = (slice(core * QUARTER, (core + 1) * QUARTER), slice(j * BLOCK, (j + 1) * BLOCK))
-            part = got_ref[core, rows, :]
-            for chip in range(1, got_ref.shape[0] // 2):
-                part = part + got_ref[2 * chip + core, rows, :]
-
-            @pl.when(step == 0)
-            def _(part=part, to=to):
-                grad_ref[to] = part
-
-            @pl.when(step > 0)
-            def _(part=part, to=to):
-                grad_ref[to] = grad_ref[to] + part
-
-
-def total(got, lse_rows):
-    step = 8
+        sum_ref[...] = jnp.sum(lines_ref[...], axis=0)
+        mine = me_ref[0] % 8
+        lane = lax.broadcasted_iota(jnp.int32, (8, BLOCK), 1)
+        row = lambda at: jnp.broadcast_to(sum_ref[pl.ds(at, 1), :], (8, BLOCK))
+        shift = BLOCK - QUARTER * (mine % 4)
+        low = pltpu.roll(row(mine // 4), shift % BLOCK, 1)
+        high = pltpu.roll(row(2 + mine // 4), (shift + QUARTER) % BLOCK, 1)
+        early = pltpu.roll(row(4 + mine // 2), (mine % 2) * (BLOCK // 2), 1)
+        loss = jnp.where(lane < QUARTER, low, high) + early + lse_ref[...]
+        loss_ref[...] = loss[0:1, :]
+
+
+def total(me, got, lse_rows):
+    step = 2 * QUARTER
     return pl.pallas_call(
         total_kernel,
         out_shape=(
             jax.ShapeDtypeStruct((2 * QUARTER, D), jnp.float32),
-            jax.ShapeDtypeStruct((8, BLOCK), jnp.float32),
-        ),
-        grid=(SHARDS // step,),
-        in_specs=[
-            pl.BlockSpec((step, SUM_ROWS + 8, BLOCK), lambda i: (i, 0, 0)),
-            full_spec(8, BLOCK),
-        ],
-        out_specs=(full_spec(2 * QUARTER, D), full_spec(8, BLOCK)),
+            jax.ShapeDtypeStruct((1, BLOCK), jnp.float32),
+        ),
+        grid_spec=pltpu.PrefetchScalarGridSpec(
+            num_scalar_prefetch=1,
+            grid=(SUM_ROWS // step,),
+            in_specs=[
+                pl.BlockSpec((SHARDS, step, BLOCK), lambda i, *_: (0, i, 0)),
+                pl.BlockSpec((SHARDS, 8, BLOCK), lambda i, *_: (0, SUM_ROWS // 8, 0)),
+                full_spec(8, BLOCK),
+            ],
+            out_specs=(
+                pl.BlockSpec((2 * QUARTER, 2 * BLOCK), lambda i, *_: (0, i)),
+                full_spec(1, BLOCK),
+            ),
+            scratch_shapes=[pltpu.VMEM((8, BLOCK), jnp.float32)],
+        ),
         name="total",
-    )(got, lse_rows)
+    )(me, got, got, lse_rows)
 
 
 def send(value, axis, d, n=4):
@@ -536,19 +563,18 @@
     mz, my, mx, mc = (lax.axis_index(a) for a in ("pb", "y", "x", "c"))
     me = my * 8 + mx * 2 + mc
     pos = jnp.stack([mz, my, mx, mc]).astype(jnp.int32)
-    flat_ids = block_ids.reshape(-1)
 
     def exchange(value):
         return lax.all_to_all(value, PLANE, split_axis=0, concat_axis=0, tiled=True)
 
-    sent0 = pack(0, flat_ids, teacher)
+    sent0 = pack(0, block_ids, teacher)
     recv0 = exchange(sent0)
-    ids1, _ = together(flat_ids, sent0)
+    ids1, _ = together(block_ids, sent0)
     sent1 = pack(1, ids1, teacher)
     s0, s1, lse, p0, p1 = score(queries, passages, teacher)
     sent1 = fill_lse(sent1, lse.reshape(LSE_ROWS, BLOCK))
     recv1 = exchange(sent1)
-    ids2, _ = together(flat_ids, lse)
+    ids2, _ = together(block_ids, lse)
     sent2 = pack(2, ids2, teacher)
     sent2, _ = together(sent2, recv1[0, 0, 0])
     recv2 = exchange(sent2)
@@ -557,6 +583,8 @@
     every = recv1[:, BLOCK:, :]
     top = jnp.max(every, axis=0)
     lse = (top + jnp.log(jnp.sum(jnp.exp(every - top[None]), axis=0))).reshape(8, 2, 256)
+    split = lse.transpose(1, 0, 2).reshape(2, SHARDS, 2, QUARTER).transpose(2, 0, 1, 3)
+    lse_half = split.reshape(2, 2, 4, 256).transpose(0, 2, 1, 3)
     ds0, loss0 = rows0_call(lists, s0, lse, [recv0, recv1])
     g0 = columns_call(pos, ds0, queries)
     z0 = [g0[0], g0[1:3], g0[3:5], g0[5:7]]
@@ -566,13 +594,12 @@
     sp0 = send(z0[1][0] + np0, "pb", 1)
     sm0 = send(z0[3][1] + nm0, "pb", -1)
 
-    ds1, loss1, own, other = rows1_call((pos,) + lists, s1, lse, recv2, q0, p1)
+    ds1, loss_other, other = rows1_call(1 - pos[3:], lists, s1, lse_half, recv2, q0, p1)
     swapped = send(other, "c", 1, 2)
-    loss_sum = (loss0 + loss1).reshape(SHARDS, 2 * QUARTER)
-    loss_sum = jnp.pad(loss_sum, ((0, 0), (0, BLOCK - 2 * QUARTER)))
-    both = combine(own, swapped, loss_sum)
+    ds1, loss_own, own = rows1_call(pos[3:], lists, s1, lse_half, recv2, q0, p1, ds1)
+    both = combine(pos, own, swapped, loss0, loss_own, loss_other)
     got = exchange(both)
-    g1 = columns_call(pos, ds1, queries)
+    g1 = columns_call(pos, ds1.reshape(ROWS, D), queries)
     z1 = [g1[0], g1[1:3], g1[3:5], g1[5:7]]
     np1, nm1 = send(z1[2][0], "pb", 1), send(z1[2][1], "pb", -1)
     fp1, fm1 = send(z1[1][1], "pb", 1), send(z1[3][0], "pb", -1)
@@ -594,7 +621,7 @@
         lse[:, 0, :].reshape(ROWS), me * (ROWS // SHARDS), ROWS // SHARDS
     )
     lse_rows = jnp.broadcast_to(jnp.pad(lse_rows, (0, BLOCK - 2 * QUARTER)), (8, BLOCK))
-    grad_queries, loss = total(got, lse_rows)
+    grad_queries, loss = total(me.astype(jnp.int32).reshape(1), got, lse_rows)
     return loss[0, : 2 * QUARTER], grad_queries, grad_passages
 
 

time: 283 us -> 285 us (level)
  Pallas kernels: 117 us -> 127 us
  starting transfers between devices: 44.1 us -> 40.2 us
  waiting for transfers between devices: 99.6 us -> 96.1 us
    pallas_call x1 -> x2, Pallas kernels: 21.1 us -> 27.5 us  [rows1_call(): pl.pallas_call(rows1_kernel, out_shape=(jax.ShapeDtypeStruct(view, jnp.bf...]
    ppermute x13, starting transfers between devices: 18.2 us -> 14.2 us  [send(): return lax.ppermute(value, axis, ring(d, n))]
  transfers between devices with their start and end apart: 17 -> 17, of which waited for: 12 -> 10; matrix products, arithmetic and copies ran while one was open for 5% -> 5% of each run, Pallas kernels for 29% -> 33%
where the time goes in v4:
time: 285 us; the launch traced here: 283 us
  Pallas kernels  127 us (45%)
  waiting for transfers between devices  96.1 us (34%)
  starting transfers between devices  40.2 us (14%)
  local copies, waits for them, and re-layouts  11.1 us (4%)
  other arithmetic  7.94 us (3%)
    all_to_all x4, waiting for transfers between devices, exchange(): return lax.all_to_all(value, PLANE, split_axis=0, concat_axis=0, tiled=True)  48.4 us
    ppermute x13, waiting for transfers between devices, send(): return lax.ppermute(value, axis, ring(d, n))  47.7 us
    pallas_call x2, Pallas kernels, rows1_call(): pl.pallas_call(rows1_kernel, out_shape=(jax.ShapeDtypeStruct(view, jnp.bf...  27.5 us
    all_to_all x4, starting transfers between devices, exchange(): return lax.all_to_all(value, PLANE, split_axis=0, concat_axis=0, tiled=True)  26 us
    pallas_call x2, Pallas kernels, columns_call(): pl.pallas_call(columns_kernel, out_shape=tuple((jax.ShapeDtypeStruct((n,...  19.5 us
    pallas_call x1, Pallas kernels, score(): pl.pallas_call(score_kernel, out_shape=(scores, scores, jax.ShapeDtypeStr...  18.7 us
    pallas_call x3, Pallas kernels, pack(): pl.pallas_call(functools.partial(pack_kernel, piece), out_shape=jax.Shape...  18.4 us
    pallas_call x1, Pallas kernels, rows0_call(): pl.pallas_call(rows0_kernel, out_shape=(jax.ShapeDtypeStruct((ROWS, D), j...  15.1 us
  transfers between devices with their start and end apart: 17, of which 10 were waited for; matrix products, arithmetic and copies ran while one was open for 5% of the time, Pallas kernels for 33%

profile of v4, /device:TPU:1, one launch (start us, length us, event | category | flops | bytes accessed | tf_op | source)
XLA Modules:
  0.0 282.7 jit_solution(15348621172984408047)
XLA Ops:
  2.0 6.2 %pack.3 = f32[32,136,128]{2,1,0:T(8,128)} custom-call(s32[16,4]{1,0:T(8,128)} %copy.13.ids_ref, f32[2048,512]{1,0:T(8,128)} %teacher_ref.5), custom_call_target="tpu_custom_call" | custom-call | tf_op jit(solution)/shard_map/pack/pallas_call | solution.py:93
  8.2 8.6 %all-to-all-start = ((f32[32,136,128]{2,1,0:T(8,128)}), f32[32,136,128]{2,1,0:T(8,128)S(1)}, u32[]{:S(2)}, u32[]{:S(2)}) async-start(f32[32,136,128]{2,1,0:T(8,128)} %pack.3), calls=%async_computation | async-start | bytes 4456448 | tf_op jit(solution)/shard_map/all_to_all | solution.py:568
  17.5 6.1 %pack.4.sent_ref = f32[32,160,128]{2,1,0:T(8,128)} custom-call(s32[16,4]{1,0:T(8,128)} %copy.14.ids_ref, f32[2048,512]{1,0:T(8,128)} %teacher_ref.5), custom_call_target="tpu_custom_call" | custom-call | tf_op jit(solution)/shard_map/pack/pallas_call | solution.py:93
  23.6 18.7 %score.1 = (f32[2048,1024]{1,0:T(8,128)}, f32[2048,1024]{1,0:T(8,128)}, f32[8,2,256]{2,1,0:T(2,128)}, bf16[1024,1024]{1,0:T(8,128)(2,1)}, bf16[1024,1024]{1,0:T(8,128)(2,1)}) custom-call(bf16[2048,1024]{1,0:T(8,128)(2,1)} %q_ref.5, bf16[2048,1024]{1,0:T(8,128)(2,1)} %p_ref.1, f32[2048,512]{1,0:T(8,128)} %teacher_ref.5), custom_call_target="tpu_custom_call" | custom-call | tf_op jit(solution)/shard_map/score/pallas_call | solution.py:216
  43.6 1.6 fill_lse.1
  45.2 1.7 all-to-all-done
  48.2 5.7 %all-to-all-start.1 = ((f32[32,160,128]{2,1,0:T(8,128)}), f32[32,160,128]{2,1,0:T(8,128)S(1)}, u32[]{:S(2)}, u32[]{:S(2)}) async-start(f32[32,160,128]{2,1,0:T(8,128)} %fill_lse.1), calls=%async_computation.1 | async-start | bytes 5242880 | tf_op jit(solution)/shard_map/all_to_all | solution.py:568
  54.6 6.1 %pack.5 = f32[32,256,128]{2,1,0:T(8,128)} custom-call(s32[16,4]{1,0:T(8,128)} %copy.18.ids_ref, f32[2048,512]{1,0:T(8,128)} %teacher_ref.5), custom_call_target="tpu_custom_call" | custom-call | tf_op jit(solution)/shard_map/pack/pallas_call | solution.py:93
  60.8 27.2 %all-to-all-done.1 = f32[32,160,128]{2,1,0:T(8,128)S(1)} async-done(((f32[32,160,128]{2,1,0:T(8,128)}), f32[32,160,128]{2,1,0:T(8,128)S(1)}, u32[]{:S(2)}, u32[]{:S(2)}) %all-to-all-start.1) | async-done | bytes 2621472 | tf_op jit(solution)/shard_map/all_to_all | solution.py:568
  87.9 6.9 %all-to-all-start.2 = ((f32[32,256,128]{2,1,0:T(8,128)}), f32[32,256,128]{2,1,0:T(8,128)}, u32[]{:S(2)}, u32[]{:S(2)}) async-start(f32[32,256,128]{2,1,0:T(8,128)} %pack.5), calls=%async_computation.2 | async-start | bytes 8388608 | tf_op jit(solution)/shard_map/all_to_all | solution.py:568
  96.4 4.2 %make_lists.1 = (s32[17]{0:T(128)}, s32[128]{0:T(128)}, s32[128]{0:T(128)}) custom-call(s32[256]{0:T(256)} %convert_element_type.10.meta_ref), custom_call_target="tpu_custom_call" | custom-call | tf_op jit(solution)/shard_map/make_lists/pallas_call | solution.py:173
  101.7 15.1 %rows0.1 = (bf16[2048,1024]{1,0:T(8,128)(2,1)}, f32[8,1,256]{2,1,0:T(1,128)}) custom-call(s32[17]{0:T(128)} %get-tuple-element.37.start_ref, s32[128]{0:T(128)} %get-tuple-element.38.row_ref, s32[128]{0:T(128)} %get-tuple-element.39.block_ref, f32[2048,1024]{1,0:T(8,128)} %get-tuple-element.44.s_ref, f32[8,2,256]{2,1,0:T(2,128)} %copy-done.10, ...), custom_call_target="tpu_custom_call" | custom-call | tf_op jit(solution)/shard_map/rows0/pallas_call | solution.py:315
  116.8 9.1 %query.1 = f32[2048,1024]{1,0:T(8,128)} custom-call(bf16[2048,1024]{1,0:T(8,128)(2,1)} %get-tuple-element.45.ds_ref, bf16[1024,1024]{1,0:T(8,128)(2,1)} %get-tuple-element.46.p_ref), custom_call_target="tpu_custom_call" | custom-call | tf_op jit(solution)/shard_map/query/pallas_call | solution.py:421
  125.9 19.6 %all-to-all-done.2 = f32[32,256,128]{2,1,0:T(8,128)} async-done(((f32[32,256,128]{2,1,0:T(8,128)}), f32[32,256,128]{2,1,0:T(8,128)}, u32[]{:S(2)}, u32[]{:S(2)}) %all-to-all-start.2) | async-done | bytes 4194336 | tf_op jit(solution)/shard_map/all_to_all | solution.py:568
  145.5 13.7 %rows1.2 = (bf16[32,2,32,1024]{3,2,1,0:T(8,128)(2,1)}, f32[4,1,256]{2,1,0:T(1,128)}, f32[32,32,1024]{2,1,0:T(8,128)}) custom-call(s32[1]{0:T(128)S(6)} %sub.13.side_ref, s32[17]{0:T(128)} %get-tuple-element.37.start_ref, s32[128]{0:T(128)} %get-tuple-element.38.row_ref, s32[128]{0:T(128)} %get-tuple-element.39.block_ref, f32[32,2,32,1024]{3,2,1,0:T(8,128)} %bitcast.26, ...), custom_call_target="tpu_custom_call" | custom-call | tf_op jit(solution)/shard_map/rows1/pallas_call | solution.py:382
  159.3 3.7 %collective-permute-start = (f32[32,32,1024]{2,1,0:T(8,128)}, f32[32,32,1024]{2,1,0:T(8,128)}, u32[]{:S(2)}, u32[]{:S(2)}) collective-permute-start(f32[32,32,1024]{2,1,0:T(8,128)} %get-tuple-element.50), channel_id=1, source_target_pairs={{0,1},{1,0},{2,3},{3,2},{4,5},{5,4},{6,7},{7,6},{8,9},{9,8},{10,11... | collective-permute-start | bytes 12582920 | tf_op jit(solution)/shard_map/ppermute | solution.py:555
  163.6 13.8 %rows1.3 = (bf16[32,2,32,1024]{3,2,1,0:T(8,128)(2,1)}, f32[4,1,256]{2,1,0:T(1,128)}, f32[32,32,1024]{2,1,0:T(8,128)}) custom-call(s32[1]{0:T(128)} %bitcast.4.side_ref, s32[17]{0:T(128)} %get-tuple-element.37.start_ref, s32[128]{0:T(128)} %get-tuple-element.38.row_ref, s32[128]{0:T(128)} %get-tuple-element.39.block_ref, ...), custom_call_target="tpu_custom_call", output_to_operand_aliasing={{0}: (9, {})} | custom-call | tf_op jit(solution)/shard_map/rows1/pallas_call | solution.py:382
  177.4 8.4 %combine.1 = f32[32,264,128]{2,1,0:T(8,128)} custom-call(s32[4]{0:T(128)} %pad_add_fusion.pos_ref, f32[32,32,1024]{2,1,0:T(8,128)} %get-tuple-element.49.own_ref, f32[32,32,1024]{2,1,0:T(8,128)} %collective-permute-done.other_ref, f32[8,1,256]{2,1,0:T(1,128)} %get-tuple-element.51.loss0_ref, f32[4,1,256]{2,1,0:T(1,128)} %get-tuple-element.52.mine_ref, ...), custom_call_target="tpu_custom_call" | custom-call | tf_op jit(solution)/shard_map/combine/pallas_call | solution.py:490
  185.8 4.8 %all-to-all-start.3 = ((f32[32,264,128]{2,1,0:T(8,128)}), f32[32,264,128]{2,1,0:T(8,128)}, u32[]{:S(2)}, u32[]{:S(2)}) async-start(f32[32,264,128]{2,1,0:T(8,128)} %combine.1), calls=%async_computation.3 | async-start | bytes 8650752 | tf_op jit(solution)/shard_map/all_to_all | solution.py:568
  190.6 9.7 %columns.2 = (f32[256,1024]{1,0:T(8,128)}, f32[128,1024]{1,0:T(8,128)}, f32[128,1024]{1,0:T(8,128)}, f32[128,1024]{1,0:T(8,128)}, f32[128,1024]{1,0:T(8,128)}, /*index=5*/f32[128,1024]{1,0:T(8,128)}, f32[128,1024]{1,0:T(8,128)}) custom-call(s32[4]{0:T(128)} %pad_add_fusion.pos_ref, bf16[2048,1024]{1,0:T(8,128)(2,1)} %get-tuple-element.45.ds_ref, ...), custom_call_target="tpu_custom_call" | custom-call | tf_op jit(solution)/shard_map/columns/pallas_call | solution.py:449
  200.3 3.4 %collective-permute-start.1 = (f32[128,1024]{1,0:T(8,128)}, f32[128,1024]{1,0:T(8,128)S(1)}, u32[]{:S(2)}, u32[]{:S(2)}) collective-permute-start(f32[128,1024]{1,0:T(8,128)} %get-tuple-element.58), channel_id=1, source_target_pairs={{0,32},{32,64},{64,96},{96,0},{1,33},{33,65},{65,97},{97,1},{2,34}... | collective-permute-start | bytes 1572872 | tf_op jit(solution)/shard_map/ppermute | solution.py:555
  204.2 9.8 %columns.3 = (f32[256,1024]{1,0:T(8,128)}, f32[128,1024]{1,0:T(8,128)}, f32[128,1024]{1,0:T(8,128)}, f32[128,1024]{1,0:T(8,128)}, f32[128,1024]{1,0:T(8,128)}, /*index=5*/f32[128,1024]{1,0:T(8,128)}, f32[128,1024]{1,0:T(8,128)}) custom-call(s32[4]{0:T(128)} %pad_add_fusion.pos_ref, bf16[2048,1024]{1,0:T(8,128)(2,1)} %bitcast.28, bf16[2048,1024]{1,0:T(8,128)(2,1)} %q_ref.5), custom_call_target="tpu_custom_call" | custom-call | tf_op jit(solution)/shard_map/columns/pallas_call | solution.py:449
  215.1 1.8 collective-permute-start.11
  219.4 9.0 %collective-permute-done.7 = f32[128,1024]{1,0:T(8,128)S(1)} collective-permute-done((f32[128,1024]{1,0:T(8,128)}, f32[128,1024]{1,0:T(8,128)S(1)}, u32[]{:S(2)}, u32[]{:S(2)}) %collective-permute-start.7) | collective-permute-done | bytes 524320 | tf_op jit(solution)/shard_map/ppermute | solution.py:555
  230.8 8.1 %collective-permute-done.3 = f32[128,1024]{1,0:T(8,128)S(1)} collective-permute-done((f32[128,1024]{1,0:T(8,128)}, f32[128,1024]{1,0:T(8,128)S(1)}, u32[]{:S(2)}, u32[]{:S(2)}) %collective-permute-start.3) | collective-permute-done | bytes 524320 | tf_op jit(solution)/shard_map/ppermute | solution.py:555
  240.1 10.6 %collective-permute-done.2 = f32[128,1024]{1,0:T(8,128)S(1)} collective-permute-done((f32[128,1024]{1,0:T(8,128)S(1)}, f32[128,1024]{1,0:T(8,128)S(1)}, u32[]{:S(2)}, u32[]{:S(2)}) %collective-permute-start.2) | collective-permute-done | bytes 524320 | tf_op jit(solution)/shard_map/ppermute | solution.py:555
  251.7 1.8 add_add_fusion.3
  253.6 7.9 %collective-permute-done.9 = f32[128,1024]{1,0:T(8,128)} collective-permute-done((f32[128,1024]{1,0:T(8,128)}, f32[128,1024]{1,0:T(8,128)}, u32[]{:S(2)}, u32[]{:S(2)}) %collective-permute-start.9) | collective-permute-done | bytes 524320 | tf_op jit(solution)/shard_map/ppermute | solution.py:555
  262.1 11.2 %collective-permute-done.8 = f32[128,1024]{1,0:T(8,128)} collective-permute-done((f32[128,1024]{1,0:T(8,128)S(1)}, f32[128,1024]{1,0:T(8,128)}, u32[]{:S(2)}, u32[]{:S(2)}) %collective-permute-start.8) | collective-permute-done | bytes 524320 | tf_op jit(solution)/shard_map/ppermute | solution.py:555
  273.3 1.8 add_add_fusion.1
  275.5 1.5 copy.19
  277.5 4.0 %total.1 = (f32[64,1024]{1,0:T(8,128)}, f32[1,128]{1,0:T(1,128)}) custom-call(s32[1]{0:T(128)} %bitcast.me_ref, f32[32,264,128]{2,1,0:T(8,128)} %all-to-all-done.3.got_ref.lines_ref, f32[32,264,128]{2,1,0:T(8,128)} %all-to-all-done.3.got_ref.lines_ref, f32[8,128]{1,0:T(8,128)} %broadcast_in_dim.4.lse_ref), custom_call_target="tpu_custom_call" | custom-call | tf_op jit(solution)/shard_map/total/pallas_call | solution.py:530
  (73 shorter events, 20.2 us)
Async XLA Ops:
  2.0 14.8 %copy-start.12 = (s32[16,4]{0,1:T(4,128)S(1)}, s32[16,4]{0,1:T(4,128)}, u32[]{:S(2)}) copy-start(s32[16,4]{0,1:T(4,128)} %param.7) | copy-start | bytes 772
  8.2 38.7 %all-to-all-start = ((f32[32,136,128]{2,1,0:T(8,128)}), f32[32,136,128]{2,1,0:T(8,128)S(1)}, u32[]{:S(2)}, u32[]{:S(2)}) async-start(f32[32,136,128]{2,1,0:T(8,128)} %pack.3), calls=%async_computation | async-start | bytes 4456448 | tf_op jit(solution)/shard_map/all_to_all | solution.py:568
  46.9 1.3 copy-start.1
  48.2 39.7 %all-to-all-start.1 = ((f32[32,160,128]{2,1,0:T(8,128)}), f32[32,160,128]{2,1,0:T(8,128)S(1)}, u32[]{:S(2)}, u32[]{:S(2)}) async-start(f32[32,160,128]{2,1,0:T(8,128)} %fill_lse.1), calls=%async_computation.1 | async-start | bytes 5242880 | tf_op jit(solution)/shard_map/all_to_all | solution.py:568
  87.9 12.8 %copy-start = (f32[32,160,128]{2,1,0:T(8,128)}, f32[32,160,128]{2,1,0:T(8,128)S(1)}, u32[]{:S(2)}) copy-start(f32[32,160,128]{2,1,0:T(8,128)S(1)} %all-to-all-done.1) | copy-start | bytes 7864324
  87.9 57.6 %all-to-all-start.2 = ((f32[32,256,128]{2,1,0:T(8,128)}), f32[32,256,128]{2,1,0:T(8,128)}, u32[]{:S(2)}, u32[]{:S(2)}) async-start(f32[32,256,128]{2,1,0:T(8,128)} %pack.5), calls=%async_computation.2 | async-start | bytes 8388608 | tf_op jit(solution)/shard_map/all_to_all | solution.py:568
  100.9 0.9 copy-start.10
  159.3 18.1 %collective-permute-start = (f32[32,32,1024]{2,1,0:T(8,128)}, f32[32,32,1024]{2,1,0:T(8,128)}, u32[]{:S(2)}, u32[]{:S(2)}) collective-permute-start(f32[32,32,1024]{2,1,0:T(8,128)} %get-tuple-element.50), channel_id=1, source_target_pairs={{0,1},{1,0},{2,3},{3,2},{4,5},{5,4},{6,7},{7,6},{8,9},{9,8},{10,11... | collective-permute-start | bytes 12582920 | tf_op jit(solution)/shard_map/ppermute | solution.py:555
  185.8 91.2 %all-to-all-start.3 = ((f32[32,264,128]{2,1,0:T(8,128)}), f32[32,264,128]{2,1,0:T(8,128)}, u32[]{:S(2)}, u32[]{:S(2)}) async-start(f32[32,264,128]{2,1,0:T(8,128)} %combine.1), calls=%async_computation.3 | async-start | bytes 8650752 | tf_op jit(solution)/shard_map/all_to_all | solution.py:568
  200.3 16.7 %collective-permute-start.1 = (f32[128,1024]{1,0:T(8,128)}, f32[128,1024]{1,0:T(8,128)S(1)}, u32[]{:S(2)}, u32[]{:S(2)}) collective-permute-start(f32[128,1024]{1,0:T(8,128)} %get-tuple-element.58), channel_id=1, source_target_pairs={{0,32},{32,64},{64,96},{96,0},{1,33},{33,65},{65,97},{97,1},{2,34}... | collective-permute-start | bytes 1572872 | tf_op jit(solution)/shard_map/ppermute | solution.py:555
  203.7 14.7 %collective-permute-start.5 = (f32[128,1024]{1,0:T(8,128)}, f32[128,1024]{1,0:T(8,128)S(1)}, u32[]{:S(2)}, u32[]{:S(2)}) collective-permute-start(f32[128,1024]{1,0:T(8,128)} %get-tuple-element.62), channel_id=1, source_target_pairs={{0,96},{32,0},{64,32},{96,64},{1,97},{33,1},{65,33},{97,65},{2,98}... | collective-permute-start | bytes 1572872 | tf_op jit(solution)/shard_map/ppermute | solution.py:555
  204.2 14.0 %copy-start.6 = (f32[128,1024]{1,0:T(8,128)S(1)}, f32[128,1024]{1,0:T(8,128)}, u32[]{:S(2)}) copy-start(f32[128,1024]{1,0:T(8,128)} %get-tuple-element.57) | copy-start | bytes 1572868
  204.2 14.2 %copy-start.5 = (f32[128,1024]{1,0:T(8,128)S(1)}, f32[128,1024]{1,0:T(8,128)}, u32[]{:S(2)}) copy-start(f32[128,1024]{1,0:T(8,128)} %get-tuple-element.61) | copy-start | bytes 1572868
  214.0 16.7 %copy-start.4 = (f32[128,1024]{1,0:T(8,128)S(1)}, f32[128,1024]{1,0:T(8,128)}, u32[]{:S(2)}) copy-start(f32[128,1024]{1,0:T(8,128)} %get-tuple-element.69) | copy-start | bytes 1572868
  214.0 37.5 %copy-start.11 = (f32[8,2,256]{2,1,0:T(2,128)S(1)}, f32[8,2,256]{2,1,0:T(2,128)}, u32[]{:S(2)}) copy-start(f32[8,2,256]{2,1,0:T(2,128)} %copy-done.10) | copy-start | bytes 49156
  214.1 37.6 %copy-start.3 = (f32[256,1024]{1,0:T(8,128)S(1)}, f32[256,1024]{1,0:T(8,128)}, u32[]{:S(2)}) copy-start(f32[256,1024]{1,0:T(8,128)} %get-tuple-element.56) | copy-start | bytes 3145732
  214.1 14.3 %collective-permute-start.7 = (f32[128,1024]{1,0:T(8,128)}, f32[128,1024]{1,0:T(8,128)S(1)}, u32[]{:S(2)}, u32[]{:S(2)}) collective-permute-start(f32[128,1024]{1,0:T(8,128)} %get-tuple-element.66), channel_id=1, source_target_pairs={{0,32},{32,64},{64,96},{96,0},{1,33},{33,65},{65,97},{97,1},{2,34}... | collective-permute-start | bytes 1572872 | tf_op jit(solution)/shard_map/ppermute | solution.py:555
  215.1 14.5 %collective-permute-start.11 = (f32[128,1024]{1,0:T(8,128)}, f32[128,1024]{1,0:T(8,128)S(1)}, u32[]{:S(2)}, u32[]{:S(2)}) collective-permute-start(f32[128,1024]{1,0:T(8,128)} %get-tuple-element.70), channel_id=1, source_target_pairs={{0,96},{32,0},{64,32},{96,64},{1,97},{33,1},{65,33},{97,65},{2,98}... | collective-permute-start | bytes 1572872 | tf_op jit(solution)/shard_map/ppermute | solution.py:555
  216.8 22.1 %collective-permute-start.3 = (f32[128,1024]{1,0:T(8,128)}, f32[128,1024]{1,0:T(8,128)S(1)}, u32[]{:S(2)}, u32[]{:S(2)}) collective-permute-start(f32[128,1024]{1,0:T(8,128)} %get-tuple-element.59), channel_id=1, source_target_pairs={{0,96},{32,0},{64,32},{96,64},{1,97},{33,1},{65,33},{97,65},{2,98}... | collective-permute-start | bytes 1572872 | tf_op jit(solution)/shard_map/ppermute | solution.py:555
  217.0 22.5 %collective-permute-start.4 = (f32[128,1024]{1,0:T(8,128)}, f32[128,1024]{1,0:T(8,128)S(1)}, u32[]{:S(2)}, u32[]{:S(2)}) collective-permute-start(f32[128,1024]{1,0:T(8,128)} %get-tuple-element.60), channel_id=1, source_target_pairs={{0,32},{32,64},{64,96},{96,0},{1,33},{33,65},{65,97},{97,1},{2,34}... | collective-permute-start | bytes 1572872 | tf_op jit(solution)/shard_map/ppermute | solution.py:555
  218.4 32.4 %collective-permute-start.2 = (f32[128,1024]{1,0:T(8,128)S(1)}, f32[128,1024]{1,0:T(8,128)S(1)}, u32[]{:S(2)}, u32[]{:S(2)}) collective-permute-start(f32[128,1024]{1,0:T(8,128)S(1)} %add.59), channel_id=1, source_target_pairs={{0,32},{32,64},{64,96},{96,0},{1,33},{33,65},{65,97},{97,1},{2,34}... | collective-permute-start | bytes 1572872 | tf_op jit(solution)/shard_map/ppermute | solution.py:555
  228.4 23.3 %collective-permute-start.6 = (f32[128,1024]{1,0:T(8,128)}, f32[128,1024]{1,0:T(8,128)}, u32[]{:S(2)}, u32[]{:S(2)}) collective-permute-start(f32[128,1024]{1,0:T(8,128)} %add.63), channel_id=1, source_target_pairs={{0,96},{32,0},{64,32},{96,64},{1,97},{33,1},{65,33},{97,65},{2,98}... | collective-permute-start | bytes 1572872 | tf_op jit(solution)/shard_map/ppermute | solution.py:555
  229.5 43.8 %copy-start.2 = (f32[256,1024]{1,0:T(8,128)S(1)}, f32[256,1024]{1,0:T(8,128)}, u32[]{:S(2)}) copy-start(f32[256,1024]{1,0:T(8,128)} %get-tuple-element.64) | copy-start | bytes 3145732
  229.5 31.9 %collective-permute-start.9 = (f32[128,1024]{1,0:T(8,128)}, f32[128,1024]{1,0:T(8,128)}, u32[]{:S(2)}, u32[]{:S(2)}) collective-permute-start(f32[128,1024]{1,0:T(8,128)} %get-tuple-element.67), channel_id=1, source_target_pairs={{0,96},{32,0},{64,32},{96,64},{1,97},{33,1},{65,33},{97,65},{2,98}... | collective-permute-start | bytes 1572872 | tf_op jit(solution)/shard_map/ppermute | solution.py:555
  238.9 11.9 %copy-start.7 = (f32[128,1024]{1,0:T(8,128)}, f32[128,1024]{1,0:T(8,128)S(1)}, u32[]{:S(2)}) copy-start(f32[128,1024]{1,0:T(8,128)S(1)} %collective-permute-done.3) | copy-start | bytes 1572868
  238.9 23.2 %collective-permute-start.10 = (f32[128,1024]{1,0:T(8,128)}, f32[128,1024]{1,0:T(8,128)}, u32[]{:S(2)}, u32[]{:S(2)}) collective-permute-start(f32[128,1024]{1,0:T(8,128)} %get-tuple-element.68), channel_id=1, source_target_pairs={{0,32},{32,64},{64,96},{96,0},{1,33},{33,65},{65,97},{97,1},{2,34}... | collective-permute-start | bytes 1572872 | tf_op jit(solution)/shard_map/ppermute | solution.py:555
  239.5 11.2 %copy-start.8 = (f32[128,1024]{1,0:T(8,128)}, f32[128,1024]{1,0:T(8,128)S(1)}, u32[]{:S(2)}) copy-start(f32[128,1024]{1,0:T(8,128)S(1)} %collective-permute-done.4) | copy-start | bytes 1572868
  239.5 33.8 %collective-permute-start.8 = (f32[128,1024]{1,0:T(8,128)S(1)}, f32[128,1024]{1,0:T(8,128)}, u32[]{:S(2)}, u32[]{:S(2)}) collective-permute-start(f32[128,1024]{1,0:T(8,128)S(1)} %add.65), channel_id=1, source_target_pairs={{0,32},{32,64},{64,96},{96,0},{1,33},{33,65},{65,97},{97,1},{2,34}... | collective-permute-start | bytes 1572872 | tf_op jit(solution)/shard_map/ppermute | solution.py:555
  250.7 0.8 copy-start.9
  251.6 21.8 %collective-permute-start.12 = (f32[128,1024]{1,0:T(8,128)S(1)}, f32[128,1024]{1,0:T(8,128)}, u32[]{:S(2)}, u32[]{:S(2)}) collective-permute-start(f32[128,1024]{1,0:T(8,128)S(1)} %add.69), channel_id=1, source_target_pairs={{0,96},{32,0},{64,32},{96,64},{1,97},{33,1},{65,33},{97,65},{2,98}... | collective-permute-start | bytes 1572872 | tf_op jit(solution)/shard_map/ppermute | solution.py:555

commit v5 on v3

--- a/solution.py
+++ b/solution.py
@@ -36,11 +36,13 @@
     return jnp.broadcast_to(row, (BLOCK, n)).T
 
 
-def pack_kernel(piece, ids_ref, teacher_ref, out_ref, slot_ref, count_ref):
+def pack_kernel(piece, ids_ref, whole_ref, out_ref, slot_ref, count_ref, teacher_ref, sem):
     step = pl.program_id(0)
 
     @pl.when(step == 0)
     def _():
+        copy = pltpu.make_async_copy(whole_ref, teacher_ref, sem)
+        copy.start()
         for i in range(SHARDS):
             count_ref[i] = 0
         for i in range(SHARDS * CAP):
@@ -54,6 +56,7 @@
             return carry
 
         lax.fori_loop(0, ENTRIES, place, 0, unroll=8)
+        copy.wait()
 
     quarter = lax.broadcasted_iota(jnp.int32, (BLOCK, BLOCK), 1) // QUARTER
     lane = lax.broadcasted_iota(jnp.int32, (8, BLOCK), 1)
@@ -95,11 +98,13 @@
         grid_spec=pltpu.PrefetchScalarGridSpec(
             num_scalar_prefetch=1,
             grid=(SHARDS // PACK_STEP,),
-            in_specs=[pl.BlockSpec((ROWS, SLOTS_DEV * BLOCK), lambda s, ids: (0, 0))],
+            in_specs=[pl.BlockSpec(memory_space=pl.ANY)],
             out_specs=pl.BlockSpec((PACK_STEP, rows, BLOCK), lambda s, ids: (s, 0, 0)),
             scratch_shapes=[
                 pltpu.SMEM((SHARDS * CAP,), jnp.int32),
                 pltpu.SMEM((SHARDS,), jnp.int32),
+                pltpu.VMEM((ROWS, SLOTS_DEV * BLOCK), jnp.float32),
+                pltpu.SemaphoreType.DMA,
             ],
         ),
         name="pack",
@@ -330,8 +335,8 @@
 
 
 def rows1_kernel(
-    pos_ref, start_ref, row_ref, block_ref, s_ref, lse_ref, recv_ref, add_ref, p_ref,
-    ds_ref, loss_ref, own_ref, other_ref, w_ref, lt_ref, acc_ref, past_ref,
+    pos_ref, start_ref, row_ref, block_ref, s_ref, lse_ref, recv_ref, add_ref, p_ref, loss0_ref,
+    ds_ref, own_ref, other_ref, w_ref, lt_ref, acc_ref, past_ref, line_ref,
 ):
     step = pl.program_id(0)
     steps = pl.num_programs(0) - 1
@@ -346,8 +351,15 @@
     acc_ref[...] = jnp.zeros_like(acc_ref)
     part = part.reshape(rb // (2 * QUARTER), 2, QUARTER, D)
     first = pos_ref[3] == 0
-    own_ref[...] = jnp.where(first, part[:, 0], part[:, 1])
-    other_ref[...] = jnp.where(first, part[:, 1], part[:, 0])
+    for j in range(D // BLOCK):
+        cols = slice(j * BLOCK, (j + 1) * BLOCK)
+        rows = slice(j * QUARTER, (j + 1) * QUARTER)
+        even, odd = part[:, 0, :, cols], part[:, 1, :, cols]
+        own_ref[:, rows, :] = jnp.where(first, even, odd)
+        other_ref[:, rows, :] = jnp.where(first, odd, even)
+    lines = (own_ref.shape[0], 8, BLOCK)
+    own_ref[:, SUM_ROWS:, :] = jnp.broadcast_to(line_ref[...][None], lines)
+    other_ref[:, SUM_ROWS:, :] = jnp.zeros(lines, jnp.float32)
 
     def fetch(n, block):
         slot = row_ref[n]
@@ -366,10 +378,13 @@
         ds = (w_ref[...] * GRAD_SCALE).astype(jnp.bfloat16)
         ds_ref[...] = ds
         past_ref[...] = ds
-        loss_ref[0] = as_row(jnp.sum(acc_ref[...], axis=1, keepdims=True))
-
-
-def rows1_call(scalars, scores, lse, recv, add, passages):
+        loss = as_row(jnp.sum(acc_ref[...], axis=1, keepdims=True)) + loss0_ref[0]
+        low = jnp.broadcast_to(loss[:, :BLOCK], (8, BLOCK))
+        high = jnp.broadcast_to(loss[:, BLOCK:], (8, BLOCK))
+        line_ref[...] = jnp.where(lax.broadcasted_iota(jnp.int32, (8, BLOCK), 0) == 0, low, high)
+
+
+def rows1_call(scalars, scores, lse, recv, add, passages, loss0):
     rb = 256
     steps = ROWS // rb
     recv = recv.reshape(-1, BLOCK)
@@ -377,13 +392,12 @@
     now3 = lambda i, *_: (jnp.minimum(i, steps - 1), 0, 0)
     past = lambda i, *_: (jnp.maximum(i - 1, 0), 0)
     past3 = lambda i, *_: (jnp.maximum(i - 1, 0), 0, 0)
-    out = pl.BlockSpec((rb // (2 * QUARTER), QUARTER, D), past3)
-    out_type = jax.ShapeDtypeStruct((SHARDS, QUARTER, D), jnp.float32)
+    out = pl.BlockSpec((rb // (2 * QUARTER), SUM_ROWS + 8, BLOCK), past3)
+    out_type = jax.ShapeDtypeStruct((SHARDS, SUM_ROWS + 8, BLOCK), jnp.float32)
     return pl.pallas_call(
         rows1_kernel,
         out_shape=(
             jax.ShapeDtypeStruct((ROWS, D), jnp.bfloat16),
-            jax.ShapeDtypeStruct((steps, 1, rb), jnp.float32),
             out_type,
             out_type,
         ),
@@ -396,12 +410,14 @@
                 full_spec(*recv.shape),
                 pl.BlockSpec((rb, D), past),
                 full_spec(D, D),
+                pl.BlockSpec((1, 1, rb), now3),
             ],
-            out_specs=(pl.BlockSpec((rb, D), now), pl.BlockSpec((1, 1, rb), now3), out, out),
-            scratch_shapes=ROW_SCRATCH + [pltpu.VMEM((rb, D), jnp.bfloat16)],
+            out_specs=(pl.BlockSpec((rb, D), now), out, out),
+            scratch_shapes=ROW_SCRATCH
+            + [pltpu.VMEM((rb, D), jnp.bfloat16), pltpu.VMEM((8, BLOCK), jnp.float32)],
         ),
         name="rows1",
-    )(*scalars, scores, lse, recv, add, passages)
+    )(*scalars, scores, lse, recv, add, passages, loss0)
 
 
 def query_kernel(ds_ref, p_ref, out_ref):
@@ -420,108 +436,93 @@
     )(ds, passages)
 
 
-def columns_kernel(pos_ref, ds_ref, q_ref, *outs):
-    groups = {0: outs[:1], 1: outs[1:3], 2: outs[3:5], 3: outs[5:7]}
-    for d in (2, 1, 3, 0):
-        off = pl.multiple_of(((pos_ref[0] + d) % 4) * (D // 4), D // 4)
-        part = lax.dot_general(
-            ds_ref[:, pl.ds(off, D // 4)],
-            q_ref[...],
-            (((0,), (0,)), ((), ())),
-            preferred_element_type=jnp.float32,
-        )
-        size = D // 4 // len(groups[d])
-        for i, out in enumerate(groups[d]):
-            out[...] = part[size * i : size * (i + 1)]
-
-
-def columns_call(pos, ds, queries):
-    full = lambda *shape: pl.BlockSpec(shape, lambda i, *_: (0,) * len(shape))
-    sizes = (D // 4,) + (D // 8,) * 6
-    return pl.pallas_call(
-        columns_kernel,
+def columns_kernel(groups, pos_ref, ds_ref, q_ref, *outs):
+    step = pl.program_id(0)
+    part = lax.dot_general(
+        ds_ref[...], q_ref[...], (((0,), (0,)), ((), ())), preferred_element_type=jnp.float32
+    )
+    at = 0
+    for i, d in enumerate(groups):
+        count = 1 if d == 0 else 2
+        mine = outs[at : at + count]
+        at += count
+
+        @pl.when(step == i)
+        def _(mine=mine):
+            size = D // 4 // len(mine)
+            for n, out in enumerate(mine):
+                out[...] = part[size * n : size * (n + 1)]
+
+
+def columns_call(pos, ds, queries, groups):
+    def column(i, pos_ref):
+        d = functools.reduce(lambda v, n: jnp.where(i == n, groups[n], v), range(len(groups)), 0)
+        return 0, (pos_ref[0] + d) % 4
+
+    sizes = sum(([D // 4] if d == 0 else [D // 8] * 2 for d in groups), [])
+    outs = pl.pallas_call(
+        functools.partial(columns_kernel, groups),
         out_shape=tuple(jax.ShapeDtypeStruct((n, D), jnp.float32) for n in sizes),
         grid_spec=pltpu.PrefetchScalarGridSpec(
             num_scalar_prefetch=1,
-            grid=(1,),
-            in_specs=[full(ROWS, D), full(ROWS, D)],
-            out_specs=tuple(full(n, D) for n in sizes),
+            grid=(len(groups),),
+            in_specs=[pl.BlockSpec((ROWS, D // 4), column), full_spec(ROWS, D)],
+            out_specs=tuple(full_spec(n, D) for n in sizes),
         ),
         name="columns",
     )(pos, ds, queries)
-
-
-def ring(d, n=4):
-    return [(i, (i + d) % n) for i in range(n)]
-
-
-def combine_kernel(own_ref, other_ref, loss_ref, out_ref):
-    for j in range(D // BLOCK):
-        cols = slice(j * BLOCK, (j + 1) * BLOCK)
-        rows = slice(j * QUARTER, (j + 1) * QUARTER)
-        out_ref[:, rows, :] = own_ref[:, :, cols] + other_ref[:, :, cols]
-    shape = (out_ref.shape[0], 8, BLOCK)
-    out_ref[:, SUM_ROWS:, :] = jnp.broadcast_to(loss_ref[...][:, None, :], shape)
-
-
-def combine(own, other, loss):
-    step = 8
-    block = pl.BlockSpec((step, QUARTER, D), lambda i: (i, 0, 0))
-    return pl.pallas_call(
-        combine_kernel,
-        out_shape=jax.ShapeDtypeStruct((SHARDS, SUM_ROWS + 8, BLOCK), jnp.float32),
-        grid=(SHARDS // step,),
-        in_specs=[block, block, pl.BlockSpec((step, BLOCK), lambda i: (i, 0))],
-        out_specs=pl.BlockSpec((step, SUM_ROWS + 8, BLOCK), lambda i: (i, 0, 0)),
-        name="combine",
-    )(own, other, loss)
-
-
-def total_kernel(got_ref, lse_ref, grad_ref, loss_ref):
-    step = pl.program_id(0)
-    loss = jnp.sum(got_ref[:, SUM_ROWS:, :], axis=0)
-
-    @pl.when(step == 0)
+    outs = list(outs)
+    return {d: [outs.pop(0) for _ in range(1 if d == 0 else 2)] for d in groups}
+
+
+def total_kernel(me_ref, got_ref, lines_ref, lse_ref, grad_ref, loss_ref, sum_ref):
+    chips = SHARDS // 2
+    for core in range(2):
+        for j in range(got_ref.shape[1] // QUARTER):
+            rows = slice(j * QUARTER, (j + 1) * QUARTER)
+            part = got_ref[core, rows, :]
+            for chip in range(1, chips):
+                part = part + got_ref[2 * chip + core, rows, :]
+            to = slice(core * QUARTER, (core + 1) * QUARTER)
+            grad_ref[to, j * BLOCK : (j + 1) * BLOCK] = part
+
+    @pl.when(pl.program_id(0) == 0)
     def _():
-        loss_ref[...] = lse_ref[...] + loss
-
-    @pl.when(step > 0)
-    def _():
-        loss_ref[...] = loss_ref[...] + loss
-
-    for core in range(2):
-        for j in range(D // BLOCK):
-            rows = slice(j * QUARTER, (j + 1) * QUARTER)
-            to = (slice(core * QUARTER, (core + 1) * QUARTER), slice(j * BLOCK, (j + 1) * BLOCK))
-            part = got_ref[core, rows, :]
-            for chip in range(1, got_ref.shape[0] // 2):
-                part = part + got_ref[2 * chip + core, rows, :]
-
-            @pl.when(step == 0)
-            def _(part=part, to=to):
-                grad_ref[to] = part
-
-            @pl.when(step > 0)
-            def _(part=part, to=to):
-                grad_ref[to] = grad_ref[to] + part
-
-
-def total(got, lse_rows):
-    step = 8
+        sum_ref[...] = jnp.sum(lines_ref[...], axis=0)
+        mine = me_ref[0] % 4
+        line = jnp.broadcast_to(sum_ref[pl.ds(mine // 2, 1), :], (8, BLOCK))
+        line = pltpu.roll(line, (mine % 2) * (BLOCK // 2), 1) + lse_ref[...]
+        loss_ref[...] = line[0:1, : 2 * QUARTER]
+
+
+def total(me, got, lse_rows):
+    step = 4 * QUARTER
     return pl.pallas_call(
         total_kernel,
         out_shape=(
             jax.ShapeDtypeStruct((2 * QUARTER, D), jnp.float32),
-            jax.ShapeDtypeStruct((8, BLOCK), jnp.float32),
-        ),
-        grid=(SHARDS // step,),
-        in_specs=[
-            pl.BlockSpec((step, SUM_ROWS + 8, BLOCK), lambda i: (i, 0, 0)),
-            full_spec(8, BLOCK),
-        ],
-        out_specs=(full_spec(2 * QUARTER, D), full_spec(8, BLOCK)),
+            jax.ShapeDtypeStruct((1, 2 * QUARTER), jnp.float32),
+        ),
+        grid_spec=pltpu.PrefetchScalarGridSpec(
+            num_scalar_prefetch=1,
+            grid=(SUM_ROWS // step,),
+            in_specs=[
+                pl.BlockSpec((SHARDS, step, BLOCK), lambda i, *_: (0, i, 0)),
+                pl.BlockSpec((SHARDS, 8, BLOCK), lambda i, *_: (0, SUM_ROWS // 8, 0)),
+                full_spec(8, BLOCK),
+            ],
+            out_specs=(
+                pl.BlockSpec((2 * QUARTER, step // QUARTER * BLOCK), lambda i, *_: (0, i)),
+                full_spec(1, 2 * QUARTER),
+            ),
+            scratch_shapes=[pltpu.VMEM((8, BLOCK), jnp.float32)],
+        ),
         name="total",
-    )(got, lse_rows)
+    )(me, got, got, lse_rows)
+
+
+def ring(d, n=4):
+    return [(i, (i + d) % n) for i in range(n)]
 
 
 def send(value, axis, d, n=4):
@@ -558,22 +559,19 @@
     top = jnp.max(every, axis=0)
     lse = (top + jnp.log(jnp.sum(jnp.exp(every - top[None]), axis=0))).reshape(8, 2, 256)
     ds0, loss0 = rows0_call(lists, s0, lse, [recv0, recv1])
-    g0 = columns_call(pos, ds0, queries)
-    z0 = [g0[0], g0[1:3], g0[3:5], g0[5:7]]
+    z0 = columns_call(pos, ds0, queries, (2, 1, 3, 0))
     np0, nm0 = send(z0[2][0], "pb", 1), send(z0[2][1], "pb", -1)
     fp0, fm0 = send(z0[1][1], "pb", 1), send(z0[3][0], "pb", -1)
     q0 = query_call(ds0, p0)
     sp0 = send(z0[1][0] + np0, "pb", 1)
     sm0 = send(z0[3][1] + nm0, "pb", -1)
 
-    ds1, loss1, own, other = rows1_call((pos,) + lists, s1, lse, recv2, q0, p1)
+    ds1, own, other = rows1_call((pos,) + lists, s1, lse, recv2, q0, p1, loss0)
     swapped = send(other, "c", 1, 2)
-    loss_sum = (loss0 + loss1).reshape(SHARDS, 2 * QUARTER)
-    loss_sum = jnp.pad(loss_sum, ((0, 0), (0, BLOCK - 2 * QUARTER)))
-    both = combine(own, swapped, loss_sum)
+    z1 = columns_call(pos, ds1, queries, (2, 1))
+    both = own + swapped
     got = exchange(both)
-    g1 = columns_call(pos, ds1, queries)
-    z1 = [g1[0], g1[1:3], g1[3:5], g1[5:7]]
+    z1.update(columns_call(pos, ds1, queries, (3, 0)))
     np1, nm1 = send(z1[2][0], "pb", 1), send(z1[2][1], "pb", -1)
     fp1, fm1 = send(z1[1][1], "pb", 1), send(z1[3][0], "pb", -1)
     sp1 = send(z1[1][0] + np1, "pb", 1)
@@ -581,10 +579,10 @@
 
     h = D // 8
     parts = [
-        z0[0][:h] + sp0 + fm0,
-        z0[0][h:] + fp0 + sm0,
-        z1[0][:h] + sp1 + fm1,
-        z1[0][h:] + fp1 + sm1,
+        z0[0][0][:h] + sp0 + fm0,
+        z0[0][0][h:] + fp0 + sm0,
+        z1[0][0][:h] + sp1 + fm1,
+        z1[0][0][h:] + fp1 + sm1,
     ]
     gp0, gp1 = jnp.concatenate(parts[:2]), jnp.concatenate(parts[2:])
     grad_passages = jnp.stack(
@@ -594,8 +592,8 @@
         lse[:, 0, :].reshape(ROWS), me * (ROWS // SHARDS), ROWS // SHARDS
     )
     lse_rows = jnp.broadcast_to(jnp.pad(lse_rows, (0, BLOCK - 2 * QUARTER)), (8, BLOCK))
-    grad_queries, loss = total(got, lse_rows)
-    return loss[0, : 2 * QUARTER], grad_queries, grad_passages
+    grad_queries, loss = total(me.astype(jnp.int32).reshape(1), got, lse_rows)
+    return loss.reshape(2 * QUARTER), grad_queries, grad_passages
 
 
 def solution(mesh):

time: 283 us -> 278 us (0.982)
  waiting for transfers between devices: 99.6 us -> 92.8 us
  other arithmetic: 8.63 us -> 14.8 us
    ppermute x13, waiting for transfers between devices: 50 us -> 43 us  [send(): return lax.ppermute(value, axis, ring(d, n))]
    add x3, other arithmetic: 4.3 us -> 8.47 us  [the longest x1 4.89 us: per_device(): both = own + swapped]
  transfers between devices with their start and end apart: 17 -> 17, of which waited for: 12 -> 10; matrix products, arithmetic and copies ran while one was open for 5% -> 5% of each run, Pallas kernels for 29% -> 31%
where the time goes in v5:
time: 278 us; the launch traced here: 276 us
  Pallas kernels  116 us (42%)
  waiting for transfers between devices  92.8 us (33%)
  starting transfers between devices  44 us (16%)
  other arithmetic  14.8 us (5%)
  local copies, waits for them, and re-layouts  7.55 us (3%)
    all_to_all x4, waiting for transfers between devices, exchange(): return lax.all_to_all(value, PLANE, split_axis=0, concat_axis=0, tiled=True)  49.8 us
    ppermute x13, waiting for transfers between devices, send(): return lax.ppermute(value, axis, ring(d, n))  43 us
    all_to_all x4, starting transfers between devices, exchange(): return lax.all_to_all(value, PLANE, split_axis=0, concat_axis=0, tiled=True)  25.8 us
    pallas_call x3, Pallas kernels, columns_call(): pl.pallas_call(functools.partial(columns_kernel, groups), out_shape=tuple...  25.3 us
    pallas_call x1, Pallas kernels, rows1_call(): pl.pallas_call(rows1_kernel, out_shape=(jax.ShapeDtypeStruct((ROWS, D), j...  21.1 us
    pallas_call x1, Pallas kernels, score(): pl.pallas_call(score_kernel, out_shape=(scores, scores, jax.ShapeDtypeStr...  18.7 us
    ppermute x13, starting transfers between devices, send(): return lax.ppermute(value, axis, ring(d, n))  18.1 us
    pallas_call x3, Pallas kernels, pack(): pl.pallas_call(functools.partial(pack_kernel, piece), out_shape=jax.Shape...  17.8 us
  transfers between devices with their start and end apart: 17, of which 10 were waited for; matrix products, arithmetic and copies ran while one was open for 5% of the time, Pallas kernels for 31%

profile of v5, /device:TPU:1, one launch (start us, length us, event | category | flops | bytes accessed | tf_op | source)
XLA Modules:
  0.0 275.9 jit_solution(11185014290139098366)
XLA Ops:
  2.0 6.0 %pack.3 = f32[32,136,128]{2,1,0:T(8,128)} custom-call(s32[64]{0:T(128)} %reshape.40.ids_ref, f32[2048,512]{1,0:T(8,128)} %whole_ref.5), custom_call_target="tpu_custom_call" | custom-call | tf_op jit(solution)/shard_map/pack/pallas_call | solution.py:95
  8.0 8.6 %all-to-all-start = ((f32[32,136,128]{2,1,0:T(8,128)}), f32[32,136,128]{2,1,0:T(8,128)S(1)}, u32[]{:S(2)}, u32[]{:S(2)}) async-start(f32[32,136,128]{2,1,0:T(8,128)} %pack.3), calls=%async_computation | async-start | bytes 4456448 | tf_op jit(solution)/shard_map/all_to_all | solution.py:543
  16.6 18.7 %score.1 = (f32[2048,1024]{1,0:T(8,128)}, f32[2048,1024]{1,0:T(8,128)}, f32[8,2,256]{2,1,0:T(2,128)}, bf16[1024,1024]{1,0:T(8,128)(2,1)}, bf16[1024,1024]{1,0:T(8,128)(2,1)}) custom-call(bf16[2048,1024]{1,0:T(8,128)(2,1)} %q_ref.7, bf16[2048,1024]{1,0:T(8,128)(2,1)} %p_ref.1, f32[2048,512]{1,0:T(8,128)} %whole_ref.5), custom_call_target="tpu_custom_call" | custom-call | tf_op jit(solution)/shard_map/score/pallas_call | solution.py:220
  36.6 6.0 %pack.4.sent_ref = f32[32,160,128]{2,1,0:T(8,128)} custom-call(s32[64]{0:T(128)} %reshape.40.ids_ref, f32[2048,512]{1,0:T(8,128)} %whole_ref.5), custom_call_target="tpu_custom_call" | custom-call | tf_op jit(solution)/shard_map/pack/pallas_call | solution.py:95
  44.2 2.5 all-to-all-done
  48.1 5.4 %all-to-all-start.1 = ((f32[32,160,128]{2,1,0:T(8,128)}), f32[32,160,128]{2,1,0:T(8,128)S(1)}, u32[]{:S(2)}, u32[]{:S(2)}) async-start(f32[32,160,128]{2,1,0:T(8,128)} %fill_lse.1), calls=%async_computation.1 | async-start | bytes 5242880 | tf_op jit(solution)/shard_map/all_to_all | solution.py:543
  53.5 5.9 %pack.5 = f32[32,256,128]{2,1,0:T(8,128)} custom-call(s32[64]{0:T(128)} %reshape.40.ids_ref, f32[2048,512]{1,0:T(8,128)} %whole_ref.5), custom_call_target="tpu_custom_call" | custom-call | tf_op jit(solution)/shard_map/pack/pallas_call | solution.py:95
  59.4 28.1 %all-to-all-done.1 = f32[32,160,128]{2,1,0:T(8,128)S(1)} async-done(((f32[32,160,128]{2,1,0:T(8,128)}), f32[32,160,128]{2,1,0:T(8,128)S(1)}, u32[]{:S(2)}, u32[]{:S(2)}) %all-to-all-start.1) | async-done | bytes 2621472 | tf_op jit(solution)/shard_map/all_to_all | solution.py:543
  87.5 7.0 %all-to-all-start.2 = ((f32[32,256,128]{2,1,0:T(8,128)}), f32[32,256,128]{2,1,0:T(8,128)}, u32[]{:S(2)}, u32[]{:S(2)}) async-start(f32[32,256,128]{2,1,0:T(8,128)} %pack.5), calls=%async_computation.2 | async-start | bytes 8388608 | tf_op jit(solution)/shard_map/all_to_all | solution.py:543
  96.7 4.2 %make_lists.1 = (s32[17]{0:T(128)}, s32[128]{0:T(128)}, s32[128]{0:T(128)}) custom-call(s32[256]{0:T(256)} %convert_element_type.10.meta_ref), custom_call_target="tpu_custom_call" | custom-call | tf_op jit(solution)/shard_map/make_lists/pallas_call | solution.py:177
  101.7 15.1 %rows0.1 = (bf16[2048,1024]{1,0:T(8,128)(2,1)}, f32[8,1,256]{2,1,0:T(1,128)}) custom-call(s32[17]{0:T(128)} %get-tuple-element.34.start_ref, s32[128]{0:T(128)} %get-tuple-element.35.row_ref, s32[128]{0:T(128)} %get-tuple-element.36.block_ref, f32[2048,1024]{1,0:T(8,128)} %get-tuple-element.41.s_ref, f32[8,2,256]{2,1,0:T(2,128)} %add.60.lse_ref, ...), custom_call_target="tpu_custom_call" | custom-call | tf_op jit(solution)/shard_map/rows0/pallas_call | solution.py:319
  116.9 9.1 %query.1.add_ref = f32[2048,1024]{1,0:T(8,128)} custom-call(bf16[2048,1024]{1,0:T(8,128)(2,1)} %get-tuple-element.42.ds_ref, bf16[1024,1024]{1,0:T(8,128)(2,1)} %get-tuple-element.43.p_ref), custom_call_target="tpu_custom_call" | custom-call | tf_op jit(solution)/shard_map/query/pallas_call | solution.py:429
  126.0 19.2 %all-to-all-done.2 = f32[32,256,128]{2,1,0:T(8,128)} async-done(((f32[32,256,128]{2,1,0:T(8,128)}), f32[32,256,128]{2,1,0:T(8,128)}, u32[]{:S(2)}, u32[]{:S(2)}) %all-to-all-start.2) | async-done | bytes 4194336 | tf_op jit(solution)/shard_map/all_to_all | solution.py:543
  145.2 21.1 %rows1.1 = (bf16[2048,1024]{1,0:T(8,128)(2,1)}, f32[32,264,128]{2,1,0:T(8,128)}, f32[32,264,128]{2,1,0:T(8,128)}) custom-call(s32[4]{0:T(128)} %pad_add_fusion.pos_ref, s32[17]{0:T(128)} %get-tuple-element.34.start_ref, s32[128]{0:T(128)} %get-tuple-element.35.row_ref, s32[128]{0:T(128)} %get-tuple-element.36.block_ref, ...), custom_call_target="tpu_custom_call" | custom-call | tf_op jit(solution)/shard_map/rows1/pallas_call | solution.py:397
  166.3 3.3 %collective-permute-start = (f32[32,264,128]{2,1,0:T(8,128)}, f32[32,264,128]{2,1,0:T(8,128)S(1)}, u32[]{:S(2)}, u32[]{:S(2)}) collective-permute-start(f32[32,264,128]{2,1,0:T(8,128)} %get-tuple-element.47), channel_id=1, source_target_pairs={{0,1},{1,0},{2,3},{3,2},{4,5},{5,4},{6,7},{7,6},{8,9},{9,8},{10,11... | collective-permute-start | bytes 12976136 | tf_op jit(solution)/shard_map/ppermute | solution.py:529
  169.6 7.2 %collective-permute-done = f32[32,264,128]{2,1,0:T(8,128)S(1)} collective-permute-done((f32[32,264,128]{2,1,0:T(8,128)}, f32[32,264,128]{2,1,0:T(8,128)S(1)}, u32[]{:S(2)}, u32[]{:S(2)}) %collective-permute-start) | collective-permute-done | bytes 4325408 | tf_op jit(solution)/shard_map/ppermute | solution.py:529
  176.8 4.9 %add.61 = f32[32,264,128]{2,1,0:T(8,128)} add(f32[32,264,128]{2,1,0:T(8,128)} %get-tuple-element.46, f32[32,264,128]{2,1,0:T(8,128)S(1)} %collective-permute-done) | non-fusion elementwise | flops 1081344 | bytes 12976128 | tf_op jit(solution)/shard_map/add | solution.py:572
  181.7 4.8 %all-to-all-start.3 = ((f32[32,264,128]{2,1,0:T(8,128)}), f32[32,264,128]{2,1,0:T(8,128)}, u32[]{:S(2)}, u32[]{:S(2)}) async-start(f32[32,264,128]{2,1,0:T(8,128)} %add.61), calls=%async_computation.3 | async-start | bytes 8650752 | tf_op jit(solution)/shard_map/all_to_all | solution.py:543
  186.5 10.7 %columns.3 = (f32[128,1024]{1,0:T(8,128)}, f32[128,1024]{1,0:T(8,128)}, f32[128,1024]{1,0:T(8,128)}, f32[128,1024]{1,0:T(8,128)}, f32[128,1024]{1,0:T(8,128)}, /*index=5*/f32[128,1024]{1,0:T(8,128)}, f32[256,1024]{1,0:T(8,128)}) custom-call(s32[4]{0:T(128)} %pad_add_fusion.pos_ref, bf16[2048,1024]{1,0:T(8,128)(2,1)} %get-tuple-element.42.ds_ref, ...), custom_call_target="tpu_custom_call" | custom-call | tf_op jit(solution)/shard_map/columns/pallas_call | solution.py:463
  197.2 2.1 collective-permute-start.1
  200.1 7.4 %columns.5 = (f32[128,1024]{1,0:T(8,128)}, f32[128,1024]{1,0:T(8,128)}, f32[128,1024]{1,0:T(8,128)}, f32[128,1024]{1,0:T(8,128)}) custom-call(s32[4]{0:T(128)} %pad_add_fusion.pos_ref, bf16[2048,1024]{1,0:T(8,128)(2,1)} %get-tuple-element.57.ds_ref, bf16[2048,1024]{1,0:T(8,128)(2,1)} %q_ref.7), custom_call_target="tpu_custom_call" | custom-call | tf_op jit(solution)/shard_map/columns/pallas_call | solution.py:463
  208.9 2.6 collective-permute-start.3
  214.8 8.9 %collective-permute-done.11 = f32[128,1024]{1,0:T(8,128)S(1)} collective-permute-done((f32[128,1024]{1,0:T(8,128)}, f32[128,1024]{1,0:T(8,128)S(1)}, u32[]{:S(2)}, u32[]{:S(2)}) %collective-permute-start.11) | collective-permute-done | bytes 524320 | tf_op jit(solution)/shard_map/ppermute | solution.py:529
  223.7 2.1 collective-permute-start.6
  225.8 7.2 %columns.4 = (f32[128,1024]{1,0:T(8,128)}, f32[128,1024]{1,0:T(8,128)}, f32[256,1024]{1,0:T(8,128)}) custom-call(s32[4]{0:T(128)} %pad_add_fusion.pos_ref, bf16[2048,1024]{1,0:T(8,128)(2,1)} %get-tuple-element.57.ds_ref, bf16[2048,1024]{1,0:T(8,128)(2,1)} %q_ref.7), custom_call_target="tpu_custom_call" | custom-call | tf_op jit(solution)/shard_map/columns/pallas_call | solution.py:463
  234.2 2.2 add.69
  236.4 2.6 collective-permute-start.9
  239.1 6.1 %collective-permute-done.2 = f32[128,1024]{1,0:T(8,128)} collective-permute-done((f32[128,1024]{1,0:T(8,128)}, f32[128,1024]{1,0:T(8,128)}, u32[]{:S(2)}, u32[]{:S(2)}) %collective-permute-start.2) | collective-permute-done | bytes 524320 | tf_op jit(solution)/shard_map/ppermute | solution.py:529
  246.5 1.8 add_add_fusion.3
  248.4 8.0 %collective-permute-done.10 = f32[128,1024]{1,0:T(8,128)} collective-permute-done((f32[128,1024]{1,0:T(8,128)}, f32[128,1024]{1,0:T(8,128)}, u32[]{:S(2)}, u32[]{:S(2)}) %collective-permute-start.10) | collective-permute-done | bytes 524320 | tf_op jit(solution)/shard_map/ppermute | solution.py:529
  257.4 11.2 %collective-permute-done.12 = f32[128,1024]{1,0:T(8,128)} collective-permute-done((f32[128,1024]{1,0:T(8,128)S(1)}, f32[128,1024]{1,0:T(8,128)}, u32[]{:S(2)}, u32[]{:S(2)}) %collective-permute-start.12) | collective-permute-done | bytes 524320 | tf_op jit(solution)/shard_map/ppermute | solution.py:529
  272.8 3.0 %total.1 = (f32[64,1024]{1,0:T(8,128)}, f32[1,64]{1,0:T(1,128)}) custom-call(s32[1]{0:T(128)} %bitcast.me_ref, f32[32,264,128]{2,1,0:T(8,128)} %all-to-all-done.3.got_ref.lines_ref, f32[32,264,128]{2,1,0:T(8,128)} %all-to-all-done.3.got_ref.lines_ref, f32[8,128]{1,0:T(8,128)} %broadcast_in_dim.4.lse_ref), custom_call_target="tpu_custom_call" | custom-call | tf_op jit(solution)/shard_map/total/pallas_call | solution.py:500
  (53 shorter events, 22.0 us)
Async XLA Ops:
  8.0 38.7 %all-to-all-start = ((f32[32,136,128]{2,1,0:T(8,128)}), f32[32,136,128]{2,1,0:T(8,128)S(1)}, u32[]{:S(2)}, u32[]{:S(2)}) async-start(f32[32,136,128]{2,1,0:T(8,128)} %pack.3), calls=%async_computation | async-start | bytes 4456448 | tf_op jit(solution)/shard_map/all_to_all | solution.py:543
  46.6 1.4 copy-start.1
  48.1 39.4 %all-to-all-start.1 = ((f32[32,160,128]{2,1,0:T(8,128)}), f32[32,160,128]{2,1,0:T(8,128)S(1)}, u32[]{:S(2)}, u32[]{:S(2)}) async-start(f32[32,160,128]{2,1,0:T(8,128)} %fill_lse.1), calls=%async_computation.1 | async-start | bytes 5242880 | tf_op jit(solution)/shard_map/all_to_all | solution.py:543
  87.5 13.5 %copy-start = (f32[32,160,128]{2,1,0:T(8,128)}, f32[32,160,128]{2,1,0:T(8,128)S(1)}, u32[]{:S(2)}) copy-start(f32[32,160,128]{2,1,0:T(8,128)S(1)} %all-to-all-done.1) | copy-start | bytes 7864324
  87.5 57.7 %all-to-all-start.2 = ((f32[32,256,128]{2,1,0:T(8,128)}), f32[32,256,128]{2,1,0:T(8,128)}, u32[]{:S(2)}, u32[]{:S(2)}) async-start(f32[32,256,128]{2,1,0:T(8,128)} %pack.5), calls=%async_computation.2 | async-start | bytes 8388608 | tf_op jit(solution)/shard_map/all_to_all | solution.py:543
  166.3 10.5 %collective-permute-start = (f32[32,264,128]{2,1,0:T(8,128)}, f32[32,264,128]{2,1,0:T(8,128)S(1)}, u32[]{:S(2)}, u32[]{:S(2)}) collective-permute-start(f32[32,264,128]{2,1,0:T(8,128)} %get-tuple-element.47), channel_id=1, source_target_pairs={{0,1},{1,0},{2,3},{3,2},{4,5},{5,4},{6,7},{7,6},{8,9},{9,8},{10,11... | collective-permute-start | bytes 12976136 | tf_op jit(solution)/shard_map/ppermute | solution.py:529
  181.7 90.6 %all-to-all-start.3 = ((f32[32,264,128]{2,1,0:T(8,128)}), f32[32,264,128]{2,1,0:T(8,128)}, u32[]{:S(2)}, u32[]{:S(2)}) async-start(f32[32,264,128]{2,1,0:T(8,128)} %add.61), calls=%async_computation.3 | async-start | bytes 8650752 | tf_op jit(solution)/shard_map/all_to_all | solution.py:543
  197.2 14.9 %collective-permute-start.1 = (f32[128,1024]{1,0:T(8,128)}, f32[128,1024]{1,0:T(8,128)S(1)}, u32[]{:S(2)}, u32[]{:S(2)}) collective-permute-start(f32[128,1024]{1,0:T(8,128)} %get-tuple-element.52), channel_id=1, source_target_pairs={{0,32},{32,64},{64,96},{96,0},{1,33},{33,65},{65,97},{97,1},{2,34}... | collective-permute-start | bytes 1572872 | tf_op jit(solution)/shard_map/ppermute | solution.py:529
  199.3 14.3 %collective-permute-start.5 = (f32[128,1024]{1,0:T(8,128)}, f32[128,1024]{1,0:T(8,128)S(1)}, u32[]{:S(2)}, u32[]{:S(2)}) collective-permute-start(f32[128,1024]{1,0:T(8,128)} %get-tuple-element.56), channel_id=1, source_target_pairs={{0,96},{32,0},{64,32},{96,64},{1,97},{33,1},{65,33},{97,65},{2,98}... | collective-permute-start | bytes 1572872 | tf_op jit(solution)/shard_map/ppermute | solution.py:529
  200.1 12.7 %copy-start.5 = (f32[128,1024]{1,0:T(8,128)S(1)}, f32[128,1024]{1,0:T(8,128)}, u32[]{:S(2)}) copy-start(f32[128,1024]{1,0:T(8,128)} %get-tuple-element.51) | copy-start | bytes 1572868
  200.1 14.7 %copy-start.4 = (f32[128,1024]{1,0:T(8,128)S(1)}, f32[128,1024]{1,0:T(8,128)}, u32[]{:S(2)}) copy-start(f32[128,1024]{1,0:T(8,128)} %get-tuple-element.55) | copy-start | bytes 1572868
  207.4 16.3 %collective-permute-start.11 = (f32[128,1024]{1,0:T(8,128)}, f32[128,1024]{1,0:T(8,128)S(1)}, u32[]{:S(2)}, u32[]{:S(2)}) collective-permute-start(f32[128,1024]{1,0:T(8,128)} %get-tuple-element.64), channel_id=1, source_target_pairs={{0,96},{32,0},{64,32},{96,64},{1,97},{33,1},{65,33},{97,65},{2,98}... | collective-permute-start | bytes 1572872 | tf_op jit(solution)/shard_map/ppermute | solution.py:529
  208.8 25.3 %collective-permute-start.7 = (f32[128,1024]{1,0:T(8,128)}, f32[128,1024]{1,0:T(8,128)}, u32[]{:S(2)}, u32[]{:S(2)}) collective-permute-start(f32[128,1024]{1,0:T(8,128)} %get-tuple-element.60), channel_id=1, source_target_pairs={{0,32},{32,64},{64,96},{96,0},{1,33},{33,65},{65,97},{97,1},{2,34}... | collective-permute-start | bytes 1572872 | tf_op jit(solution)/shard_map/ppermute | solution.py:529
  208.9 27.5 %collective-permute-start.3 = (f32[128,1024]{1,0:T(8,128)}, f32[128,1024]{1,0:T(8,128)}, u32[]{:S(2)}, u32[]{:S(2)}) collective-permute-start(f32[128,1024]{1,0:T(8,128)} %get-tuple-element.53), channel_id=1, source_target_pairs={{0,96},{32,0},{64,32},{96,64},{1,97},{33,1},{65,33},{97,65},{2,98}... | collective-permute-start | bytes 1572872 | tf_op jit(solution)/shard_map/ppermute | solution.py:529
  212.1 26.9 %collective-permute-start.4 = (f32[128,1024]{1,0:T(8,128)}, f32[128,1024]{1,0:T(8,128)}, u32[]{:S(2)}, u32[]{:S(2)}) collective-permute-start(f32[128,1024]{1,0:T(8,128)} %get-tuple-element.54), channel_id=1, source_target_pairs={{0,32},{32,64},{64,96},{96,0},{1,33},{33,65},{65,97},{97,1},{2,34}... | collective-permute-start | bytes 1572872 | tf_op jit(solution)/shard_map/ppermute | solution.py:529
  213.6 31.6 %collective-permute-start.2 = (f32[128,1024]{1,0:T(8,128)}, f32[128,1024]{1,0:T(8,128)}, u32[]{:S(2)}, u32[]{:S(2)}) collective-permute-start(f32[128,1024]{1,0:T(8,128)} %add.63), channel_id=1, source_target_pairs={{0,32},{32,64},{64,96},{96,0},{1,33},{33,65},{65,97},{97,1},{2,34}... | collective-permute-start | bytes 1572872 | tf_op jit(solution)/shard_map/ppermute | solution.py:529
  214.8 31.7 %slice-start = ((f32[8,2,256]{2,1,0:T(2,128)}), f32[8,1,256]{2,1,0:T(1,128)S(1)}, s32[]{:S(2)}) async-start(f32[8,2,256]{2,1,0:T(2,128)} %add.60.lse_ref), calls=%async_computation.4 | async-start | bytes 16384 | tf_op jit(solution)/shard_map/slice | solution.py:592
  214.8 31.7 %copy-start.2 = (f32[256,1024]{1,0:T(8,128)S(1)}, f32[256,1024]{1,0:T(8,128)}, u32[]{:S(2)}) copy-start(f32[256,1024]{1,0:T(8,128)} %get-tuple-element.50) | copy-start | bytes 3145732
  223.7 22.8 %collective-permute-start.6 = (f32[128,1024]{1,0:T(8,128)S(1)}, f32[128,1024]{1,0:T(8,128)}, u32[]{:S(2)}, u32[]{:S(2)}) collective-permute-start(f32[128,1024]{1,0:T(8,128)S(1)} %add.67), channel_id=1, source_target_pairs={{0,96},{32,0},{64,32},{96,64},{1,97},{33,1},{65,33},{97,65},{2,98}... | collective-permute-start | bytes 1572872 | tf_op jit(solution)/shard_map/ppermute | solution.py:529
  234.1 34.5 %copy-start.3 = (f32[256,1024]{1,0:T(8,128)S(1)}, f32[256,1024]{1,0:T(8,128)}, u32[]{:S(2)}) copy-start(f32[256,1024]{1,0:T(8,128)} %get-tuple-element.58) | copy-start | bytes 3145732
  234.1 22.3 %collective-permute-start.10 = (f32[128,1024]{1,0:T(8,128)}, f32[128,1024]{1,0:T(8,128)}, u32[]{:S(2)}, u32[]{:S(2)}) collective-permute-start(f32[128,1024]{1,0:T(8,128)} %get-tuple-element.62), channel_id=1, source_target_pairs={{0,32},{32,64},{64,96},{96,0},{1,33},{33,65},{65,97},{97,1},{2,34}... | collective-permute-start | bytes 1572872 | tf_op jit(solution)/shard_map/ppermute | solution.py:529
  236.4 21.0 %collective-permute-start.9 = (f32[128,1024]{1,0:T(8,128)}, f32[128,1024]{1,0:T(8,128)}, u32[]{:S(2)}, u32[]{:S(2)}) collective-permute-start(f32[128,1024]{1,0:T(8,128)} %get-tuple-element.61), channel_id=1, source_target_pairs={{0,96},{32,0},{64,32},{96,64},{1,97},{33,1},{65,33},{97,65},{2,98}... | collective-permute-start | bytes 1572872 | tf_op jit(solution)/shard_map/ppermute | solution.py:529
  239.0 29.6 %collective-permute-start.12 = (f32[128,1024]{1,0:T(8,128)S(1)}, f32[128,1024]{1,0:T(8,128)}, u32[]{:S(2)}, u32[]{:S(2)}) collective-permute-start(f32[128,1024]{1,0:T(8,128)S(1)} %add.73), channel_id=1, source_target_pairs={{0,96},{32,0},{64,32},{96,64},{1,97},{33,1},{65,33},{97,65},{2,98}... | collective-permute-start | bytes 1572872 | tf_op jit(solution)/shard_map/ppermute | solution.py:529
  245.2 23.4 %collective-permute-start.8 = (f32[128,1024]{1,0:T(8,128)}, f32[128,1024]{1,0:T(8,128)}, u32[]{:S(2)}, u32[]{:S(2)}) collective-permute-start(f32[128,1024]{1,0:T(8,128)} %add.69), channel_id=1, source_target_pairs={{0,32},{32,64},{64,96},{96,0},{1,33},{33,65},{65,97},{97,1},{2,34}... | collective-permute-start | bytes 1572872 | tf_op jit(solution)/shard_map/ppermute | solution.py:529

commit v6 on v5

--- a/solution.py
+++ b/solution.py
@@ -330,6 +330,7 @@
             out_specs=(block, pl.BlockSpec((1, 1, rb), lambda i, *_: (i, 0, 0))),
             scratch_shapes=ROW_SCRATCH,
         ),
+        compiler_params=pltpu.CompilerParams(vmem_limit_bytes=30 << 20),
         name="rows0",
     )(*lists, scores, lse, *recvs)
 
@@ -416,6 +417,7 @@
             scratch_shapes=ROW_SCRATCH
             + [pltpu.VMEM((rb, D), jnp.bfloat16), pltpu.VMEM((8, BLOCK), jnp.float32)],
         ),
+        compiler_params=pltpu.CompilerParams(vmem_limit_bytes=32 << 20),
         name="rows1",
     )(*scalars, scores, lse, recv, add, passages, loss0)
 
@@ -432,6 +434,7 @@
         grid=(ROWS // rb,),
         in_specs=[pl.BlockSpec((rb, D), lambda i: (i, 0)), full_spec(D, D)],
         out_specs=pl.BlockSpec((rb, D), lambda i: (i, 0)),
+        compiler_params=pltpu.CompilerParams(vmem_limit_bytes=30 << 20),
         name="query",
     )(ds, passages)
 
@@ -469,6 +472,7 @@
             in_specs=[pl.BlockSpec((ROWS, D // 4), column), full_spec(ROWS, D)],
             out_specs=tuple(full_spec(n, D) for n in sizes),
         ),
+        compiler_params=pltpu.CompilerParams(vmem_limit_bytes=30 << 20),
         name="columns",
     )(pos, ds, queries)
     outs = list(outs)
@@ -517,6 +521,7 @@
             ),
             scratch_shapes=[pltpu.VMEM((8, BLOCK), jnp.float32)],
         ),
+        compiler_params=pltpu.CompilerParams(vmem_limit_bytes=16 << 20),
         name="total",
     )(me, got, got, lse_rows)
 

time: 278 us -> 273 us (0.982)
  Pallas kernels: 116 us -> 91.6 us
  local copies, waits for them, and re-layouts: 7.55 us -> 25.7 us
  waiting for transfers between devices: 92.8 us -> 99.7 us
  other arithmetic: 14.8 us -> 10.4 us
    unnamed x13 -> x41, local copies, waits for them, and re-layouts: 2.21 us -> 21.5 us
    pallas_call x3, Pallas kernels: 25.3 us -> 13.7 us  [columns_call(): pl.pallas_call(functools.partial(columns_kernel, groups), out_shape=tuple...]
    ppermute x13, waiting for transfers between devices: 43 us -> 51.8 us  [send(): return lax.ppermute(value, axis, ring(d, n))]
    pallas_call x1, Pallas kernels: 15.1 us -> 9.83 us  [rows0_call(): pl.pallas_call(rows0_kernel, out_shape=(jax.ShapeDtypeStruct((ROWS, D), j...]
    pallas_call x1, Pallas kernels: 9.1 us -> 5.03 us  [query_call(): pl.pallas_call(query_kernel, out_shape=jax.ShapeDtypeStruct((ROWS, D), jn...]
    pallas_call x1, Pallas kernels: 21.1 us -> 17.4 us  [rows1_call(): pl.pallas_call(rows1_kernel, out_shape=(jax.ShapeDtypeStruct((ROWS, D), j...]
  transfers between devices with their start and end apart: 17 -> 17, of which waited for: 10 -> 11; matrix products, arithmetic and copies ran while one was open for 5% -> 4% of each run, Pallas kernels for 31% -> 24%
where the time goes in v6:
time: 273 us; the launch traced here: 272 us
  waiting for transfers between devices  99.7 us (37%)
  Pallas kernels  91.6 us (34%)
  starting transfers between devices  43.4 us (16%)
  local copies, waits for them, and re-layouts  25.7 us (9%)
  other arithmetic  10.4 us (4%)
    ppermute x13, waiting for transfers between devices, send(): return lax.ppermute(value, axis, ring(d, n))  51.8 us
    all_to_all x4, waiting for transfers between devices, exchange(): return lax.all_to_all(value, PLANE, split_axis=0, concat_axis=0, tiled=True)  47.9 us
    all_to_all x4, starting transfers between devices, exchange(): return lax.all_to_all(value, PLANE, split_axis=0, concat_axis=0, tiled=True)  25.8 us
    unnamed x41, local copies, waits for them, and re-layouts  21.5 us
    pallas_call x1, Pallas kernels, score(): pl.pallas_call(score_kernel, out_shape=(scores, scores, jax.ShapeDtypeStr...  18.7 us
    pallas_call x3, Pallas kernels, pack(): pl.pallas_call(functools.partial(pack_kernel, piece), out_shape=jax.Shape...  18 us
    ppermute x13, starting transfers between devices, send(): return lax.ppermute(value, axis, ring(d, n))  17.6 us
    pallas_call x1, Pallas kernels, rows1_call(): pl.pallas_call(rows1_kernel, out_shape=(jax.ShapeDtypeStruct((ROWS, D), j...  17.4 us
  transfers between devices with their start and end apart: 17, of which 11 were waited for; matrix products, arithmetic and copies ran while one was open for 4% of the time, Pallas kernels for 24%

profile of v6, /device:TPU:1, one launch (start us, length us, event | category | flops | bytes accessed | tf_op | source)
XLA Modules:
  0.0 271.8 jit_solution(17571733423512049322)
XLA Ops:
  2.0 6.0 %pack.3 = f32[32,136,128]{2,1,0:T(8,128)} custom-call(s32[64]{0:T(128)} %reshape.40.ids_ref, f32[2048,512]{1,0:T(8,128)} %whole_ref.5), custom_call_target="tpu_custom_call" | custom-call | tf_op jit(solution)/shard_map/pack/pallas_call | solution.py:95
  8.0 8.6 %all-to-all-start = ((f32[32,136,128]{2,1,0:T(8,128)}), f32[32,136,128]{2,1,0:T(8,128)S(1)}, u32[]{:S(2)}, u32[]{:S(2)}) async-start(f32[32,136,128]{2,1,0:T(8,128)} %pack.3), calls=%async_computation | async-start | bytes 4456448 | tf_op jit(solution)/shard_map/all_to_all | solution.py:548
  16.6 18.7 %score.1 = (f32[2048,1024]{1,0:T(8,128)}, f32[2048,1024]{1,0:T(8,128)}, f32[8,2,256]{2,1,0:T(2,128)}, bf16[1024,1024]{1,0:T(8,128)(2,1)}, bf16[1024,1024]{1,0:T(8,128)(2,1)}) custom-call(bf16[2048,1024]{1,0:T(8,128)(2,1)} %q_ref.7, bf16[2048,1024]{1,0:T(8,128)(2,1)} %p_ref.1, f32[2048,512]{1,0:T(8,128)} %whole_ref.5), custom_call_target="tpu_custom_call" | custom-call | tf_op jit(solution)/shard_map/score/pallas_call | solution.py:220
  36.6 6.0 %pack.4.sent_ref = f32[32,160,128]{2,1,0:T(8,128)} custom-call(s32[64]{0:T(128)} %reshape.40.ids_ref, f32[2048,512]{1,0:T(8,128)} %whole_ref.5), custom_call_target="tpu_custom_call" | custom-call | tf_op jit(solution)/shard_map/pack/pallas_call | solution.py:95
  44.2 2.4 all-to-all-done
  48.0 5.4 %all-to-all-start.1 = ((f32[32,160,128]{2,1,0:T(8,128)}), f32[32,160,128]{2,1,0:T(8,128)S(1)}, u32[]{:S(2)}, u32[]{:S(2)}) async-start(f32[32,160,128]{2,1,0:T(8,128)} %fill_lse.1), calls=%async_computation.1 | async-start | bytes 5242880 | tf_op jit(solution)/shard_map/all_to_all | solution.py:548
  53.5 6.0 %pack.5 = f32[32,256,128]{2,1,0:T(8,128)} custom-call(s32[64]{0:T(128)} %reshape.40.ids_ref, f32[2048,512]{1,0:T(8,128)} %whole_ref.5), custom_call_target="tpu_custom_call" | custom-call | tf_op jit(solution)/shard_map/pack/pallas_call | solution.py:95
  59.5 28.0 %all-to-all-done.1 = f32[32,160,128]{2,1,0:T(8,128)S(1)} async-done(((f32[32,160,128]{2,1,0:T(8,128)}), f32[32,160,128]{2,1,0:T(8,128)S(1)}, u32[]{:S(2)}, u32[]{:S(2)}) %all-to-all-start.1) | async-done | bytes 2621472 | tf_op jit(solution)/shard_map/all_to_all | solution.py:548
  87.5 7.0 %all-to-all-start.2 = ((f32[32,256,128]{2,1,0:T(8,128)}), f32[32,256,128]{2,1,0:T(8,128)}, u32[]{:S(2)}, u32[]{:S(2)}) async-start(f32[32,256,128]{2,1,0:T(8,128)} %pack.5), calls=%async_computation.2 | async-start | bytes 8388608 | tf_op jit(solution)/shard_map/all_to_all | solution.py:548
  96.2 4.2 %make_lists.1 = (s32[17]{0:T(128)}, s32[128]{0:T(128)}, s32[128]{0:T(128)}) custom-call(s32[256]{0:T(256)} %convert_element_type.10.meta_ref), custom_call_target="tpu_custom_call" | custom-call | tf_op jit(solution)/shard_map/make_lists/pallas_call | solution.py:177
  102.2 3.4 %copy-done.8 = f32[2048,1024]{1,0:T(8,128)S(1)} copy-done((f32[2048,1024]{1,0:T(8,128)S(1)}, f32[2048,1024]{1,0:T(8,128)}, u32[]{:S(2)}) %copy-start.8) | copy-done | bytes 8388632
  107.4 9.8 %rows0.1 = (bf16[2048,1024]{1,0:T(8,128)(2,1)S(1)}, f32[8,1,256]{2,1,0:T(1,128)S(1)}) custom-call(s32[17]{0:T(128)S(1)} %copy-done.11, s32[128]{0:T(128)S(1)} %copy-done.13, s32[128]{0:T(128)S(1)} %copy-done.15, f32[2048,1024]{1,0:T(8,128)S(1)} %copy-done.8, f32[8,2,256]{2,1,0:T(2,128)S(1)} %add.60.lse_ref, f32[4352,128]{1,0:T(8,128)S(1)} %bitcast.14, ...), custom_call_target="tpu_custom_call" | custom-call | tf_op jit(solution)/shard_map/rows0/pallas_call | solution.py:319
  117.3 5.0 %query.1.add_ref = f32[2048,1024]{1,0:T(8,128)S(1)} custom-call(bf16[2048,1024]{1,0:T(8,128)(2,1)S(1)} %get-tuple-element.42.ds_ref, bf16[1024,1024]{1,0:T(8,128)(2,1)S(1)} %copy-done.10), custom_call_target="tpu_custom_call" | custom-call | tf_op jit(solution)/shard_map/query/pallas_call | solution.py:431
  122.4 3.2 %copy-done.1 = f32[2048,1024]{1,0:T(8,128)} copy-done((f32[2048,1024]{1,0:T(8,128)}, f32[2048,1024]{1,0:T(8,128)S(1)}, u32[]{:S(2)}) %copy-start.1) | copy-done | bytes 8388632
  127.6 17.5 %all-to-all-done.2 = f32[32,256,128]{2,1,0:T(8,128)} async-done(((f32[32,256,128]{2,1,0:T(8,128)}), f32[32,256,128]{2,1,0:T(8,128)}, u32[]{:S(2)}, u32[]{:S(2)}) %all-to-all-start.2) | async-done | bytes 4194336 | tf_op jit(solution)/shard_map/all_to_all | solution.py:548
  145.2 17.4 %rows1.1 = (bf16[2048,1024]{1,0:T(8,128)(2,1)S(1)}, f32[32,264,128]{2,1,0:T(8,128)S(1)}, f32[32,264,128]{2,1,0:T(8,128)S(1)}) custom-call(s32[4]{0:T(128)S(1)} %pad_add_fusion.pos_ref, s32[17]{0:T(128)S(1)} %copy-done.12, s32[128]{0:T(128)S(1)} %copy-done.14, s32[128]{0:T(128)S(1)} %copy-done.16, f32[2048,1024]{1,0:T(8,128)} %get-tuple-element.37.s_ref, ...), custom_call_target="tpu_custom_call" | custom-call | tf_op jit(solution)/shard_map/rows1/pallas_call | solution.py:398
  164.7 3.3 %collective-permute-start = (f32[32,264,128]{2,1,0:T(8,128)S(1)}, f32[32,264,128]{2,1,0:T(8,128)S(1)}, u32[]{:S(2)}, u32[]{:S(2)}) collective-permute-start(f32[32,264,128]{2,1,0:T(8,128)S(1)} %get-tuple-element.47), channel_id=1, source_target_pairs={{0,1},{1,0},{2,3},{3,2},{4,5},{5,4},{6,7},{7,6},{8,9},{9,8},{10,11... | collective-permute-start | bytes 12976136 | tf_op jit(solution)/shard_map/ppermute | solution.py:534
  168.0 7.0 %collective-permute-done = f32[32,264,128]{2,1,0:T(8,128)S(1)} collective-permute-done((f32[32,264,128]{2,1,0:T(8,128)S(1)}, f32[32,264,128]{2,1,0:T(8,128)S(1)}, u32[]{:S(2)}, u32[]{:S(2)}) %collective-permute-start) | collective-permute-done | bytes 4325408 | tf_op jit(solution)/shard_map/ppermute | solution.py:534
  175.0 2.5 add.61
  177.4 4.8 %all-to-all-start.3 = ((f32[32,264,128]{2,1,0:T(8,128)}), f32[32,264,128]{2,1,0:T(8,128)}, u32[]{:S(2)}, u32[]{:S(2)}) async-start(f32[32,264,128]{2,1,0:T(8,128)} %add.61), calls=%async_computation.3 | async-start | bytes 8650752 | tf_op jit(solution)/shard_map/all_to_all | solution.py:548
  186.6 6.6 %columns.3 = (f32[128,1024]{1,0:T(8,128)S(1)}, f32[128,1024]{1,0:T(8,128)S(1)}, f32[128,1024]{1,0:T(8,128)S(1)}, f32[128,1024]{1,0:T(8,128)S(1)}, f32[128,1024]{...) custom-call(s32[4]{0:T(128)S(1)} %pad_add_fusion.pos_ref, bf16[2048,1024]{1,0:T(8,128)(2,1)S(1)} %copy-done.3, ...), custom_call_target="tpu_custom_call" | custom-call | tf_op jit(solution)/shard_map/columns/pallas_call | solution.py:466
  193.3 2.8 %collective-permute-start.1 = (f32[128,1024]{1,0:T(8,128)S(1)}, f32[128,1024]{1,0:T(8,128)S(1)}, u32[]{:S(2)}, u32[]{:S(2)}) collective-permute-start(f32[128,1024]{1,0:T(8,128)S(1)} %get-tuple-element.52), channel_id=1, source_target_pairs={{0,32},{32,64},{64,96},{96,0},{1,33},{33,65},{65,97},{97,1},{2,34}... | collective-permute-start | bytes 1572872 | tf_op jit(solution)/shard_map/ppermute | solution.py:534
  196.4 3.6 %columns.5 = (f32[128,1024]{1,0:T(8,128)S(1)}, f32[128,1024]{1,0:T(8,128)S(1)}, f32[128,1024]{1,0:T(8,128)S(1)}, f32[128,1024]{1,0:T(8,128)S(1)}) custom-call(s32[4]{0:T(128)S(1)} %pad_add_fusion.pos_ref, bf16[2048,1024]{1,0:T(8,128)(2,1)S(1)} %copy-done.5, bf16[2048,1024]{1,0:T(8,128)(2,1)S(1)} %copy-done), custom_call_target="tpu_custom_call" | custom-call | tf_op jit(solution)/shard_map/columns/pallas_call | solution.py:466
  201.5 2.4 collective-permute-start.3
  204.0 4.1 %collective-permute-done.1 = f32[128,1024]{1,0:T(8,128)S(1)} collective-permute-done((f32[128,1024]{1,0:T(8,128)S(1)}, f32[128,1024]{1,0:T(8,128)S(1)}, u32[]{:S(2)}, u32[]{:S(2)}) %collective-permute-start.1) | collective-permute-done | bytes 524320 | tf_op jit(solution)/shard_map/ppermute | solution.py:534
  210.8 9.3 %collective-permute-done.11 = f32[128,1024]{1,0:T(8,128)S(1)} collective-permute-done((f32[128,1024]{1,0:T(8,128)S(1)}, f32[128,1024]{1,0:T(8,128)S(1)}, u32[]{:S(2)}, u32[]{:S(2)}) %collective-permute-start.11) | collective-permute-done | bytes 524320 | tf_op jit(solution)/shard_map/ppermute | solution.py:534
  222.2 3.6 %columns.4 = (f32[128,1024]{1,0:T(8,128)S(1)}, f32[128,1024]{1,0:T(8,128)S(1)}, f32[256,1024]{1,0:T(8,128)S(1)}) custom-call(s32[4]{0:T(128)S(1)} %pad_add_fusion.pos_ref, bf16[2048,1024]{1,0:T(8,128)(2,1)S(1)} %copy-done.5, bf16[2048,1024]{1,0:T(8,128)(2,1)S(1)} %copy-done), custom_call_target="tpu_custom_call" | custom-call | tf_op jit(solution)/shard_map/columns/pallas_call | solution.py:466
  227.5 3.8 %collective-permute-done.3 = f32[128,1024]{1,0:T(8,128)S(1)} collective-permute-done((f32[128,1024]{1,0:T(8,128)S(1)}, f32[128,1024]{1,0:T(8,128)S(1)}, u32[]{:S(2)}, u32[]{:S(2)}) %collective-permute-start.3) | collective-permute-done | bytes 524320 | tf_op jit(solution)/shard_map/ppermute | solution.py:534
  233.4 8.3 %collective-permute-done.2 = f32[128,1024]{1,0:T(8,128)S(1)} collective-permute-done((f32[128,1024]{1,0:T(8,128)S(1)}, f32[128,1024]{1,0:T(8,128)S(1)}, u32[]{:S(2)}, u32[]{:S(2)}) %collective-permute-start.2) | collective-permute-done | bytes 524320 | tf_op jit(solution)/shard_map/ppermute | solution.py:534
  245.7 7.3 %collective-permute-done.10 = f32[128,1024]{1,0:T(8,128)} collective-permute-done((f32[128,1024]{1,0:T(8,128)S(1)}, f32[128,1024]{1,0:T(8,128)}, u32[]{:S(2)}, u32[]{:S(2)}) %collective-permute-start.10) | collective-permute-done | bytes 524320 | tf_op jit(solution)/shard_map/ppermute | solution.py:534
  253.8 11.2 %collective-permute-done.12 = f32[128,1024]{1,0:T(8,128)} collective-permute-done((f32[128,1024]{1,0:T(8,128)}, f32[128,1024]{1,0:T(8,128)}, u32[]{:S(2)}, u32[]{:S(2)}) %collective-permute-start.12) | collective-permute-done | bytes 524320 | tf_op jit(solution)/shard_map/ppermute | solution.py:534
  268.7 3.0 %total.1 = (f32[64,1024]{1,0:T(8,128)}, f32[1,64]{1,0:T(1,128)}) custom-call(s32[1]{0:T(128)} %bitcast.me_ref, f32[32,264,128]{2,1,0:T(8,128)} %all-to-all-done.3.got_ref.lines_ref, f32[32,264,128]{2,1,0:T(8,128)} %all-to-all-done.3.got_ref.lines_ref, f32[8,128]{1,0:T(8,128)S(1)} %broadcast_in_dim.4.lse_ref), custom_call_target="tpu_custom_call" | custom-call | tf_op jit(solution)/shard_map/total/pallas_call | solution.py:504
  (80 shorter events, 38.7 us)
Async XLA Ops:
  8.0 38.7 %all-to-all-start = ((f32[32,136,128]{2,1,0:T(8,128)}), f32[32,136,128]{2,1,0:T(8,128)S(1)}, u32[]{:S(2)}, u32[]{:S(2)}) async-start(f32[32,136,128]{2,1,0:T(8,128)} %pack.3), calls=%async_computation | async-start | bytes 4456448 | tf_op jit(solution)/shard_map/all_to_all | solution.py:548
  48.0 39.4 %all-to-all-start.1 = ((f32[32,160,128]{2,1,0:T(8,128)}), f32[32,160,128]{2,1,0:T(8,128)S(1)}, u32[]{:S(2)}, u32[]{:S(2)}) async-start(f32[32,160,128]{2,1,0:T(8,128)} %fill_lse.1), calls=%async_computation.1 | async-start | bytes 5242880 | tf_op jit(solution)/shard_map/all_to_all | solution.py:548
  87.5 57.7 %all-to-all-start.2 = ((f32[32,256,128]{2,1,0:T(8,128)}), f32[32,256,128]{2,1,0:T(8,128)}, u32[]{:S(2)}, u32[]{:S(2)}) async-start(f32[32,256,128]{2,1,0:T(8,128)} %pack.5), calls=%async_computation.2 | async-start | bytes 8388608 | tf_op jit(solution)/shard_map/all_to_all | solution.py:548
  100.6 1.6 copy-start.7
  102.2 3.4 %copy-start.8 = (f32[2048,1024]{1,0:T(8,128)S(1)}, f32[2048,1024]{1,0:T(8,128)}, u32[]{:S(2)}) copy-start(f32[2048,1024]{1,0:T(8,128)} %get-tuple-element.41.s_ref) | copy-start | bytes 25165828
  107.4 9.8 %copy-start.10 = (bf16[1024,1024]{1,0:T(8,128)(2,1)S(1)}, bf16[1024,1024]{1,0:T(8,128)(2,1)}, u32[]{:S(2)}) copy-start(bf16[1024,1024]{1,0:T(8,128)(2,1)} %get-tuple-element.43.p_ref) | copy-start | bytes 6291460
  117.3 27.9 %copy-start.9 = (bf16[1024,1024]{1,0:T(8,128)(2,1)S(1)}, bf16[1024,1024]{1,0:T(8,128)(2,1)}, u32[]{:S(2)}) copy-start(bf16[1024,1024]{1,0:T(8,128)(2,1)} %get-tuple-element.44.p_ref) | copy-start | bytes 6291460
  117.3 27.9 %copy-start.12 = (s32[17]{0:T(128)S(1)}, s32[17]{0:T(128)}, u32[]{:S(2)}) copy-start(s32[17]{0:T(128)} %get-tuple-element.34.start_ref) | copy-start | bytes 208
  117.3 27.9 %copy-start.14 = (s32[128]{0:T(128)S(1)}, s32[128]{0:T(128)}, u32[]{:S(2)}) copy-start(s32[128]{0:T(128)} %get-tuple-element.35.row_ref) | copy-start | bytes 1540
  117.3 27.9 %copy-start.16 = (s32[128]{0:T(128)S(1)}, s32[128]{0:T(128)}, u32[]{:S(2)}) copy-start(s32[128]{0:T(128)} %get-tuple-element.36.block_ref) | copy-start | bytes 1540
  122.4 3.2 %copy-start.1 = (f32[2048,1024]{1,0:T(8,128)}, f32[2048,1024]{1,0:T(8,128)S(1)}, u32[]{:S(2)}) copy-start(f32[2048,1024]{1,0:T(8,128)S(1)} %query.1.add_ref) | copy-start | bytes 25165828
  125.6 2.0 copy-start.2
  162.6 2.1 copy-start.4
  164.7 10.3 %collective-permute-start = (f32[32,264,128]{2,1,0:T(8,128)S(1)}, f32[32,264,128]{2,1,0:T(8,128)S(1)}, u32[]{:S(2)}, u32[]{:S(2)}) collective-permute-start(f32[32,264,128]{2,1,0:T(8,128)S(1)} %get-tuple-element.47), channel_id=1, source_target_pairs={{0,1},{1,0},{2,3},{3,2},{4,5},{5,4},{6,7},{7,6},{8,9},{9,8},{10,11... | collective-permute-start | bytes 12976136 | tf_op jit(solution)/shard_map/ppermute | solution.py:534
  177.4 91.3 %all-to-all-start.3 = ((f32[32,264,128]{2,1,0:T(8,128)}), f32[32,264,128]{2,1,0:T(8,128)}, u32[]{:S(2)}, u32[]{:S(2)}) async-start(f32[32,264,128]{2,1,0:T(8,128)} %add.61), calls=%async_computation.3 | async-start | bytes 8650752 | tf_op jit(solution)/shard_map/all_to_all | solution.py:548
  182.2 2.2 copy-start
  184.4 2.2 copy-start.3
  186.6 9.8 %copy-start.5 = (bf16[2048,1024]{1,0:T(8,128)(2,1)S(1)}, bf16[2048,1024]{1,0:T(8,128)(2,1)}, u32[]{:S(2)}) copy-start(bf16[2048,1024]{1,0:T(8,128)(2,1)} %copy-done.4) | copy-start | bytes 12582916
  193.3 14.8 %collective-permute-start.1 = (f32[128,1024]{1,0:T(8,128)S(1)}, f32[128,1024]{1,0:T(8,128)S(1)}, u32[]{:S(2)}, u32[]{:S(2)}) collective-permute-start(f32[128,1024]{1,0:T(8,128)S(1)} %get-tuple-element.52), channel_id=1, source_target_pairs={{0,32},{32,64},{64,96},{96,0},{1,33},{33,65},{65,97},{97,1},{2,34}... | collective-permute-start | bytes 1572872 | tf_op jit(solution)/shard_map/ppermute | solution.py:534
  196.0 13.2 %collective-permute-start.5 = (f32[128,1024]{1,0:T(8,128)S(1)}, f32[128,1024]{1,0:T(8,128)S(1)}, u32[]{:S(2)}, u32[]{:S(2)}) collective-permute-start(f32[128,1024]{1,0:T(8,128)S(1)} %get-tuple-element.56), channel_id=1, source_target_pairs={{0,96},{32,0},{64,32},{96,64},{1,97},{33,1},{65,33},{97,65},{2,98}... | collective-permute-start | bytes 1572872 | tf_op jit(solution)/shard_map/ppermute | solution.py:534
  200.0 20.1 %collective-permute-start.11 = (f32[128,1024]{1,0:T(8,128)S(1)}, f32[128,1024]{1,0:T(8,128)S(1)}, u32[]{:S(2)}, u32[]{:S(2)}) collective-permute-start(f32[128,1024]{1,0:T(8,128)S(1)} %get-tuple-element.64), channel_id=1, source_target_pairs={{0,96},{32,0},{64,32},{96,64},{1,97},{33,1},{65,33},{97,65},{2,98}... | collective-permute-start | bytes 1572872 | tf_op jit(solution)/shard_map/ppermute | solution.py:534
  201.3 25.3 %collective-permute-start.7 = (f32[128,1024]{1,0:T(8,128)S(1)}, f32[128,1024]{1,0:T(8,128)S(1)}, u32[]{:S(2)}, u32[]{:S(2)}) collective-permute-start(f32[128,1024]{1,0:T(8,128)S(1)} %get-tuple-element.60), channel_id=1, source_target_pairs={{0,32},{32,64},{64,96},{96,0},{1,33},{33,65},{65,97},{97,1},{2,34}... | collective-permute-start | bytes 1572872 | tf_op jit(solution)/shard_map/ppermute | solution.py:534
  201.5 29.7 %collective-permute-start.3 = (f32[128,1024]{1,0:T(8,128)S(1)}, f32[128,1024]{1,0:T(8,128)S(1)}, u32[]{:S(2)}, u32[]{:S(2)}) collective-permute-start(f32[128,1024]{1,0:T(8,128)S(1)} %get-tuple-element.53), channel_id=1, source_target_pairs={{0,96},{32,0},{64,32},{96,64},{1,97},{33,1},{65,33},{97,65},{2,98}... | collective-permute-start | bytes 1572872 | tf_op jit(solution)/shard_map/ppermute | solution.py:534
  208.0 25.2 %collective-permute-start.4 = (f32[128,1024]{1,0:T(8,128)S(1)}, f32[128,1024]{1,0:T(8,128)S(1)}, u32[]{:S(2)}, u32[]{:S(2)}) collective-permute-start(f32[128,1024]{1,0:T(8,128)S(1)} %get-tuple-element.54), channel_id=1, source_target_pairs={{0,32},{32,64},{64,96},{96,0},{1,33},{33,65},{65,97},{97,1},{2,34}... | collective-permute-start | bytes 1572872 | tf_op jit(solution)/shard_map/ppermute | solution.py:534
  209.3 32.4 %collective-permute-start.2 = (f32[128,1024]{1,0:T(8,128)S(1)}, f32[128,1024]{1,0:T(8,128)S(1)}, u32[]{:S(2)}, u32[]{:S(2)}) collective-permute-start(f32[128,1024]{1,0:T(8,128)S(1)} %add.63), channel_id=1, source_target_pairs={{0,32},{32,64},{64,96},{96,0},{1,33},{33,65},{65,97},{97,1},{2,34}... | collective-permute-start | bytes 1572872 | tf_op jit(solution)/shard_map/ppermute | solution.py:534
  220.1 23.6 %collective-permute-start.6 = (f32[128,1024]{1,0:T(8,128)}, f32[128,1024]{1,0:T(8,128)}, u32[]{:S(2)}, u32[]{:S(2)}) collective-permute-start(f32[128,1024]{1,0:T(8,128)} %add.67), channel_id=1, source_target_pairs={{0,96},{32,0},{64,32},{96,64},{1,97},{33,1},{65,33},{97,65},{2,98}... | collective-permute-start | bytes 1572872 | tf_op jit(solution)/shard_map/ppermute | solution.py:534
  226.6 26.4 %collective-permute-start.10 = (f32[128,1024]{1,0:T(8,128)S(1)}, f32[128,1024]{1,0:T(8,128)}, u32[]{:S(2)}, u32[]{:S(2)}) collective-permute-start(f32[128,1024]{1,0:T(8,128)S(1)} %get-tuple-element.62), channel_id=1, source_target_pairs={{0,32},{32,64},{64,96},{96,0},{1,33},{33,65},{65,97},{97,1},{2,34}... | collective-permute-start | bytes 1572872 | tf_op jit(solution)/shard_map/ppermute | solution.py:534
  231.3 10.4 %copy-start.17 = (f32[128,1024]{1,0:T(8,128)}, f32[128,1024]{1,0:T(8,128)S(1)}, u32[]{:S(2)}) copy-start(f32[128,1024]{1,0:T(8,128)S(1)} %collective-permute-done.3) | copy-start | bytes 1572868
  231.3 22.6 %collective-permute-start.9 = (f32[128,1024]{1,0:T(8,128)S(1)}, f32[128,1024]{1,0:T(8,128)}, u32[]{:S(2)}, u32[]{:S(2)}) collective-permute-start(f32[128,1024]{1,0:T(8,128)S(1)} %get-tuple-element.61), channel_id=1, source_target_pairs={{0,96},{32,0},{64,32},{96,64},{1,97},{33,1},{65,33},{97,65},{2,98}... | collective-permute-start | bytes 1572872 | tf_op jit(solution)/shard_map/ppermute | solution.py:534
  233.3 8.4 %copy-start.18 = (f32[128,1024]{1,0:T(8,128)}, f32[128,1024]{1,0:T(8,128)S(1)}, u32[]{:S(2)}) copy-start(f32[128,1024]{1,0:T(8,128)S(1)} %collective-permute-done.4) | copy-start | bytes 1572868
  233.3 31.8 %collective-permute-start.12 = (f32[128,1024]{1,0:T(8,128)}, f32[128,1024]{1,0:T(8,128)}, u32[]{:S(2)}, u32[]{:S(2)}) collective-permute-start(f32[128,1024]{1,0:T(8,128)} %add.73), channel_id=1, source_target_pairs={{0,96},{32,0},{64,32},{96,64},{1,97},{33,1},{65,33},{97,65},{2,98}... | collective-permute-start | bytes 1572872 | tf_op jit(solution)/shard_map/ppermute | solution.py:534
  242.5 22.6 %collective-permute-start.8 = (f32[128,1024]{1,0:T(8,128)}, f32[128,1024]{1,0:T(8,128)}, u32[]{:S(2)}, u32[]{:S(2)}) collective-permute-start(f32[128,1024]{1,0:T(8,128)} %add.69), channel_id=1, source_target_pairs={{0,32},{32,64},{64,96},{96,0},{1,33},{33,65},{65,97},{97,1},{2,34}... | collective-permute-start | bytes 1572872 | tf_op jit(solution)/shard_map/ppermute | solution.py:534
  (5 other events, 4.0 us)

commit v7 on v6

--- a/solution.py
+++ b/solution.py
@@ -19,7 +19,7 @@
 ENTRIES = 64
 PACK_STEP = 8
 QUARTER = 32
-LSE_ROWS = 32
+LSE_ROWS = 16
 SUM_ROWS = 256
 PLANE = ("y", "x", "c")
 SCORE_SCALE = 0.0625
@@ -112,7 +112,9 @@
 
 
 def fill_kernel(lse_ref, sent_ref, out_ref):
-    out_ref[...] = jnp.broadcast_to(lse_ref[...][None], out_ref.shape)
+    halves = lse_ref[...].reshape(1, 2, LSE_ROWS, BLOCK)
+    pairs = jnp.broadcast_to(halves, (SHARDS // 2, 2, LSE_ROWS, BLOCK))
+    out_ref[...] = pairs.reshape(out_ref.shape)
 
 
 def fill_lse(sent, lse):
@@ -121,7 +123,7 @@
         out_shape=jax.ShapeDtypeStruct(sent.shape, sent.dtype),
         grid=(1,),
         in_specs=[
-            pl.BlockSpec((LSE_ROWS, BLOCK), lambda i: (0, 0)),
+            pl.BlockSpec((2 * LSE_ROWS, BLOCK), lambda i: (0, 0)),
             pl.BlockSpec(memory_space=pl.ANY),
         ],
         out_specs=pl.BlockSpec((SHARDS, LSE_ROWS, BLOCK), lambda i: (0, BLOCK // LSE_ROWS, 0)),
@@ -552,7 +554,7 @@
     ids1, _ = together(flat_ids, sent0)
     sent1 = pack(1, ids1, teacher)
     s0, s1, lse, p0, p1 = score(queries, passages, teacher)
-    sent1 = fill_lse(sent1, lse.reshape(LSE_ROWS, BLOCK))
+    sent1 = fill_lse(sent1, lse.reshape(2 * LSE_ROWS, BLOCK))
     recv1 = exchange(sent1)
     ids2, _ = together(flat_ids, lse)
     sent2 = pack(2, ids2, teacher)
@@ -562,7 +564,10 @@
     lists = tuple(make_lists(meta))
     every = recv1[:, BLOCK:, :]
     top = jnp.max(every, axis=0)
-    lse = (top + jnp.log(jnp.sum(jnp.exp(every - top[None]), axis=0))).reshape(8, 2, 256)
+    mine = top + jnp.log(jnp.sum(jnp.exp(every - top[None]), axis=0))
+    theirs = send(mine, "c", 1, 2)
+    even, odd = jnp.where(mc == 0, mine, theirs), jnp.where(mc == 0, theirs, mine)
+    lse = jnp.concatenate([even, odd], axis=0).reshape(8, 2, 256)
     ds0, loss0 = rows0_call(lists, s0, lse, [recv0, recv1])
     z0 = columns_call(pos, ds0, queries, (2, 1, 3, 0))
     np0, nm0 = send(z0[2][0], "pb", 1), send(z0[2][1], "pb", -1)

time: 273 us -> 270 us (0.989)
  waiting for transfers between devices: 99.7 us -> 96.2 us
    all_to_all x4, waiting for transfers between devices: 47.9 us -> 45 us  [exchange(): return lax.all_to_all(value, PLANE, split_axis=0, concat_axis=0, tiled=True)]
    ppermute x13 -> x14, starting transfers between devices: 17.6 us -> 18.8 us  [send(): return lax.ppermute(value, axis, ring(d, n))]
    ppermute x13 -> x14, waiting for transfers between devices: 51.8 us -> 51.2 us  [send(): return lax.ppermute(value, axis, ring(d, n))]
  transfers between devices with their start and end apart: 17 -> 18, of which waited for: 11 -> 10; matrix products, arithmetic and copies ran while one was open for 4% -> 4% of each run, Pallas kernels for 24% -> 24%
where the time goes in v7:
time: 270 us; the launch traced here: 269 us
  waiting for transfers between devices  96.2 us (36%)
  Pallas kernels  91.4 us (34%)
  starting transfers between devices  44.3 us (16%)
  local copies, waits for them, and re-layouts  25.6 us (9%)
  other arithmetic  10.4 us (4%)
    ppermute x14, waiting for transfers between devices, send(): return lax.ppermute(value, axis, ring(d, n))  51.2 us
    all_to_all x4, waiting for transfers between devices, exchange(): return lax.all_to_all(value, PLANE, split_axis=0, concat_axis=0, tiled=True)  45 us
    all_to_all x4, starting transfers between devices, exchange(): return lax.all_to_all(value, PLANE, split_axis=0, concat_axis=0, tiled=True)  25.5 us
    unnamed x41, local copies, waits for them, and re-layouts  21.5 us
    ppermute x14, starting transfers between devices, send(): return lax.ppermute(value, axis, ring(d, n))  18.8 us
    pallas_call x1, Pallas kernels, score(): pl.pallas_call(score_kernel, out_shape=(scores, scores, jax.ShapeDtypeStr...  18.7 us
    pallas_call x3, Pallas kernels, pack(): pl.pallas_call(functools.partial(pack_kernel, piece), out_shape=jax.Shape...  17.9 us
    pallas_call x1, Pallas kernels, rows1_call(): pl.pallas_call(rows1_kernel, out_shape=(jax.ShapeDtypeStruct((ROWS, D), j...  17.4 us
  transfers between devices with their start and end apart: 18, of which 10 were waited for; matrix products, arithmetic and copies ran while one was open for 4% of the time, Pallas kernels for 24%

profile of v7, /device:TPU:1, one launch (start us, length us, event | category | flops | bytes accessed | tf_op | source)
XLA Modules:
  0.0 268.8 jit_solution(9575752450869891521)
XLA Ops:
  2.0 6.0 %pack.3 = f32[32,136,128]{2,1,0:T(8,128)} custom-call(s32[64]{0:T(128)} %reshape.38.ids_ref, f32[2048,512]{1,0:T(8,128)} %whole_ref.5), custom_call_target="tpu_custom_call" | custom-call | tf_op jit(solution)/shard_map/pack/pallas_call | solution.py:95
  8.0 8.6 %all-to-all-start = ((f32[32,136,128]{2,1,0:T(8,128)}), f32[32,136,128]{2,1,0:T(8,128)S(1)}, u32[]{:S(2)}, u32[]{:S(2)}) async-start(f32[32,136,128]{2,1,0:T(8,128)} %pack.3), calls=%async_computation | async-start | bytes 4456448 | tf_op jit(solution)/shard_map/all_to_all | solution.py:550
  16.6 18.7 %score.1 = (f32[2048,1024]{1,0:T(8,128)}, f32[2048,1024]{1,0:T(8,128)}, f32[8,2,256]{2,1,0:T(2,128)}, bf16[1024,1024]{1,0:T(8,128)(2,1)}, bf16[1024,1024]{1,0:T(8,128)(2,1)}) custom-call(bf16[2048,1024]{1,0:T(8,128)(2,1)} %q_ref.7, bf16[2048,1024]{1,0:T(8,128)(2,1)} %p_ref.1, f32[2048,512]{1,0:T(8,128)} %whole_ref.5), custom_call_target="tpu_custom_call" | custom-call | tf_op jit(solution)/shard_map/score/pallas_call | solution.py:222
  36.6 5.9 %pack.4.sent_ref = f32[32,144,128]{2,1,0:T(8,128)} custom-call(s32[64]{0:T(128)} %reshape.38.ids_ref, f32[2048,512]{1,0:T(8,128)} %whole_ref.5), custom_call_target="tpu_custom_call" | custom-call | tf_op jit(solution)/shard_map/pack/pallas_call | solution.py:95
  44.0 2.6 all-to-all-done
  48.0 5.4 %all-to-all-start.1 = ((f32[32,144,128]{2,1,0:T(8,128)}), f32[32,144,128]{2,1,0:T(8,128)S(1)}, u32[]{:S(2)}, u32[]{:S(2)}) async-start(f32[32,144,128]{2,1,0:T(8,128)} %fill_lse.1), calls=%async_computation.1 | async-start | bytes 4718592 | tf_op jit(solution)/shard_map/all_to_all | solution.py:550
  53.5 6.0 %pack.5 = f32[32,256,128]{2,1,0:T(8,128)} custom-call(s32[64]{0:T(128)} %reshape.38.ids_ref, f32[2048,512]{1,0:T(8,128)} %whole_ref.5), custom_call_target="tpu_custom_call" | custom-call | tf_op jit(solution)/shard_map/pack/pallas_call | solution.py:95
  59.5 25.3 %all-to-all-done.1 = f32[32,144,128]{2,1,0:T(8,128)S(1)} async-done(((f32[32,144,128]{2,1,0:T(8,128)}), f32[32,144,128]{2,1,0:T(8,128)S(1)}, u32[]{:S(2)}, u32[]{:S(2)}) %all-to-all-start.1) | async-done | bytes 2359328 | tf_op jit(solution)/shard_map/all_to_all | solution.py:550
  84.7 6.7 %all-to-all-start.2 = ((f32[32,256,128]{2,1,0:T(8,128)}), f32[32,256,128]{2,1,0:T(8,128)}, u32[]{:S(2)}, u32[]{:S(2)}) async-start(f32[32,256,128]{2,1,0:T(8,128)} %pack.5), calls=%async_computation.2 | async-start | bytes 8388608 | tf_op jit(solution)/shard_map/all_to_all | solution.py:550
  93.7 4.2 %make_lists.1 = (s32[17]{0:T(128)}, s32[128]{0:T(128)}, s32[128]{0:T(128)}) custom-call(s32[256]{0:T(256)} %convert_element_type.10.meta_ref), custom_call_target="tpu_custom_call" | custom-call | tf_op jit(solution)/shard_map/make_lists/pallas_call | solution.py:179
  99.7 3.4 %copy-done.8 = f32[2048,1024]{1,0:T(8,128)S(1)} copy-done((f32[2048,1024]{1,0:T(8,128)S(1)}, f32[2048,1024]{1,0:T(8,128)}, u32[]{:S(2)}) %copy-start.8) | copy-done | bytes 8388632
  104.9 9.8 %rows0.1 = (bf16[2048,1024]{1,0:T(8,128)(2,1)S(1)}, f32[8,1,256]{2,1,0:T(1,128)S(1)}) custom-call(s32[17]{0:T(128)S(1)} %copy-done.11, s32[128]{0:T(128)S(1)} %copy-done.13, s32[128]{0:T(128)S(1)} %copy-done.15, f32[2048,1024]{1,0:T(8,128)S(1)} %copy-done.8, f32[8,2,256]{2,1,0:T(2,128)S(1)} %reshape.40.lse_ref, f32[4352,128]{1,0:T(8,128)S(1)} %bitcast.14, ...), custom_call_target="tpu_custom_call" | custom-call | tf_op jit(solution)/shard_map/rows0/pallas_call | solution.py:321
  114.8 5.0 %query.1.add_ref = f32[2048,1024]{1,0:T(8,128)S(1)} custom-call(bf16[2048,1024]{1,0:T(8,128)(2,1)S(1)} %get-tuple-element.42.ds_ref, bf16[1024,1024]{1,0:T(8,128)(2,1)S(1)} %copy-done.10), custom_call_target="tpu_custom_call" | custom-call | tf_op jit(solution)/shard_map/query/pallas_call | solution.py:433
  119.8 3.2 %copy-done.1 = f32[2048,1024]{1,0:T(8,128)} copy-done((f32[2048,1024]{1,0:T(8,128)}, f32[2048,1024]{1,0:T(8,128)S(1)}, u32[]{:S(2)}) %copy-start.1) | copy-done | bytes 8388632
  125.1 17.1 %all-to-all-done.2 = f32[32,256,128]{2,1,0:T(8,128)} async-done(((f32[32,256,128]{2,1,0:T(8,128)}), f32[32,256,128]{2,1,0:T(8,128)}, u32[]{:S(2)}, u32[]{:S(2)}) %all-to-all-start.2) | async-done | bytes 4194336 | tf_op jit(solution)/shard_map/all_to_all | solution.py:550
  142.1 17.4 %rows1.1 = (bf16[2048,1024]{1,0:T(8,128)(2,1)S(1)}, f32[32,264,128]{2,1,0:T(8,128)S(1)}, f32[32,264,128]{2,1,0:T(8,128)S(1)}) custom-call(s32[4]{0:T(128)S(1)} %pad_add_fusion.pos_ref, s32[17]{0:T(128)S(1)} %copy-done.12, s32[128]{0:T(128)S(1)} %copy-done.14, s32[128]{0:T(128)S(1)} %copy-done.16, f32[2048,1024]{1,0:T(8,128)} %get-tuple-element.37.s_ref, ...), custom_call_target="tpu_custom_call" | custom-call | tf_op jit(solution)/shard_map/rows1/pallas_call | solution.py:400
  161.6 3.3 %collective-permute-start.1 = (f32[32,264,128]{2,1,0:T(8,128)S(1)}, f32[32,264,128]{2,1,0:T(8,128)S(1)}, u32[]{:S(2)}, u32[]{:S(2)}) collective-permute-start(f32[32,264,128]{2,1,0:T(8,128)S(1)} %get-tuple-element.47), channel_id=1, source_target_pairs={{0,1},{1,0},{2,3},{3,2},{4,5},{5,4},{6,7},{7,6},{8,9},{9,8},{10,11... | collective-permute-start | bytes 12976136 | tf_op jit(solution)/shard_map/ppermute | solution.py:536
  165.0 7.0 %collective-permute-done.1 = f32[32,264,128]{2,1,0:T(8,128)S(1)} collective-permute-done((f32[32,264,128]{2,1,0:T(8,128)S(1)}, f32[32,264,128]{2,1,0:T(8,128)S(1)}, u32[]{:S(2)}, u32[]{:S(2)}) %collective-permute-start.1) | collective-permute-done | bytes 4325408 | tf_op jit(solution)/shard_map/ppermute | solution.py:536
  171.9 2.5 add.56
  174.4 4.8 %all-to-all-start.3 = ((f32[32,264,128]{2,1,0:T(8,128)}), f32[32,264,128]{2,1,0:T(8,128)}, u32[]{:S(2)}, u32[]{:S(2)}) async-start(f32[32,264,128]{2,1,0:T(8,128)} %add.56), calls=%async_computation.3 | async-start | bytes 8650752 | tf_op jit(solution)/shard_map/all_to_all | solution.py:550
  183.6 6.6 %columns.3 = (f32[128,1024]{1,0:T(8,128)S(1)}, f32[128,1024]{1,0:T(8,128)S(1)}, f32[128,1024]{1,0:T(8,128)S(1)}, f32[128,1024]{1,0:T(8,128)S(1)}, f32[128,1024]{...) custom-call(s32[4]{0:T(128)S(1)} %pad_add_fusion.pos_ref, bf16[2048,1024]{1,0:T(8,128)(2,1)S(1)} %copy-done.3, ...), custom_call_target="tpu_custom_call" | custom-call | tf_op jit(solution)/shard_map/columns/pallas_call | solution.py:468
  190.2 2.8 %collective-permute-start.2 = (f32[128,1024]{1,0:T(8,128)S(1)}, f32[128,1024]{1,0:T(8,128)S(1)}, u32[]{:S(2)}, u32[]{:S(2)}) collective-permute-start(f32[128,1024]{1,0:T(8,128)S(1)} %get-tuple-element.52), channel_id=1, source_target_pairs={{0,32},{32,64},{64,96},{96,0},{1,33},{33,65},{65,97},{97,1},{2,34}... | collective-permute-start | bytes 1572872 | tf_op jit(solution)/shard_map/ppermute | solution.py:536
  193.4 3.6 %columns.5 = (f32[128,1024]{1,0:T(8,128)S(1)}, f32[128,1024]{1,0:T(8,128)S(1)}, f32[128,1024]{1,0:T(8,128)S(1)}, f32[128,1024]{1,0:T(8,128)S(1)}) custom-call(s32[4]{0:T(128)S(1)} %pad_add_fusion.pos_ref, bf16[2048,1024]{1,0:T(8,128)(2,1)S(1)} %copy-done.5, bf16[2048,1024]{1,0:T(8,128)(2,1)S(1)} %copy-done), custom_call_target="tpu_custom_call" | custom-call | tf_op jit(solution)/shard_map/columns/pallas_call | solution.py:468
  198.5 2.4 collective-permute-start.4
  200.9 4.1 %collective-permute-done.2 = f32[128,1024]{1,0:T(8,128)S(1)} collective-permute-done((f32[128,1024]{1,0:T(8,128)S(1)}, f32[128,1024]{1,0:T(8,128)S(1)}, u32[]{:S(2)}, u32[]{:S(2)}) %collective-permute-start.2) | collective-permute-done | bytes 524320 | tf_op jit(solution)/shard_map/ppermute | solution.py:536
  207.8 9.3 %collective-permute-done.12 = f32[128,1024]{1,0:T(8,128)S(1)} collective-permute-done((f32[128,1024]{1,0:T(8,128)S(1)}, f32[128,1024]{1,0:T(8,128)S(1)}, u32[]{:S(2)}, u32[]{:S(2)}) %collective-permute-start.12) | collective-permute-done | bytes 524320 | tf_op jit(solution)/shard_map/ppermute | solution.py:536
  219.1 3.6 %columns.4 = (f32[128,1024]{1,0:T(8,128)S(1)}, f32[128,1024]{1,0:T(8,128)S(1)}, f32[256,1024]{1,0:T(8,128)S(1)}) custom-call(s32[4]{0:T(128)S(1)} %pad_add_fusion.pos_ref, bf16[2048,1024]{1,0:T(8,128)(2,1)S(1)} %copy-done.5, bf16[2048,1024]{1,0:T(8,128)(2,1)S(1)} %copy-done), custom_call_target="tpu_custom_call" | custom-call | tf_op jit(solution)/shard_map/columns/pallas_call | solution.py:468
  224.4 3.9 %collective-permute-done.4 = f32[128,1024]{1,0:T(8,128)S(1)} collective-permute-done((f32[128,1024]{1,0:T(8,128)S(1)}, f32[128,1024]{1,0:T(8,128)S(1)}, u32[]{:S(2)}, u32[]{:S(2)}) %collective-permute-start.4) | collective-permute-done | bytes 524320 | tf_op jit(solution)/shard_map/ppermute | solution.py:536
  230.9 7.6 %collective-permute-done.3 = f32[128,1024]{1,0:T(8,128)S(1)} collective-permute-done((f32[128,1024]{1,0:T(8,128)S(1)}, f32[128,1024]{1,0:T(8,128)S(1)}, u32[]{:S(2)}, u32[]{:S(2)}) %collective-permute-start.3) | collective-permute-done | bytes 524320 | tf_op jit(solution)/shard_map/ppermute | solution.py:536
  242.7 8.1 %collective-permute-done.10 = f32[128,1024]{1,0:T(8,128)} collective-permute-done((f32[128,1024]{1,0:T(8,128)S(1)}, f32[128,1024]{1,0:T(8,128)}, u32[]{:S(2)}, u32[]{:S(2)}) %collective-permute-start.10) | collective-permute-done | bytes 524320 | tf_op jit(solution)/shard_map/ppermute | solution.py:536
  250.8 11.2 %collective-permute-done.13 = f32[128,1024]{1,0:T(8,128)} collective-permute-done((f32[128,1024]{1,0:T(8,128)}, f32[128,1024]{1,0:T(8,128)}, u32[]{:S(2)}, u32[]{:S(2)}) %collective-permute-start.13) | collective-permute-done | bytes 524320 | tf_op jit(solution)/shard_map/ppermute | solution.py:536
  265.7 3.0 %total.1 = (f32[64,1024]{1,0:T(8,128)}, f32[1,64]{1,0:T(1,128)}) custom-call(s32[1]{0:T(128)} %bitcast.me_ref, f32[32,264,128]{2,1,0:T(8,128)} %all-to-all-done.3.got_ref.lines_ref, f32[32,264,128]{2,1,0:T(8,128)} %all-to-all-done.3.got_ref.lines_ref, f32[8,128]{1,0:T(8,128)S(1)} %broadcast_in_dim.4.lse_ref), custom_call_target="tpu_custom_call" | custom-call | tf_op jit(solution)/shard_map/total/pallas_call | solution.py:506
  (84 shorter events, 38.6 us)
Async XLA Ops:
  8.0 38.7 %all-to-all-start = ((f32[32,136,128]{2,1,0:T(8,128)}), f32[32,136,128]{2,1,0:T(8,128)S(1)}, u32[]{:S(2)}, u32[]{:S(2)}) async-start(f32[32,136,128]{2,1,0:T(8,128)} %pack.3), calls=%async_computation | async-start | bytes 4456448 | tf_op jit(solution)/shard_map/all_to_all | solution.py:550
  48.0 36.7 %all-to-all-start.1 = ((f32[32,144,128]{2,1,0:T(8,128)}), f32[32,144,128]{2,1,0:T(8,128)S(1)}, u32[]{:S(2)}, u32[]{:S(2)}) async-start(f32[32,144,128]{2,1,0:T(8,128)} %fill_lse.1), calls=%async_computation.1 | async-start | bytes 4718592 | tf_op jit(solution)/shard_map/all_to_all | solution.py:550
  84.7 57.4 %all-to-all-start.2 = ((f32[32,256,128]{2,1,0:T(8,128)}), f32[32,256,128]{2,1,0:T(8,128)}, u32[]{:S(2)}, u32[]{:S(2)}) async-start(f32[32,256,128]{2,1,0:T(8,128)} %pack.5), calls=%async_computation.2 | async-start | bytes 8388608 | tf_op jit(solution)/shard_map/all_to_all | solution.py:550
  91.6 6.3 %collective-permute-start = (f32[16,128]{1,0:T(8,128)S(1)}, f32[16,128]{1,0:T(8,128)S(1)}, u32[]{:S(2)}, u32[]{:S(2)}) collective-permute-start(f32[16,128]{1,0:T(8,128)S(1)} %log_add_fusion), channel_id=1, source_target_pairs={{0,1},{1,0},{2,3},{3,2},{4,5},{5,4},{6,7},{7,6},{8,9},{9,8},{10,11... | collective-permute-start | bytes 24584 | tf_op jit(solution)/shard_map/ppermute | solution.py:536
  99.7 3.4 %copy-start.8 = (f32[2048,1024]{1,0:T(8,128)S(1)}, f32[2048,1024]{1,0:T(8,128)}, u32[]{:S(2)}) copy-start(f32[2048,1024]{1,0:T(8,128)} %get-tuple-element.41.s_ref) | copy-start | bytes 25165828
  104.9 9.8 %copy-start.10 = (bf16[1024,1024]{1,0:T(8,128)(2,1)S(1)}, bf16[1024,1024]{1,0:T(8,128)(2,1)}, u32[]{:S(2)}) copy-start(bf16[1024,1024]{1,0:T(8,128)(2,1)} %get-tuple-element.43.p_ref) | copy-start | bytes 6291460
  114.7 27.4 %copy-start.9 = (bf16[1024,1024]{1,0:T(8,128)(2,1)S(1)}, bf16[1024,1024]{1,0:T(8,128)(2,1)}, u32[]{:S(2)}) copy-start(bf16[1024,1024]{1,0:T(8,128)(2,1)} %get-tuple-element.44.p_ref) | copy-start | bytes 6291460
  114.7 27.4 %copy-start.12 = (s32[17]{0:T(128)S(1)}, s32[17]{0:T(128)}, u32[]{:S(2)}) copy-start(s32[17]{0:T(128)} %get-tuple-element.34.start_ref) | copy-start | bytes 208
  114.7 27.4 %copy-start.14 = (s32[128]{0:T(128)S(1)}, s32[128]{0:T(128)}, u32[]{:S(2)}) copy-start(s32[128]{0:T(128)} %get-tuple-element.35.row_ref) | copy-start | bytes 1540
  114.7 27.4 %copy-start.16 = (s32[128]{0:T(128)S(1)}, s32[128]{0:T(128)}, u32[]{:S(2)}) copy-start(s32[128]{0:T(128)} %get-tuple-element.36.block_ref) | copy-start | bytes 1540
  119.8 3.3 %copy-start.1 = (f32[2048,1024]{1,0:T(8,128)}, f32[2048,1024]{1,0:T(8,128)S(1)}, u32[]{:S(2)}) copy-start(f32[2048,1024]{1,0:T(8,128)S(1)} %query.1.add_ref) | copy-start | bytes 25165828
  123.1 2.0 copy-start.2
  159.6 2.1 copy-start.4
  161.6 10.3 %collective-permute-start.1 = (f32[32,264,128]{2,1,0:T(8,128)S(1)}, f32[32,264,128]{2,1,0:T(8,128)S(1)}, u32[]{:S(2)}, u32[]{:S(2)}) collective-permute-start(f32[32,264,128]{2,1,0:T(8,128)S(1)} %get-tuple-element.47), channel_id=1, source_target_pairs={{0,1},{1,0},{2,3},{3,2},{4,5},{5,4},{6,7},{7,6},{8,9},{9,8},{10,11... | collective-permute-start | bytes 12976136 | tf_op jit(solution)/shard_map/ppermute | solution.py:536
  174.4 91.3 %all-to-all-start.3 = ((f32[32,264,128]{2,1,0:T(8,128)}), f32[32,264,128]{2,1,0:T(8,128)}, u32[]{:S(2)}, u32[]{:S(2)}) async-start(f32[32,264,128]{2,1,0:T(8,128)} %add.56), calls=%async_computation.3 | async-start | bytes 8650752 | tf_op jit(solution)/shard_map/all_to_all | solution.py:550
  179.2 2.2 copy-start
  181.4 2.2 copy-start.3
  183.6 9.8 %copy-start.5 = (bf16[2048,1024]{1,0:T(8,128)(2,1)S(1)}, bf16[2048,1024]{1,0:T(8,128)(2,1)}, u32[]{:S(2)}) copy-start(bf16[2048,1024]{1,0:T(8,128)(2,1)} %copy-done.4) | copy-start | bytes 12582916
  190.2 14.7 %collective-permute-start.2 = (f32[128,1024]{1,0:T(8,128)S(1)}, f32[128,1024]{1,0:T(8,128)S(1)}, u32[]{:S(2)}, u32[]{:S(2)}) collective-permute-start(f32[128,1024]{1,0:T(8,128)S(1)} %get-tuple-element.52), channel_id=1, source_target_pairs={{0,32},{32,64},{64,96},{96,0},{1,33},{33,65},{65,97},{97,1},{2,34}... | collective-permute-start | bytes 1572872 | tf_op jit(solution)/shard_map/ppermute | solution.py:536
  193.0 13.2 %collective-permute-start.6 = (f32[128,1024]{1,0:T(8,128)S(1)}, f32[128,1024]{1,0:T(8,128)S(1)}, u32[]{:S(2)}, u32[]{:S(2)}) collective-permute-start(f32[128,1024]{1,0:T(8,128)S(1)} %get-tuple-element.56), channel_id=1, source_target_pairs={{0,96},{32,0},{64,32},{96,64},{1,97},{33,1},{65,33},{97,65},{2,98}... | collective-permute-start | bytes 1572872 | tf_op jit(solution)/shard_map/ppermute | solution.py:536
  197.0 20.2 %collective-permute-start.12 = (f32[128,1024]{1,0:T(8,128)S(1)}, f32[128,1024]{1,0:T(8,128)S(1)}, u32[]{:S(2)}, u32[]{:S(2)}) collective-permute-start(f32[128,1024]{1,0:T(8,128)S(1)} %get-tuple-element.64), channel_id=1, source_target_pairs={{0,96},{32,0},{64,32},{96,64},{1,97},{33,1},{65,33},{97,65},{2,98}... | collective-permute-start | bytes 1572872 | tf_op jit(solution)/shard_map/ppermute | solution.py:536
  198.2 25.3 %collective-permute-start.8 = (f32[128,1024]{1,0:T(8,128)S(1)}, f32[128,1024]{1,0:T(8,128)S(1)}, u32[]{:S(2)}, u32[]{:S(2)}) collective-permute-start(f32[128,1024]{1,0:T(8,128)S(1)} %get-tuple-element.60), channel_id=1, source_target_pairs={{0,32},{32,64},{64,96},{96,0},{1,33},{33,65},{65,97},{97,1},{2,34}... | collective-permute-start | bytes 1572872 | tf_op jit(solution)/shard_map/ppermute | solution.py:536
  198.5 29.8 %collective-permute-start.4 = (f32[128,1024]{1,0:T(8,128)S(1)}, f32[128,1024]{1,0:T(8,128)S(1)}, u32[]{:S(2)}, u32[]{:S(2)}) collective-permute-start(f32[128,1024]{1,0:T(8,128)S(1)} %get-tuple-element.53), channel_id=1, source_target_pairs={{0,96},{32,0},{64,32},{96,64},{1,97},{33,1},{65,33},{97,65},{2,98}... | collective-permute-start | bytes 1572872 | tf_op jit(solution)/shard_map/ppermute | solution.py:536
  205.0 24.0 %collective-permute-start.5 = (f32[128,1024]{1,0:T(8,128)S(1)}, f32[128,1024]{1,0:T(8,128)S(1)}, u32[]{:S(2)}, u32[]{:S(2)}) collective-permute-start(f32[128,1024]{1,0:T(8,128)S(1)} %get-tuple-element.54), channel_id=1, source_target_pairs={{0,32},{32,64},{64,96},{96,0},{1,33},{33,65},{65,97},{97,1},{2,34}... | collective-permute-start | bytes 1572872 | tf_op jit(solution)/shard_map/ppermute | solution.py:536
  206.3 32.3 %collective-permute-start.3 = (f32[128,1024]{1,0:T(8,128)S(1)}, f32[128,1024]{1,0:T(8,128)S(1)}, u32[]{:S(2)}, u32[]{:S(2)}) collective-permute-start(f32[128,1024]{1,0:T(8,128)S(1)} %add.58), channel_id=1, source_target_pairs={{0,32},{32,64},{64,96},{96,0},{1,33},{33,65},{65,97},{97,1},{2,34}... | collective-permute-start | bytes 1572872 | tf_op jit(solution)/shard_map/ppermute | solution.py:536
  217.1 23.6 %collective-permute-start.7 = (f32[128,1024]{1,0:T(8,128)}, f32[128,1024]{1,0:T(8,128)}, u32[]{:S(2)}, u32[]{:S(2)}) collective-permute-start(f32[128,1024]{1,0:T(8,128)} %add.62), channel_id=1, source_target_pairs={{0,96},{32,0},{64,32},{96,64},{1,97},{33,1},{65,33},{97,65},{2,98}... | collective-permute-start | bytes 1572872 | tf_op jit(solution)/shard_map/ppermute | solution.py:536
  223.5 27.3 %collective-permute-start.10 = (f32[128,1024]{1,0:T(8,128)S(1)}, f32[128,1024]{1,0:T(8,128)}, u32[]{:S(2)}, u32[]{:S(2)}) collective-permute-start(f32[128,1024]{1,0:T(8,128)S(1)} %get-tuple-element.61), channel_id=1, source_target_pairs={{0,96},{32,0},{64,32},{96,64},{1,97},{33,1},{65,33},{97,65},{2,98}... | collective-permute-start | bytes 1572872 | tf_op jit(solution)/shard_map/ppermute | solution.py:536
  228.3 10.3 %copy-start.17 = (f32[128,1024]{1,0:T(8,128)}, f32[128,1024]{1,0:T(8,128)S(1)}, u32[]{:S(2)}) copy-start(f32[128,1024]{1,0:T(8,128)S(1)} %collective-permute-done.4) | copy-start | bytes 1572868
  228.3 22.6 %collective-permute-start.11 = (f32[128,1024]{1,0:T(8,128)S(1)}, f32[128,1024]{1,0:T(8,128)}, u32[]{:S(2)}, u32[]{:S(2)}) collective-permute-start(f32[128,1024]{1,0:T(8,128)S(1)} %get-tuple-element.62), channel_id=1, source_target_pairs={{0,32},{32,64},{64,96},{96,0},{1,33},{33,65},{65,97},{97,1},{2,34}... | collective-permute-start | bytes 1572872 | tf_op jit(solution)/shard_map/ppermute | solution.py:536
  229.0 9.6 %copy-start.18 = (f32[128,1024]{1,0:T(8,128)}, f32[128,1024]{1,0:T(8,128)S(1)}, u32[]{:S(2)}) copy-start(f32[128,1024]{1,0:T(8,128)S(1)} %collective-permute-done.5) | copy-start | bytes 1572868
  229.0 33.1 %collective-permute-start.13 = (f32[128,1024]{1,0:T(8,128)}, f32[128,1024]{1,0:T(8,128)}, u32[]{:S(2)}, u32[]{:S(2)}) collective-permute-start(f32[128,1024]{1,0:T(8,128)} %add.68), channel_id=1, source_target_pairs={{0,96},{32,0},{64,32},{96,64},{1,97},{33,1},{65,33},{97,65},{2,98}... | collective-permute-start | bytes 1572872 | tf_op jit(solution)/shard_map/ppermute | solution.py:536
  239.4 22.7 %collective-permute-start.9 = (f32[128,1024]{1,0:T(8,128)}, f32[128,1024]{1,0:T(8,128)}, u32[]{:S(2)}, u32[]{:S(2)}) collective-permute-start(f32[128,1024]{1,0:T(8,128)} %add.64), channel_id=1, source_target_pairs={{0,32},{32,64},{64,96},{96,0},{1,33},{33,65},{65,97},{97,1},{2,34}... | collective-permute-start | bytes 1572872 | tf_op jit(solution)/shard_map/ppermute | solution.py:536
  (6 other events, 5.6 us)
